TPU v7x, 32 devices: a whole 2x2x4 slice. The times are simulated.
32 devices in a mesh: dp: 4 (over z), sp: 8 (over y, x, core).
Axes of the slice: x: 2, y: 2, z: 4, core: 2. Of those that a mesh axis runs over, the one named last changes fastest.
Arguments:
- token_ids: int32 [8, 2048], P('dp'), may hold values from 0 to 50303
- targets: int32 [8, 2048], P('dp'), may hold values from 0 to 50303
- stream_ids: int32 [8], replicated, may hold values 0 or 1
- embed_table: float32 [50304, 1024], P('sp', 'dp'), may hold values from -6 to 6
- embed_first: float32 [50304, 1024], P('sp', 'dp'), may hold values from -2.9802322e-08 to 2.9802322e-08
- embed_second: float32 [50304, 1024], P('sp', 'dp'), may hold values from 9.47911e-17 to 3.791644e-16
- unembed: float32 [1024, 50304], P('dp', 'sp'), may hold values from -0.25 to 0.25
- unembed_first: float32 [1024, 50304], P('dp', 'sp'), may hold values from -5.9604645e-07 to 5.9604645e-07
- unembed_second: float32 [1024, 50304], P('dp', 'sp'), may hold values from 4.3245172e-14 to 1.7298069e-13
- proj_in: float32 [1024, 7168], P(('dp', 'sp')), may hold values from -0.1875 to 0.1875
- proj_in_first: float32 [1024, 7168], P(('dp', 'sp')), may hold values from -5.9604645e-07 to 5.9604645e-07
- proj_in_second: float32 [1024, 7168], P(('dp', 'sp')), may hold values from 4.3245172e-14 to 1.7298069e-13
- proj_out: float32 [5120, 1024], P(('dp', 'sp')), may hold values from -1.25 to 1.25
- proj_out_first: float32 [5120, 1024], P(('dp', 'sp')), may hold values from -5.9604645e-07 to 5.9604645e-07
- proj_out_second: float32 [5120, 1024], P(('dp', 'sp')), may hold values from 4.3245172e-14 to 1.7298069e-13
- norm_params: float32 [6, 1024], P(None, ('dp', 'sp')), may hold values from -0.6 to 1.3
- norm_first: float32 [6, 1024], P(None, ('dp', 'sp')), may hold values from -5.722046e-06 to 5.722046e-06
- norm_second: float32 [6, 1024], P(None, ('dp', 'sp')), may hold values from 4.3245173e-12 to 1.729807e-11
- biases: float32 [8192], P(('dp', 'sp')), may hold values from -1.25 to 1.25
- bias_first: float32 [8192], P(('dp', 'sp')), may hold values from -5.722046e-06 to 5.722046e-06
- bias_second: float32 [8192], P(('dp', 'sp')), may hold values from 4.3245173e-12 to 1.729807e-11
Outputs:
- mean_loss: float32 [], replicated
- grad_norm: float32 [], replicated
- embed_new: float32 [50304, 1024], P('sp', 'dp')
- embed_first_new: float32 [50304, 1024], P('sp', 'dp')
- embed_second_new: float32 [50304, 1024], P('sp', 'dp')
- unembed_new: float32 [1024, 50304], P('dp', 'sp')
- unembed_first_new: float32 [1024, 50304], P('dp', 'sp')
- unembed_second_new: float32 [1024, 50304], P('dp', 'sp')
- proj_in_new: float32 [1024, 7168], P(('dp', 'sp'))
- proj_in_first_new: float32 [1024, 7168], P(('dp', 'sp'))
- proj_in_second_new: float32 [1024, 7168], P(('dp', 'sp'))
- proj_out_new: float32 [5120, 1024], P(('dp', 'sp'))
- proj_out_first_new: float32 [5120, 1024], P(('dp', 'sp'))
- proj_out_second_new: float32 [5120, 1024], P(('dp', 'sp'))
- norm_new: float32 [6, 1024], P(None, ('dp', 'sp'))
- norm_first_new: float32 [6, 1024], P(None, ('dp', 'sp'))
- norm_second_new: float32 [6, 1024], P(None, ('dp', 'sp'))
- bias_new: float32 [8192], P(('dp', 'sp'))
- bias_first_new: float32 [8192], P(('dp', 'sp'))
- bias_second_new: float32 [8192], P(('dp', 'sp'))
All inputs are finite; a program needn't handle non-finite values.
Results may differ from a plain program's by a relative error of at most 0.018.
Values may be sent and summed in bfloat16 or wider, within the bound.
A program may use at most 320 MiB of HBM per device.

v0:
```python
from functools import partial

import jax
import jax.numpy as jnp
from jax import lax
from jax.sharding import PartitionSpec as P

HEADS = 16
ROT = 16
STEP_COUNT = 10


NORM_EPS = 1e-05
BETA_ONE = 0.9
BETA_TWO = 0.95
ADAM_EPS = 1e-08
WEIGHT_DECAY = 0.01
CLIP_LEVEL = 0.01
REPLAY_WEIGHT = 4.0
NEGATIVE_FILL = -1e30


def merged(value, axis, join):
    gathered = jax.tree.map(
        lambda a, kind: lax.all_gather(a.astype(kind), axis),
        value,
        jax.tree.map(lambda a: jnp.bfloat16 if a.dtype == jnp.float32 else a.dtype, value),
    )

    def take(source):
        return jax.tree.map(
            lambda a, own: lax.dynamic_index_in_dim(a, source, 0, False).astype(own.dtype),
            gathered,
            value,
        )

    return lax.fori_loop(
        1, lax.axis_size(axis), lambda source, state: join(state, take(source)), take(0)
    )


def layer_norm(values, gain_row, shift_row):
    average = jnp.mean(values, axis=-1, keepdims=True)
    centered = values - average
    variance = jnp.mean(centered * centered, axis=-1, keepdims=True)
    return centered * lax.rsqrt(variance + NORM_EPS) * gain_row + shift_row


def gelu_exact(values):
    return jax.nn.gelu(values, approximate=False)


def rotary_tables(positions):
    halfway = ROT // 2
    frequency = 10000.0 ** (-2.0 * jnp.arange(halfway, dtype=jnp.float32) / ROT)
    angles = positions.astype(jnp.float32)[:, None] * frequency[None, :]
    angles = jnp.concatenate([angles, angles], axis=-1)
    return (jnp.cos(angles), jnp.sin(angles))


def rotate(values, cosine, sine_part):
    halfway = ROT // 2
    turned_part = values[..., :ROT]
    turned = jnp.concatenate([-turned_part[..., halfway:], turned_part[..., :halfway]], axis=-1)
    rotated = turned_part * cosine[:, None, :] + turned * sine_part[:, None, :]
    return jnp.concatenate([rotated, values[..., ROT:]], axis=-1)


def merge_parts(first_part, second_part):
    highest = jnp.maximum(first_part[0], second_part[0])
    summed = first_part[1] * jnp.exp(first_part[0] - highest) + second_part[1] * jnp.exp(
        second_part[0] - highest
    )
    return (highest, summed, first_part[2] + second_part[2])


def block_scores(query_block, keys_all, start, block, scale):
    scores = (
        jnp.einsum("sqhd,skhd->shqk", query_block, keys_all, preferred_element_type=jnp.float32)
        * scale
    )
    allowed = (start + jnp.arange(block))[:, None] >= jnp.arange(keys_all.shape[1])[None, :]
    return jnp.where(allowed, scores, NEGATIVE_FILL)


def attend_forward(queries, keys_all, values_all, block, scale):
    total = queries.shape[1]

    def one_block(index):
        start = index * block
        query_block = lax.dynamic_slice_in_dim(queries, start, block, 1)
        scores = block_scores(query_block, keys_all, start, block, scale)
        highest = jnp.max(scores, axis=-1, keepdims=True)
        powers = jnp.exp(scores - highest)
        totals = jnp.sum(powers, axis=-1, keepdims=True)
        probs_low = (powers / totals).astype(jnp.bfloat16)
        result = jnp.einsum(
            "shqk,skhd->sqhd", probs_low, values_all, preferred_element_type=jnp.float32
        )
        return (result.astype(jnp.bfloat16), (highest + jnp.log(totals))[..., 0])

    outputs, log_totals = lax.map(one_block, jnp.arange(total // block))
    outputs = jnp.moveaxis(outputs, 0, 1).reshape(queries.shape)
    return (outputs, log_totals)


def attend_backward(queries, keys_all, values_all, log_totals, grad_out, block, scale):
    total = queries.shape[1]

    def one_block(carry, index):
        key_grad, value_grad = carry
        start = index * block
        query_block = lax.dynamic_slice_in_dim(queries, start, block, 1)
        grad_block = lax.dynamic_slice_in_dim(grad_out, start, block, 1)
        scores = block_scores(query_block, keys_all, start, block, scale)
        probs = jnp.exp(scores - log_totals[index][..., None])
        grad_probs = jnp.einsum(
            "sqhd,skhd->shqk", grad_block, values_all, preferred_element_type=jnp.float32
        )
        centre = jnp.sum(probs * grad_probs, axis=-1, keepdims=True)
        grad_scores = (probs * (grad_probs - centre)).astype(jnp.bfloat16)
        query_grad = (
            jnp.einsum("shqk,skhd->sqhd", grad_scores, keys_all, preferred_element_type=jnp.float32)
            * scale
        )
        key_grad = (
            key_grad
            + jnp.einsum(
                "shqk,sqhd->skhd", grad_scores, query_block, preferred_element_type=jnp.float32
            )
            * scale
        )
        value_grad = value_grad + jnp.einsum(
            "shqk,sqhd->skhd",
            probs.astype(jnp.bfloat16),
            grad_block,
            preferred_element_type=jnp.float32,
        )
        return ((key_grad, value_grad), query_grad)

    zeros_kv = jnp.zeros(keys_all.shape, jnp.float32)
    (key_grad, value_grad), query_grad = lax.scan(
        one_block, (zeros_kv, zeros_kv), jnp.arange(total // block)
    )
    query_grad = jnp.moveaxis(query_grad, 0, 1).reshape(queries.shape)
    return (query_grad, key_grad, value_grad)


def adam_update(weight, first, second, grad, clip_factor, rate, decay):
    grad = grad * clip_factor
    first_new = BETA_ONE * first + (1.0 - BETA_ONE) * grad
    second_new = BETA_TWO * second + (1.0 - BETA_TWO) * grad * grad
    fix_one = 1.0 - BETA_ONE**STEP_COUNT
    fix_two = 1.0 - BETA_TWO**STEP_COUNT
    direction = first_new / fix_one / (jnp.sqrt(second_new / fix_two) + ADAM_EPS)
    return (weight - rate * (direction + decay * weight), first_new, second_new)


def local(
    token_ids,
    targets,
    stream_ids,
    embed_table,
    embed_first,
    embed_second,
    unembed,
    unembed_first,
    unembed_second,
    proj_in,
    proj_in_first,
    proj_in_second,
    proj_out,
    proj_out_first,
    proj_out_second,
    norm_params,
    norm_first,
    norm_second,
    biases,
    bias_first,
    bias_second,
):
    lowtype = jnp.bfloat16
    span = lax.axis_size("sp")
    sp_index = lax.axis_index("sp")
    dp_index = lax.axis_index("dp")
    seq_here, length = token_ids.shape
    stretch = length // span
    wide_in, wide_out, norm_full, bias_full = (
        lax.all_gather(proj_in.astype(lowtype), ("dp", "sp"), axis=0, tiled=True),
        lax.all_gather(proj_out.astype(lowtype), ("dp", "sp"), axis=0, tiled=True),
        lax.all_gather(norm_params.astype(lowtype), ("dp", "sp"), axis=1, tiled=True),
        lax.all_gather(biases.astype(lowtype), ("dp", "sp"), axis=0, tiled=True),
    )
    embed_local, unembed_local = (
        lax.all_gather(embed_table.astype(lowtype), "dp", axis=1, tiled=True),
        lax.all_gather(unembed.astype(lowtype), "dp", axis=0, tiled=True),
    )
    norm_vals = norm_full.astype(jnp.float32)
    bias_vals = bias_full.astype(jnp.float32)
    width = wide_out.shape[1]
    hidden_units = wide_in.shape[1] - 3 * width
    heads_here = HEADS // span
    head_dim = width // HEADS
    scale = head_dim ** (-0.5)
    vocab_local = embed_local.shape[0]
    offset = sp_index * vocab_local
    local_ids = token_ids - offset
    in_slice = (local_ids >= 0) & (local_ids < vocab_local)
    safe_ids = jnp.clip(local_ids, 0, vocab_local - 1)
    picked = jnp.where(
        in_slice[..., None], jnp.take(embed_local, safe_ids, axis=0), jnp.zeros((), lowtype)
    )
    hidden0 = lax.psum_scatter(picked, "sp", scatter_dimension=1, tiled=True).astype(jnp.float32)
    normed_one_f, pull_one = jax.vjp(layer_norm, hidden0, norm_vals[0], norm_vals[1])
    normed_two_f, pull_two = jax.vjp(layer_norm, hidden0, norm_vals[2], norm_vals[3])
    normed_one = normed_one_f.astype(lowtype)
    normed_two = normed_two_f.astype(lowtype)
    joint_proj = (
        jnp.dot(normed_one, wide_in[:, : 3 * width], preferred_element_type=jnp.float32)
        + bias_vals[: 3 * width]
    )
    joint_proj = joint_proj.reshape(seq_here, stretch, HEADS, 3, head_dim)
    cosine, sine_part = rotary_tables(sp_index * stretch + jnp.arange(stretch))
    turn = partial(rotate, cosine=cosine, sine_part=sine_part)
    queries_f, pull_queries = jax.vjp(turn, joint_proj[..., 0, :])
    keys_f, pull_keys = jax.vjp(turn, joint_proj[..., 1, :])
    packed = jnp.stack([queries_f, keys_f, joint_proj[..., 2, :]], axis=3).astype(lowtype)
    packed = packed.reshape(seq_here, stretch, HEADS, 3 * head_dim)
    heads_side = lax.all_to_all(packed, "sp", split_axis=2, concat_axis=1, tiled=True)
    queries = heads_side[..., :head_dim]
    keys_all = heads_side[..., head_dim : 2 * head_dim]
    values_all = heads_side[..., 2 * head_dim :]
    attn_block = min(512, length)
    attended_heads, log_totals = attend_forward(queries, keys_all, values_all, attn_block, scale)
    attended = lax.all_to_all(
        attended_heads, "sp", split_axis=1, concat_axis=2, tiled=True
    ).reshape(seq_here, stretch, width)
    up_values = (
        jnp.dot(normed_two, wide_in[:, 3 * width :], preferred_element_type=jnp.float32)
        + bias_vals[3 * width : 3 * width + hidden_units]
    )
    act_f, pull_gelu = jax.vjp(gelu_exact, up_values)
    joined = jnp.concatenate([attended, act_f.astype(lowtype)], axis=-1)
    hidden1 = (
        hidden0
        + jnp.dot(joined, wide_out, preferred_element_type=jnp.float32)
        + bias_vals[3 * width + hidden_units :]
    )
    final_f, pull_final = jax.vjp(layer_norm, hidden1, norm_vals[4], norm_vals[5])
    final_all = lax.all_gather(final_f.astype(lowtype), "sp", axis=1, tiled=True)
    rows_all = final_all.reshape(-1, width)
    labels = targets.reshape(-1)
    grand = rows_all.shape[0]
    head_block = min(512, grand)
    head_count = grand // head_block
    columns = jnp.arange(vocab_local) + offset

    def head_logits(index):
        rows_block = lax.dynamic_slice_in_dim(rows_all, index * head_block, head_block, 0)
        label_block = lax.dynamic_slice_in_dim(labels, index * head_block, head_block, 0)
        logits = jnp.dot(rows_block, unembed_local, preferred_element_type=jnp.float32)
        return (rows_block, label_block, logits)

    def head_forward(index):
        rows_block, label_block, logits = head_logits(index)
        highest = jnp.max(logits, axis=-1)
        summed = jnp.sum(jnp.exp(logits - highest[:, None]), axis=-1)
        chosen = jnp.sum(jnp.where(columns[None, :] == label_block[:, None], logits, 0.0), axis=-1)
        return (highest, summed, chosen)

    local_parts = lax.map(head_forward, jnp.arange(head_count))
    highest, summed, chosen = merged(local_parts, "sp", merge_parts)
    log_sum = (highest + jnp.log(summed)).reshape(-1)
    token_loss = (log_sum - chosen.reshape(-1)).reshape(seq_here, length)
    weight_all = 1.0 + (REPLAY_WEIGHT - 1.0) * stream_ids.astype(jnp.float32)
    total_weight = jnp.sum(weight_all)
    seq_weight = lax.dynamic_slice_in_dim(weight_all, dp_index * seq_here, seq_here, 0)
    loss_local = jnp.sum(seq_weight * jnp.mean(token_loss, axis=1))
    token_scale = jnp.broadcast_to(
        (seq_weight / (total_weight * length))[:, None], (seq_here, length)
    ).reshape(-1)

    def head_backward(carry, index):
        rows_block, label_block, logits = head_logits(index)
        lse_block = lax.dynamic_slice_in_dim(log_sum, index * head_block, head_block, 0)
        scale_block = lax.dynamic_slice_in_dim(token_scale, index * head_block, head_block, 0)
        probs = jnp.exp(logits - lse_block[:, None])
        target_hit = (columns[None, :] == label_block[:, None]).astype(jnp.float32)
        grad_logits = (scale_block[:, None] * (probs - target_hit)).astype(lowtype)
        carry = carry + lax.dot_general(
            rows_block, grad_logits, (((0,), (0,)), ((), ())), preferred_element_type=jnp.float32
        )
        grad_rows = lax.dot_general(
            grad_logits, unembed_local, (((1,), (1,)), ((), ())), preferred_element_type=jnp.float32
        )
        return (carry, grad_rows)

    unembed_grad, grad_rows = lax.scan(
        head_backward, jnp.zeros(unembed_local.shape, jnp.float32), jnp.arange(head_count)
    )
    final_grad = lax.psum_scatter(
        grad_rows.reshape(seq_here, length, width).astype(jnp.bfloat16),
        "sp",
        scatter_dimension=1,
        tiled=True,
    ).astype(jnp.float32)
    d_hidden1, g_gain_final, g_shift_final = pull_final(final_grad)
    d_branch = d_hidden1.astype(lowtype)
    g_out = jnp.einsum("scj,scd->jd", joined, d_branch, preferred_element_type=jnp.float32)
    g_bias_out = jnp.sum(d_branch.astype(jnp.float32), axis=(0, 1))
    d_joined = jnp.einsum("scd,jd->scj", d_branch, wide_out, preferred_element_type=jnp.float32)
    d_attended = d_joined[..., :width].astype(lowtype).reshape(seq_here, stretch, HEADS, head_dim)
    d_heads = lax.all_to_all(d_attended, "sp", split_axis=2, concat_axis=1, tiled=True)
    query_grad, key_grad, value_grad = attend_backward(
        queries, keys_all, values_all, log_totals, d_heads, attn_block, scale
    )
    d_packed = jnp.stack([query_grad, key_grad, value_grad], axis=3).astype(lowtype)
    d_packed = d_packed.reshape(seq_here, length, heads_here, 3 * head_dim)
    d_stretches = lax.all_to_all(d_packed, "sp", split_axis=1, concat_axis=2, tiled=True)
    d_stretches = d_stretches.reshape(seq_here, stretch, HEADS, 3, head_dim).astype(jnp.float32)
    d_joint = jnp.stack(
        [
            pull_queries(d_stretches[..., 0, :])[0],
            pull_keys(d_stretches[..., 1, :])[0],
            d_stretches[..., 2, :],
        ],
        axis=3,
    )
    d_joint = d_joint.astype(lowtype).reshape(seq_here, stretch, 3 * width)
    d_up = pull_gelu(d_joined[..., width:])[0].astype(lowtype)
    g_in = jnp.concatenate(
        [
            jnp.einsum("scd,scn->dn", normed_one, d_joint, preferred_element_type=jnp.float32),
            jnp.einsum("scd,scn->dn", normed_two, d_up, preferred_element_type=jnp.float32),
        ],
        axis=1,
    )
    g_bias = jnp.concatenate(
        [
            jnp.sum(d_joint.astype(jnp.float32), axis=(0, 1)),
            jnp.sum(d_up.astype(jnp.float32), axis=(0, 1)),
            g_bias_out,
        ]
    )
    d_normed_one = jnp.einsum(
        "scn,dn->scd", d_joint, wide_in[:, : 3 * width], preferred_element_type=jnp.float32
    )
    d_normed_two = jnp.einsum(
        "scn,dn->scd", d_up, wide_in[:, 3 * width :], preferred_element_type=jnp.float32
    )
    d_from_one, g_gain_one, g_shift_one = pull_one(d_normed_one)
    d_from_two, g_gain_two, g_shift_two = pull_two(d_normed_two)
    g_norm = jnp.stack(
        [g_gain_one, g_shift_one, g_gain_two, g_shift_two, g_gain_final, g_shift_final]
    )
    d_hidden0 = (d_hidden1 + d_from_one + d_from_two).astype(lowtype)
    grad_all = lax.all_gather(d_hidden0, "sp", axis=1, tiled=True).reshape(-1, width)
    masked = jnp.where(in_slice.reshape(-1)[:, None], grad_all.astype(jnp.float32), 0.0)
    embed_grad = jnp.zeros((vocab_local, width), jnp.float32).at[safe_ids.reshape(-1)].add(masked)
    r_in, r_out, r_norm, r_bias = (
        lax.psum_scatter(g_in, ("dp", "sp"), scatter_dimension=0, tiled=True),
        lax.psum_scatter(g_out, ("dp", "sp"), scatter_dimension=0, tiled=True),
        lax.psum_scatter(g_norm, ("dp", "sp"), scatter_dimension=1, tiled=True),
        lax.psum_scatter(g_bias, ("dp", "sp"), scatter_dimension=0, tiled=True),
    )
    r_embed, r_unembed = (
        lax.psum_scatter(
            embed_grad.astype(jnp.bfloat16), "dp", scatter_dimension=1, tiled=True
        ).astype(jnp.float32),
        lax.psum_scatter(
            unembed_grad.astype(jnp.bfloat16), "dp", scatter_dimension=0, tiled=True
        ).astype(jnp.float32),
    )
    reduced = (r_embed, r_unembed, r_in, r_out, r_norm, r_bias)
    squares = jnp.float32(0.0)
    for grad_piece in reduced:
        squares = squares + jnp.sum(grad_piece * grad_piece)
    loss_term = jnp.where(sp_index == 0, loss_local, 0.0)
    squares_total, loss_total = lax.psum((squares, loss_term), ("dp", "sp"))
    grad_norm = jnp.sqrt(squares_total)
    mean_loss = loss_total / total_weight
    clip_factor = jnp.minimum(1.0, CLIP_LEVEL / (grad_norm + 1e-06))
    masters = (embed_table, unembed, proj_in, proj_out, norm_params, biases)
    firsts = (embed_first, unembed_first, proj_in_first, proj_out_first, norm_first, bias_first)
    seconds = (
        embed_second,
        unembed_second,
        proj_in_second,
        proj_out_second,
        norm_second,
        bias_second,
    )
    rates = (1.0, 0.05, 0.05, 0.1, 0.5, 0.5)
    decays = (WEIGHT_DECAY, WEIGHT_DECAY, WEIGHT_DECAY, WEIGHT_DECAY, 0.0, 0.0)
    results = []
    for index in range(6):
        results.extend(
            adam_update(
                masters[index],
                firsts[index],
                seconds[index],
                reduced[index],
                clip_factor,
                rates[index],
                decays[index],
            )
        )
    return (
        mean_loss,
        grad_norm,
        results[0],
        results[1],
        results[2],
        results[3],
        results[4],
        results[5],
        results[6],
        results[7],
        results[8],
        results[9],
        results[10],
        results[11],
        results[12],
        results[13],
        results[14],
        results[15],
        results[16],
        results[17],
    )


def solution(mesh):
    in_specs = (
        P("dp", None),
        P("dp", None),
        P(),
        P("sp", "dp"),
        P("sp", "dp"),
        P("sp", "dp"),
        P("dp", "sp"),
        P("dp", "sp"),
        P("dp", "sp"),
        P(("dp", "sp"), None),
        P(("dp", "sp"), None),
        P(("dp", "sp"), None),
        P(("dp", "sp"), None),
        P(("dp", "sp"), None),
        P(("dp", "sp"), None),
        P(None, ("dp", "sp")),
        P(None, ("dp", "sp")),
        P(None, ("dp", "sp")),
        P(("dp", "sp")),
        P(("dp", "sp")),
        P(("dp", "sp")),
    )
    out_specs = (
        P(),
        P(),
        P("sp", "dp"),
        P("sp", "dp"),
        P("sp", "dp"),
        P("dp", "sp"),
        P("dp", "sp"),
        P("dp", "sp"),
        P(("dp", "sp"), None),
        P(("dp", "sp"), None),
        P(("dp", "sp"), None),
        P(("dp", "sp"), None),
        P(("dp", "sp"), None),
        P(("dp", "sp"), None),
        P(None, ("dp", "sp")),
        P(None, ("dp", "sp")),
        P(None, ("dp", "sp")),
        P(("dp", "sp")),
        P(("dp", "sp")),
        P(("dp", "sp")),
    )
    return jax.shard_map(local, mesh=mesh, in_specs=in_specs, out_specs=out_specs, check_vma=False)
```

profile of v0, /device:TPU:0, one launch (start us, length us, event | category | flops | bytes accessed | tf_op | source)
XLA Modules:
  0.0 3100.7 jit_solution(13344512973926615551)
XLA Ops:
  13.7 224.6 %all-gather.12.cloned.1.call-done = bf16[6288,1024]{1,0:T(8,128)(2,1)} async-done(((bf16[6288,256]{1,0:T(8,128)(2,1)}), bf16[6288,1024]{1,0:T(8,128)(2,1)}) %all-gather.12.cloned.1.call-update) | async-done | bytes 12877840 | tf_op jit(solution)/shard_map/all_gather | solution.py:195
  238.3 27.2 gather_fusion
  276.0 39.9 %all-gather.3 = bf16[32,32,6]{1,2,0:T(8,128)(2,1)S(1)} all-gather(bf16[1,32,6]{1,2,0:T(8,128)(2,1)S(1)} %convert_bitcast_fusion.3), channel_id=1, replica_groups=mesh['dp'=4,'sp'=8] {'dp','sp'}, dimensions={0}, use_global_device_ids=true | all-gather | bytes 12672 | tf_op jit(solution)/shard_map/all_gather | solution.py:191
  316.0 37.5 %all-gather.4 = bf16[32,1,256]{2,1,0:T(2,128)(2,1)S(1)} all-gather(bf16[1,1,256]{2,1,0:T(2,128)(2,1)S(1)} %reshape.391), channel_id=1, replica_groups=mesh['dp'=4,'sp'=8] {'dp','sp'}, dimensions={0}, use_global_device_ids=true | all-gather | bytes 16896 | tf_op jit(solution)/shard_map/all_gather | solution.py:192
  354.3 27.0 reduce-scatter.10.cloned.1.call-done
  420.8 49.9 %all-to-all-done = bf16[2,256,16,192]{1,3,0,2:T(8,128)(2,1)S(1)} async-done(((bf16[2,256,16,192]{1,3,0,2:T(8,128)(2,1)}), bf16[2,256,16,192]{1,3,0,2:T(8,128)(2,1)S(1)}, u32[]{:S(2)}, u32[]{:S(2)}) %all-to-all-start) | async-done | bytes 3145760 | tf_op jit(solution)/shard_map/all_to_all | solution.py:229
  483.3 69.1 %while.74 = (s32[]{:T(128)}, bf16[4,2,512,2,64]{2,4,3,1,0:T(8,128)(2,1)}, f32[4,2,2,512]{3,2,1,0:T(2,128)}, s32[4]{0:T(128)S(1)}, bf16[2,2048,2,64]{1,3,2,0:T(8,...) while((s32[]{:T(128)}, ...), condition=%wide.region_6.7_spmd, body=%wide.region_3.6_spmd.sunk | while | flops 1125251584 | bytes 57217216 | solution.py:102
  568.0 26.3 multiply_convert_fusion.2
  618.6 98.2 %all-gather.20.cloned.1.call-done = bf16[1024,6288]{0,1:T(8,128)(2,1)} async-done(((bf16[256,6288]{0,1:T(8,128)(2,1)}), bf16[1024,6288]{0,1:T(8,128)(2,1)}) %all-gather.20.cloned.1.call-update) | async-done | bytes 12877840 | tf_op jit(solution)/shard_map/all_gather | solution.py:196
  733.6 38.1 %all-gather.18.cloned.1.call-done = bf16[2,2048,1024]{2,1,0:T(8,128)(2,1)} async-done(((bf16[2,256,1024]{2,1,0:T(8,128)(2,1)}), bf16[2,2048,1024]{2,1,0:T(8,128)(2,1)}) %all-gather.18.cloned.1.call-update) | async-done | bytes 8388624 | tf_op jit(solution)/shard_map/all_gather | solution.py:250
  771.7 211.5 %while.76 = (s32[]{:T(128)}, bf16[8,512]{1,0:T(8,128)(2,1)S(1)}, bf16[8,512]{1,0:T(8,128)(2,1)S(1)}, bf16[8,512]{1,0:T(8,128)(2,1)S(1)}, s32[8]{0:T(128)S(1)}, /...) while((s32[]{:T(128)}, bf16[8,512]{1,0:T(8,128)(2,1)S(1)}, ...), condition=%wide.region_13.14_spmd.clone, body=%wide.region_9.13_spmd.clone.sunk | while | flops 6612767232 | bytes 39988568 | solution.py:271
  1011.4 379.8 %while.77 = (s32[]{:T(128)}, f32[1024,6288]{0,1:T(8,128)}, bf16[8,512,1024]{2,1,0:T(8,128)(2,1)}, s32[8]{0:T(128)S(1)}, bf16[4096,1024]{1,0:T(8,128)(2,1)}, /*in...) while((s32[]{:T(128)}, f32[1024,6288]{0,1:T(8,128)}, ...), condition=%wide.region_22.23_spmd.clone, body=%wide.region_21.22_spmd.clone.sunk | while | flops 19812538368 | bytes 101305704 | solution.py:298
  1311.3 19.0 select_add_fusion.2
  1391.3 71.6 %reduce-scatter.12.cloned.1.call-done = bf16[2,256,1024]{2,1,0:T(8,128)(2,1)} async-done(((bf16[2,2048,1024]{2,1,0:T(8,128)(2,1)}), bf16[2,256,1024]{2,1,0:T(8,128)(2,1)}) %reduce-scatter.12.cloned.1.call-update) | async-done | bytes 1048592 | tf_op jit(solution)/shard_map/reduce_scatter | solution.py:301
  1505.1 258.1 %while.78 = (s32[]{:T(128)}, f32[2,2048,2,64]{1,3,2,0:T(8,128)}, f32[2,2048,2,64]{1,3,2,0:T(8,128)}, bf16[4,2,512,2,64]{2,4,3,1,0:T(8,128)(2,1)}, s32[4]{0:T(128...) while((s32[]{:T(128)}, f32[2,2048,2,64]{1,3,2,0:T(8,128)}, ...), condition=%wide.region_28.29_spmd.clone, body=%wide.region_26.28_spmd.clone.sunk | while | flops 2751068672 | bytes 231272976 | solution.py:142
  1802.3 30.3 all-to-all-done.3
  1893.7 23.1 all-gather.22.cloned.1.call-done
  1916.8 46.5 %scatter_custom_fusion = f32[6288,1024]{1,0:T(8,128)} fusion(s32[4096]{0:T(1024)S(1)} %bitcast.330, bf16[4096,1024]{1,0:T(8,128)(2,1)} %bitcast.286, f32[]{:T(128)} %constant.133.clone.1, pred[4096]{0:T(1024)(128)(4,1)S(1)} %broadcast_in_dim.164), kind=kCustom, calls=%fused_computation.72 | custom fusion | flops 12582912 | bytes 34149376 | tf_op jit(solution)/shard_map/scatter-add | solution.py:359
  2008.4 47.2 %all-reduce.8 = f32[8192]{0:T(1024)S(1)} all-reduce(f32[8192]{0:T(1024)S(1)} %pad_maximum_fusion.8), channel_id=12, replica_groups=mesh['dp'=4,'sp'=8] {'dp','sp'}, use_global_device_ids=true, to_apply=%region_53.54.clone | all-reduce | flops 8192 | bytes 65536
  2057.7 180.3 %reduce-scatter.16.cloned.1.call-done = bf16[256,6288]{0,1:T(8,128)(2,1)} async-done(((bf16[1024,6288]{0,1:T(8,128)(2,1)}), bf16[256,6288]{0,1:T(8,128)(2,1)}) %reduce-scatter.16.cloned.1.call-update) | async-done | bytes 3219472 | tf_op jit(solution)/shard_map/reduce_scatter | solution.py:370
  2242.3 224.1 %reduce-scatter.20.cloned.1.call-done = f32[160,1024]{1,0:T(8,128)} async-done(((f32[5120,1024]{1,0:T(8,128)}), f32[160,1024]{1,0:T(8,128)}) %reduce-scatter.20.cloned.1.call-update) | async-done | bytes 655376 | tf_op jit(solution)/shard_map/reduce_scatter | solution.py:362
  2468.2 221.6 %reduce-scatter.14.cloned.1.call-done = bf16[6288,256]{1,0:T(8,128)(2,1)} async-done(((bf16[6288,1024]{1,0:T(8,128)(2,1)}), bf16[6288,256]{1,0:T(8,128)(2,1)}) %reduce-scatter.14.cloned.1.call-update) | async-done | bytes 3219472 | tf_op jit(solution)/shard_map/reduce_scatter | solution.py:367
  2695.3 308.2 %reduce-scatter.18.cloned.1.call-done = f32[32,7168]{1,0:T(8,128)} async-done(((f32[1024,7168]{1,0:T(8,128)}), f32[32,7168]{1,0:T(8,128)}) %reduce-scatter.18.cloned.1.call-update) | async-done | bytes 917520 | tf_op jit(solution)/shard_map/reduce_scatter | solution.py:361
  3008.2 47.2 %all-reduce.9 = (f32[]{:T(128)}, f32[]{:T(128)}) all-reduce(f32[]{:T(128)S(6)} %select_n.85, f32[]{:T(128)S(6)} %add.453), channel_id=1, replica_groups=mesh['dp'=4,'sp'=8] {'dp','sp'}, use_global_device_ids=true, to_apply=%region_19.20 | all-reduce | flops 2 | bytes 16 | tf_op jit(solution)/shard_map/psum | solution.py:379
  (657 shorter events, 1260.9 us)
Async XLA Ops:
  8.0 230.3 %all-gather.12.cloned.1.call-start = ((), (), s32[]{:S(2)}) async-start(), calls=%async_computation.11 | async-start | bytes 16097280 | tf_op jit(solution)/shard_map/all_gather | solution.py:195
  12.9 368.4 %reduce-scatter.10.cloned.1.call-start = ((), (), s32[]{:S(2)}) async-start(), calls=%async_computation.12 | async-start | bytes 9437184 | tf_op jit(solution)/shard_map/reduce_scatter | solution.py:213
  273.1 113.9 %all-gather.14.cloned.1.call-start = ((), (), s32[]{:S(2)}) async-start(), calls=%async_computation.13 | async-start | bytes 15138816 | tf_op jit(solution)/shard_map/all_gather | solution.py:189
  275.1 328.6 %all-gather.16.cloned.1.call-start = ((), (), s32[]{:S(2)}) async-start(), calls=%async_computation.14 | async-start | bytes 10813440 | tf_op jit(solution)/shard_map/all_gather | solution.py:190
  410.5 60.3 %all-to-all-start = ((bf16[2,256,16,192]{1,3,0,2:T(8,128)(2,1)}), bf16[2,256,16,192]{1,3,0,2:T(8,128)(2,1)S(1)}, u32[]{:S(2)}, u32[]{:S(2)}) async-start(bf16[2,256,16,192]{1,3,0,2:T(8,128)(2,1)} %copy.159), calls=%async_computation.1 | async-start | bytes 6291456 | tf_op jit(solution)/shard_map/all_to_all | solution.py:229
  414.1 302.6 %all-gather.20.cloned.1.call-start = ((), (), s32[]{:S(2)}) async-start(), calls=%async_computation.16 | async-start | bytes 16097280 | tf_op jit(solution)/shard_map/all_gather | solution.py:196
  563.1 31.2 %all-to-all-start.1 = ((bf16[8,2,32768]{2,1,0:T(2,128)(2,1)}), bf16[8,2,32768]{2,1,0:T(2,128)(2,1)}, u32[]{:S(2)}, u32[]{:S(2)}) async-start(bf16[8,2,32768]{2,1,0:T(2,128)(2,1)} %reshape.408), calls=%async_computation.2 | async-start | bytes 2097152 | tf_op jit(solution)/shard_map/all_to_all | solution.py:235
  567.4 204.3 %all-gather.18.cloned.1.call-start = ((), (), s32[]{:S(2)}) async-start(), calls=%async_computation.15 | async-start | bytes 9437184 | tf_op jit(solution)/shard_map/all_gather | solution.py:250
  617.0 845.8 %reduce-scatter.12.cloned.1.call-start = ((), (), s32[]{:S(2)}) async-start(), calls=%async_computation.17 | async-start | bytes 9437184 | tf_op jit(solution)/shard_map/reduce_scatter | solution.py:301
  1484.3 18.9 all-to-all-start.2
  1778.7 53.8 %all-to-all-start.3 = ((bf16[2,2048,2,192]{3,2,0,1:T(2,128)(2,1)}), bf16[2,2048,2,192]{3,2,0,1:T(2,128)(2,1)}, u32[]{:S(2)}, u32[]{:S(2)}) async-start(bf16[2,2048,2,192]{3,2,0,1:T(2,128)(2,1)} %copy.174), calls=%async_computation.5 | async-start | bytes 8388608 | tf_op jit(solution)/shard_map/all_to_all | solution.py:319
  1783.5 133.3 %all-gather.22.cloned.1.call-start = ((), (), s32[]{:S(2)}) async-start(), calls=%async_computation.18 | async-start | bytes 9437184 | tf_op jit(solution)/shard_map/all_gather | solution.py:357
  1862.8 193.5 %reduce-scatter.22.cloned.1.call-start = ((), (), s32[]{:S(2)}) async-start(), calls=%async_computation.23 | async-start | bytes 540672
  1864.0 374.0 %reduce-scatter.16.cloned.1.call-start = ((), (), s32[]{:S(2)}) async-start(), calls=%async_computation.20 | async-start | bytes 16097280 | tf_op jit(solution)/shard_map/reduce_scatter | solution.py:370
  1878.2 588.2 %reduce-scatter.20.cloned.1.call-start = ((), (), s32[]{:S(2)}) async-start(), calls=%async_computation.22 | async-start | bytes 21626880 | tf_op jit(solution)/shard_map/reduce_scatter | solution.py:362
  1892.9 797.0 %reduce-scatter.14.cloned.1.call-start = ((), (), s32[]{:S(2)}) async-start(), calls=%async_computation.19 | async-start | bytes 16097280 | tf_op jit(solution)/shard_map/reduce_scatter | solution.py:367
  1976.9 1026.6 %reduce-scatter.18.cloned.1.call-start = ((), (), s32[]{:S(2)}) async-start(), calls=%async_computation.21 | async-start | bytes 30277632 | tf_op jit(solution)/shard_map/reduce_scatter | solution.py:361
  2007.5 1050.0 %copy-start.75 = (f32[6,32]{1,0:T(8,128)S(1)}, f32[6,32]{1,0:T(8,128)}, u32[]{:S(2)}) copy-start(f32[6,32]{1,0:T(8,128)} %param.46) | copy-start | bytes 2308
  2007.5 1050.0 %copy-start.78 = (f32[6,32]{1,0:T(8,128)S(1)}, f32[6,32]{1,0:T(8,128)}, u32[]{:S(2)}) copy-start(f32[6,32]{1,0:T(8,128)} %param.47) | copy-start | bytes 2308
  2007.5 1050.0 %copy-start.79 = (f32[6,32]{1,0:T(8,128)S(1)}, f32[6,32]{1,0:T(8,128)}, u32[]{:S(2)}) copy-start(f32[6,32]{1,0:T(8,128)} %param.48) | copy-start | bytes 2308
  2007.5 1050.6 %copy-start.86 = (f32[256]{0:T(256)S(1)}, f32[256]{0:T(256)}, u32[]{:S(2)}) copy-start(f32[256]{0:T(256)} %param.49) | copy-start | bytes 3076
  2007.6 1050.6 %copy-start.87 = (f32[256]{0:T(256)S(1)}, f32[256]{0:T(256)}, u32[]{:S(2)}) copy-start(f32[256]{0:T(256)} %param.50) | copy-start | bytes 3076
  2007.6 1050.6 %copy-start.88 = (f32[256]{0:T(256)S(1)}, f32[256]{0:T(256)}, u32[]{:S(2)}) copy-start(f32[256]{0:T(256)} %param.51) | copy-start | bytes 3076
  2238.0 837.0 %slice-start.6 = ((s8[6438912]{0:T(1024)(128)(4,1)}), s8[2244608]{0:T(1024)(128)(4,1)S(1)}, s32[]{:S(2)}) async-start(s8[6438912]{0:T(1024)(128)(4,1)} %bitcast.272), calls=%async_computation.30 | async-start | bytes 4489216
  (122 other events, 1930.4 us)
Sparse Core Ops, SparseCore 0:
  13.1 225.2 all-gather.11
  273.3 107.9 reduce-scatter.9
  1391.4 71.3 reduce-scatter.11
  1862.9 53.7 all-gather.21
Sparse Core Ops, SparseCore 1:
  277.1 109.9 all-gather.13
  390.3 103.7 all-gather.15
  496.0 220.7 all-gather.19
  719.3 52.4 all-gather.17
  1866.4 154.4 reduce-scatter.21
  2023.3 214.7 reduce-scatter.15
  2240.2 226.2 reduce-scatter.19
  2468.6 221.2 reduce-scatter.13
  2692.0 311.5 reduce-scatter.17
where the time goes:
time: 3110 us; the launch traced here: 3100 us
  waiting for transfers between devices  1520 us (49%)
  matrix products  836 us (27%)
  other arithmetic  315 us (10%)
  blocking collectives  198 us (6%)
  local copies, waits for them, and re-layouts  166 us (5%)
    reduce_scatter x1, waiting for transfers between devices, local(): lax.psum_scatter(g_in, ('dp', 'sp'), scatter_dimension=0, tiled=True)  308 us
    dot_general x16, matrix products, head_logits(): jnp.dot(rows_block, unembed_local, preferred_element_type=jnp.float32)  264 us
    all_gather x1, waiting for transfers between devices, local(): lax.all_gather(embed_table.astype(lowtype), 'dp', axis=1, tiled=True)  225 us
    reduce_scatter x1, waiting for transfers between devices, local(): lax.psum_scatter(g_out, ('dp', 'sp'), scatter_dimension=0, tiled=True)  224 us
    reduce_scatter x1, waiting for transfers between devices, local(): lax.psum_scatter(embed_grad.astype(jnp.bfloat16), 'dp', scatter_dimension...  222 us
    reduce_scatter x1, waiting for transfers between devices, local(): lax.psum_scatter(unembed_grad.astype(jnp.bfloat16), 'dp', scatter_dimensi...  180 us
    dot_general x8, matrix products, head_backward(): lax.dot_general(rows_block, grad_logits, (((0,), (0,)), ((), ())), prefer...  147 us
    dot_general x8, matrix products, head_backward(): lax.dot_general(grad_logits, unembed_local, (((1,), (1,)), ((), ())), pre...  102 us
  transfers between devices with their start and end apart: 17, of which 14 were waited for; matrix products, arithmetic and copies ran while one was open for 11% of the time, Pallas kernels for 0%

commit v1 on v0

v1 whole, which is shorter than its diff:
```python
from functools import partial

import jax
import jax.numpy as jnp
from jax import lax
from jax.experimental import pallas as pl
from jax.experimental.pallas import tpu as pltpu
from jax.sharding import PartitionSpec as P

HEADS = 16
ROT = 16
STEP_COUNT = 10


NORM_EPS = 1e-05
BETA_ONE = 0.9
BETA_TWO = 0.95
ADAM_EPS = 1e-08
WEIGHT_DECAY = 0.01
CLIP_LEVEL = 0.01
REPLAY_WEIGHT = 4.0
NEGATIVE_FILL = -1e30
LOW = jnp.bfloat16
WIDE = jnp.float32
CHUNKS = 5
LANES = 128
HEAD_ROWS = 512
ATTEND_ROWS = 1024
VMEM_LIMIT = 60 * 1024 * 1024


def lane_of(shape):
    return lax.broadcasted_iota(jnp.int32, shape, 1)


def head_forward_kernel(real, rows_ref, table_ref, label_ref, powers_ref, stats_ref, lines_ref):
    padded = table_ref.shape[0]
    part = padded // CHUNKS
    rows = rows_ref[...]
    count = rows.shape[0]
    label = label_ref[...]
    lane = lane_of((count, LANES))
    stats = jnp.zeros((count, LANES), WIDE)
    tops, sums = [], []
    chosen = jnp.zeros((count, 1), WIDE)
    for c in range(CHUNKS):
        logits = lax.dot_general(
            rows,
            table_ref[c * part : (c + 1) * part, :],
            (((1,), (1,)), ((), ())),
            preferred_element_type=WIDE,
        )
        column = lane_of(logits.shape) + c * part
        chosen = chosen + jnp.sum(jnp.where(column == label, logits, 0.0), axis=1, keepdims=True)
        if (c + 1) * part > real:
            logits = jnp.where(column < real, logits, NEGATIVE_FILL)
        top = jnp.max(logits, axis=1, keepdims=True)
        powers = jnp.exp(logits - top)
        sums.append(jnp.sum(powers, axis=1, keepdims=True))
        tops.append(top)
        powers_ref[:, c * part : (c + 1) * part] = powers.astype(LOW)
        stats = jnp.where(lane == 8 + c, top, stats)
    highest = tops[0]
    for c in range(1, CHUNKS):
        highest = jnp.maximum(highest, tops[c])
    total = jnp.zeros((count, 1), WIDE)
    for c in range(CHUNKS):
        total = total + sums[c] * jnp.exp(tops[c] - highest)
    stats = jnp.where(lane == 0, highest, stats)
    stats = jnp.where(lane == 1, total, stats)
    stats = jnp.where(lane == 2, chosen, stats)
    stats_ref[...] = stats
    lines_ref[...] = jnp.transpose(stats)[0:8, :]


def head_forward(rows, table, label, real):
    total, width = rows.shape
    padded = table.shape[0]
    count = min(HEAD_ROWS, total)
    return pl.pallas_call(
        partial(head_forward_kernel, real),
        grid=(total // count,),
        in_specs=[
            pl.BlockSpec((count, width), lambda i: (i, 0)),
            pl.BlockSpec((padded, width), lambda i: (0, 0), pipeline_mode=pl.Buffered(1)),
            pl.BlockSpec((count, 1), lambda i: (i, 0)),
        ],
        out_specs=[
            pl.BlockSpec((count, padded), lambda i: (i, 0)),
            pl.BlockSpec((count, LANES), lambda i: (i, 0)),
            pl.BlockSpec((8, count), lambda i: (0, i)),
        ],
        out_shape=[
            jax.ShapeDtypeStruct((total, padded), LOW),
            jax.ShapeDtypeStruct((total, LANES), WIDE),
            jax.ShapeDtypeStruct((8, total), WIDE),
        ],
        cost_estimate=pl.CostEstimate(
            flops=2 * total * width * padded,
            bytes_accessed=2 * (total * (width + padded) + width * padded),
            transcendentals=total * padded,
        ),
        compiler_params=pltpu.CompilerParams(vmem_limit_bytes=VMEM_LIMIT),
        name="head_forward",
    )(rows, table, label)


def head_backward_kernel(stats_ref, lines_ref, label_ref, powers_ref, table_ref, slope_ref, grad_ref):
    padded = table_ref.shape[0]
    part = padded // CHUNKS
    stats = stats_ref[...]
    label = label_ref[...]
    lines = lines_ref[...]
    lines = jnp.transpose(jnp.concatenate([lines] * (LANES // 8), axis=0))
    lse = lines[:, 0:1]
    scale = lines[:, 1:2]
    total = None
    for c in range(CHUNKS):
        ratio = scale * jnp.exp(stats[:, 8 + c : 9 + c] - lse)
        slope = powers_ref[:, c * part : (c + 1) * part].astype(WIDE) * ratio
        column = lane_of(slope.shape) + c * part
        slope = jnp.where(column == label, slope - scale, slope).astype(LOW)
        slope_ref[:, c * part : (c + 1) * part] = slope
        piece = jnp.dot(
            slope, table_ref[c * part : (c + 1) * part, :], preferred_element_type=WIDE
        )
        total = piece if total is None else total + piece
    grad_ref[...] = total.astype(LOW)


def head_backward(stats, lines, label, powers, table):
    total, padded = powers.shape
    width = table.shape[1]
    count = min(HEAD_ROWS, total)
    return pl.pallas_call(
        head_backward_kernel,
        grid=(total // count,),
        in_specs=[
            pl.BlockSpec((count, LANES), lambda i: (i, 0)),
            pl.BlockSpec((8, count), lambda i: (0, i)),
            pl.BlockSpec((count, 1), lambda i: (i, 0)),
            pl.BlockSpec((count, padded), lambda i: (i, 0)),
            pl.BlockSpec((padded, width), lambda i: (0, 0), pipeline_mode=pl.Buffered(1)),
        ],
        out_specs=[
            pl.BlockSpec((count, padded), lambda i: (i, 0)),
            pl.BlockSpec((count, width), lambda i: (i, 0)),
        ],
        out_shape=[
            jax.ShapeDtypeStruct((total, padded), LOW),
            jax.ShapeDtypeStruct((total, width), LOW),
        ],
        cost_estimate=pl.CostEstimate(
            flops=2 * total * width * padded,
            bytes_accessed=2 * (total * (width + 2 * padded) + width * padded),
            transcendentals=0,
        ),
        compiler_params=pltpu.CompilerParams(vmem_limit_bytes=VMEM_LIMIT),
        name="head_backward",
    )(stats, lines, label, powers, table)


def attend_forward_kernel(heads, scale, query_ref, key_ref, value_ref, out_ref, lse_ref):
    pieces, stretch, wide = query_ref.shape
    block = pieces * stretch
    head = wide // heads
    index = pl.program_id(1)
    query = query_ref[...].reshape(block, wide) * jnp.asarray(scale, LOW)
    lane = lane_of((block, wide))
    mine = [(lane >= h * head) & (lane < (h + 1) * head) for h in range(heads)]
    own = [jnp.where(mine[h], query, jnp.zeros_like(query)) for h in range(heads)]

    def step(c, state, masked):
        spots = pl.ds(c * pieces, pieces)
        keys = key_ref[spots].reshape(block, wide)
        values = value_ref[spots].reshape(block, wide)
        fresh = []
        for h in range(heads):
            top, total, summed = state[h]
            scores = lax.dot_general(
                own[h], keys, (((1,), (1,)), ((), ())), preferred_element_type=WIDE
            )
            if masked:
                here = lax.broadcasted_iota(jnp.int32, scores.shape, 0)
                scores = jnp.where(here >= lane_of(scores.shape), scores, NEGATIVE_FILL)
            higher = jnp.maximum(top, jnp.max(scores, axis=1, keepdims=True))
            powers = jnp.exp(scores - higher)
            shrink = jnp.exp(top - higher)
            total = total * shrink + jnp.sum(powers, axis=1, keepdims=True)
            summed = summed * shrink + jnp.dot(
                powers.astype(LOW), values, preferred_element_type=WIDE
            )
            fresh.append((higher, total, summed))
        return tuple(fresh)

    state = tuple(
        (
            jnp.full((block, 1), NEGATIVE_FILL, WIDE),
            jnp.zeros((block, 1), WIDE),
            jnp.zeros((block, wide), WIDE),
        )
        for _ in range(heads)
    )
    state = lax.fori_loop(0, index, lambda c, s: step(c, s, False), state)
    state = step(index, state, True)
    result = None
    spot = lane_of((block, LANES))
    logs = jnp.zeros((block, LANES), WIDE)
    for h in range(heads):
        top, total, summed = state[h]
        piece = summed / total
        result = piece if result is None else jnp.where(mine[h], piece, result)
        logs = jnp.where(spot == h, top + jnp.log(total), logs)
    out_ref[...] = result.astype(LOW).reshape(pieces, stretch, wide)
    lse_ref[...] = jnp.transpose(logs)[0:8, :]


def attend_specs(triple, block):
    span, _, seqs, stretch, wide = triple.shape
    pieces = min(block, span * stretch) // stretch
    part = pl.BlockSpec((pieces, None, stretch, wide), lambda s, i: (i, s, 0, 0))
    query = pl.BlockSpec((pieces, None, None, stretch, wide), lambda s, i: (i, 0, s, 0, 0))
    keys = pl.BlockSpec((span, None, None, stretch, wide), lambda s, i: (0, 1, s, 0, 0))
    values = pl.BlockSpec((span, None, None, stretch, wide), lambda s, i: (0, 2, s, 0, 0))
    logs = pl.BlockSpec((None, 8, pieces * stretch), lambda s, i: (s, 0, i))
    return (seqs, span // pieces), part, query, keys, values, logs


def attend_forward(triple, heads, block, scale):
    span, _, seqs, stretch, wide = triple.shape
    length = span * stretch
    grid, part, query, keys, values, logs = attend_specs(triple, block)
    pairs = seqs * heads * length * length // 2
    return pl.pallas_call(
        partial(attend_forward_kernel, heads, scale),
        grid=grid,
        in_specs=[query, keys, values],
        out_specs=[part, logs],
        out_shape=[
            jax.ShapeDtypeStruct((span, seqs, stretch, wide), LOW),
            jax.ShapeDtypeStruct((seqs, 8, length), WIDE),
        ],
        cost_estimate=pl.CostEstimate(
            flops=pairs, bytes_accessed=seqs * length * wide, transcendentals=0
        ),
        compiler_params=pltpu.CompilerParams(vmem_limit_bytes=VMEM_LIMIT),
        name="attend_forward",
    )(triple, triple, triple)


def attend_backward_kernel(
    heads, scale, query_ref, key_ref, value_ref, out_ref, grad_ref, lse_ref, triple_ref, dk_sum, dv_sum
):
    pieces, stretch, wide = query_ref.shape
    block = pieces * stretch
    span = key_ref.shape[0]
    head = wide // heads
    index = pl.program_id(1)

    @pl.when(index == 0)
    def _():
        dk_sum[...] = jnp.zeros_like(dk_sum)
        dv_sum[...] = jnp.zeros_like(dv_sum)

    query = query_ref[...].reshape(block, wide) * jnp.asarray(scale, LOW)
    grad = grad_ref[...].reshape(block, wide)
    lane = lane_of((block, wide))
    mine = [(lane >= h * head) & (lane < (h + 1) * head) for h in range(heads)]
    zero = jnp.zeros_like(query)
    own_query = [jnp.where(mine[h], query, zero) for h in range(heads)]
    own_grad = [jnp.where(mine[h], grad, zero) for h in range(heads)]
    product = out_ref[...].reshape(block, wide).astype(WIDE) * grad.astype(WIDE)
    spot = lane_of((block, LANES))
    centres = jnp.zeros((block, LANES), WIDE)
    for h in range(heads):
        centre = jnp.sum(jnp.where(mine[h], product, 0.0), axis=1, keepdims=True)
        centres = jnp.where(spot == h, centre, centres)
    centres = jnp.transpose(centres)
    logs = lse_ref[...]

    def step(c, state, masked):
        spots = pl.ds(c * pieces, pieces)
        rows = pl.ds(pl.multiple_of(c * block, block), block)
        keys = key_ref[spots].reshape(block, wide)
        values = value_ref[spots].reshape(block, wide)
        fresh = []
        key_part, value_part = None, None
        for h in range(heads):
            scores = lax.dot_general(
                keys, own_query[h], (((1,), (1,)), ((), ())), preferred_element_type=WIDE
            )
            probs = jnp.exp(scores - logs[h : h + 1, :])
            if masked:
                here = lax.broadcasted_iota(jnp.int32, scores.shape, 0)
                probs = jnp.where(here <= lane_of(scores.shape), probs, 0.0)
            grad_probs = lax.dot_general(
                values, own_grad[h], (((1,), (1,)), ((), ())), preferred_element_type=WIDE
            )
            slope = (probs * (grad_probs - centres[h : h + 1, :])).astype(LOW)
            a = jnp.dot(slope, own_query[h], preferred_element_type=WIDE)
            b = jnp.dot(probs.astype(LOW), own_grad[h], preferred_element_type=WIDE)
            key_part = a if key_part is None else key_part + a
            value_part = b if value_part is None else value_part + b
            fresh.append(
                state[h]
                + lax.dot_general(slope, keys, (((0,), (0,)), ((), ())), preferred_element_type=WIDE)
            )
        dk_sum[rows, :] += key_part
        dv_sum[rows, :] += value_part
        return tuple(fresh)

    state = tuple(jnp.zeros((block, wide), WIDE) for _ in range(heads))
    state = lax.fori_loop(0, index, lambda c, s: step(c, s, False), state)
    state = step(index, state, True)
    result = state[0]
    for h in range(1, heads):
        result = jnp.where(mine[h], state[h], result)
    triple_ref[pl.ds(index * pieces, pieces), 0] = (
        (result * scale).astype(LOW).reshape(pieces, stretch, wide)
    )

    @pl.when(index == pl.num_programs(1) - 1)
    def _():
        triple_ref[:, 1] = dk_sum[...].astype(LOW).reshape(span, stretch, wide)
        triple_ref[:, 2] = dv_sum[...].astype(LOW).reshape(span, stretch, wide)


def attend_backward(triple, attended, grad, lse, heads, block, scale):
    span, _, seqs, stretch, wide = triple.shape
    length = span * stretch
    grid, part, query, keys, values, logs = attend_specs(triple, block)
    pairs = seqs * heads * length * length // 2
    return pl.pallas_call(
        partial(attend_backward_kernel, heads, scale),
        grid=grid,
        in_specs=[query, keys, values, part, part, logs],
        out_specs=pl.BlockSpec((span, 3, None, stretch, wide), lambda s, i: (0, 0, s, 0, 0)),
        out_shape=jax.ShapeDtypeStruct((span, 3, seqs, stretch, wide), LOW),
        scratch_shapes=[pltpu.VMEM((length, wide), WIDE), pltpu.VMEM((length, wide), WIDE)],
        cost_estimate=pl.CostEstimate(
            flops=pairs, bytes_accessed=seqs * length * wide, transcendentals=0
        ),
        compiler_params=pltpu.CompilerParams(vmem_limit_bytes=VMEM_LIMIT),
        name="attend_backward",
    )(triple, triple, triple, attended, grad, lse)


def turn_tables(positions, repeats, parts, wide, head):
    halfway = ROT // 2
    place = jnp.arange(parts * wide)
    entry = place % head
    turned = (place // wide < 2) & (entry < ROT)
    frequency = 10000.0 ** (-2.0 * (entry % halfway).astype(WIDE) / ROT)
    angles = positions.astype(WIDE)[:, None] * frequency[None, :]
    sine = jnp.where(turned, jnp.sin(angles), 0.0)
    cosine = jnp.where(turned, jnp.cos(angles), 1.0)
    later = jnp.where(entry < halfway, -sine, 0.0)
    earlier = jnp.where(entry < halfway, 0.0, sine)
    return tuple(jnp.tile(table, (1, repeats)) for table in (cosine, later, earlier))


def turn_packs(span, wide):
    return 1 if (3 * wide) % LANES == 0 else 2


def queries_kernel(seqs, wide, rows_ref, table_ref, bias_ref, cosine_ref, later_ref, earlier_ref, out_ref):
    halfway = ROT // 2
    columns = table_ref.shape[1]
    values = jnp.dot(rows_ref[...], table_ref[...], preferred_element_type=WIDE) + bias_ref[...]
    stretch = cosine_ref.shape[0]
    for s in range(seqs):
        part = values[s * stretch : (s + 1) * stretch]
        part = (
            part * cosine_ref[...]
            + pltpu.roll(part, columns - halfway, 1) * later_ref[...]
            + pltpu.roll(part, halfway, 1) * earlier_ref[...]
        ).astype(LOW)
        for j in range(columns // wide):
            out_ref[j // 3, j % 3, s] = part[:, j * wide : (j + 1) * wide]


def project_queries(rows, table, bias, tables, span, seqs, wide):
    total, width = rows.shape
    stretch = total // seqs
    packs = turn_packs(span, wide)
    columns = packs * 3 * wide
    fixed = pl.BlockSpec((stretch, columns), lambda g: (0, 0))
    return pl.pallas_call(
        partial(queries_kernel, seqs, wide),
        grid=(span // packs,),
        in_specs=[
            pl.BlockSpec((total, width), lambda g: (0, 0)),
            pl.BlockSpec((width, columns), lambda g: (0, g)),
            pl.BlockSpec((1, columns), lambda g: (0, g)),
            fixed,
            fixed,
            fixed,
        ],
        out_specs=pl.BlockSpec((packs, 3, seqs, stretch, wide), lambda g: (g, 0, 0, 0, 0)),
        out_shape=jax.ShapeDtypeStruct((span, 3, seqs, stretch, wide), LOW),
        cost_estimate=pl.CostEstimate(
            flops=2 * total * width * span * 3 * wide,
            bytes_accessed=2 * width * span * 3 * wide,
            transcendentals=0,
        ),
        compiler_params=pltpu.CompilerParams(vmem_limit_bytes=VMEM_LIMIT),
        name="project_queries",
    )(rows, table, bias, *tables)


def unturn_kernel(seqs, wide, triple_ref, cosine_ref, later_ref, earlier_ref, out_ref):
    halfway = ROT // 2
    columns = out_ref.shape[1]
    stretch = cosine_ref.shape[0]
    for s in range(seqs):
        part = jnp.concatenate(
            [triple_ref[j // 3, j % 3, s].astype(WIDE) for j in range(columns // wide)], axis=1
        )
        part = (
            part * cosine_ref[...]
            - pltpu.roll(part, columns - halfway, 1) * later_ref[...]
            - pltpu.roll(part, halfway, 1) * earlier_ref[...]
        )
        out_ref[s * stretch : (s + 1) * stretch, :] = part.astype(LOW)


def unturn(triple, tables):
    span, _, seqs, stretch, wide = triple.shape
    packs = turn_packs(span, wide)
    columns = packs * 3 * wide
    fixed = pl.BlockSpec((stretch, columns), lambda g: (0, 0))
    return pl.pallas_call(
        partial(unturn_kernel, seqs, wide),
        grid=(span // packs,),
        in_specs=[
            pl.BlockSpec((packs, 3, seqs, stretch, wide), lambda g: (g, 0, 0, 0, 0)),
            fixed,
            fixed,
            fixed,
        ],
        out_specs=pl.BlockSpec((seqs * stretch, columns), lambda g: (0, g)),
        out_shape=jax.ShapeDtypeStruct((seqs * stretch, span * 3 * wide), LOW),
        compiler_params=pltpu.CompilerParams(vmem_limit_bytes=VMEM_LIMIT),
        name="unturn",
    )(triple, *tables)


def gelu_exact(values):
    return jax.nn.gelu(values, approximate=False)


def standardize(values):
    average = jnp.mean(values, axis=-1, keepdims=True)
    centered = values - average
    variance = jnp.mean(centered * centered, axis=-1, keepdims=True)
    inverse = lax.rsqrt(variance + NORM_EPS)
    return centered * inverse, inverse


def standardize_pull(scaled, normal, inverse):
    return inverse * (
        scaled
        - jnp.mean(scaled, axis=-1, keepdims=True)
        - normal * jnp.mean(scaled * normal, axis=-1, keepdims=True)
    )


def adam_update(weight, first, second, grad, clip_factor, rate, decay):
    grad = grad * clip_factor
    first_new = BETA_ONE * first + (1.0 - BETA_ONE) * grad
    second_new = BETA_TWO * second + (1.0 - BETA_TWO) * grad * grad
    fix_one = 1.0 - BETA_ONE**STEP_COUNT
    fix_two = 1.0 - BETA_TWO**STEP_COUNT
    direction = first_new / fix_one / (jnp.sqrt(second_new / fix_two) + ADAM_EPS)
    return (weight - rate * (direction + decay * weight), first_new, second_new)


def summed_over(vector, axes):
    for axis in axes:
        vector = jnp.sum(lax.all_gather(vector, axis), axis=0)
    return vector


def scattered(gradient):
    return lax.psum_scatter(gradient, ("dp", "sp"), scatter_dimension=0, tiled=True).astype(WIDE)


def local(
    token_ids,
    targets,
    stream_ids,
    embed_table,
    embed_first,
    embed_second,
    unembed,
    unembed_first,
    unembed_second,
    proj_in,
    proj_in_first,
    proj_in_second,
    proj_out,
    proj_out_first,
    proj_out_second,
    norm_params,
    norm_first,
    norm_second,
    biases,
    bias_first,
    bias_second,
):
    span = lax.axis_size("sp")
    teams = lax.axis_size("dp")
    sp_index = lax.axis_index("sp")
    dp_index = lax.axis_index("dp")
    seq_here, length = token_ids.shape
    stretch = length // span
    vocab_local = embed_table.shape[0]
    slab, in_columns = proj_in.shape
    width = proj_out.shape[1]
    triple_columns = 3 * width
    hidden_units = in_columns - triple_columns
    heads_here = HEADS // span
    head_dim = width // HEADS
    wide = heads_here * head_dim
    scale = head_dim ** (-0.5)
    tokens_here = seq_here * stretch
    offset = sp_index * vocab_local

    ids_all = lax.all_gather(token_ids, "dp")
    ids_all = ids_all.reshape(teams, seq_here, span, stretch).transpose(2, 0, 1, 3).reshape(-1)
    local_ids = ids_all - offset
    in_slice = (local_ids >= 0) & (local_ids < vocab_local)
    safe_ids = jnp.clip(local_ids, 0, vocab_local - 1)
    picked = jnp.where(
        in_slice[:, None],
        embed_table.astype(LOW).at[safe_ids].get(mode="promise_in_bounds"),
        jnp.zeros((), LOW),
    )
    hidden0 = lax.psum_scatter(picked, "sp", scatter_dimension=0, tiled=True)
    hidden0 = lax.all_to_all(hidden0, "dp", split_axis=0, concat_axis=1, tiled=True).astype(WIDE)

    bias_rows = biases.shape[0] // slab
    norm_rows = norm_params.shape[0]
    shard_triple = proj_in[:, :triple_columns].astype(LOW)
    shard_triple = shard_triple.reshape(slab, span, heads_here, 3, head_dim).transpose(0, 1, 3, 2, 4)
    shard_triple = shard_triple.reshape(slab, triple_columns)
    extras = jnp.concatenate([norm_params.T, biases.reshape(slab, bias_rows)], axis=1).astype(LOW)
    extras = jnp.pad(extras, ((0, 0), (0, LANES - extras.shape[1])))
    wide_in = lax.all_gather(
        jnp.concatenate([shard_triple, proj_in[:, triple_columns:].astype(LOW), extras], axis=1),
        ("dp", "sp"),
        axis=0,
        tiled=True,
    )
    wide_out = lax.all_gather(proj_out.astype(LOW), ("dp", "sp"), axis=0, tiled=True)
    vocab_step = CHUNKS * LANES
    vocab_padded = -(-vocab_local // vocab_step) * vocab_step
    head_table = lax.all_gather(
        jnp.pad(unembed.T.astype(LOW), ((0, vocab_padded - vocab_local), (0, 0))),
        "dp",
        axis=1,
        tiled=True,
    )
    norm_vals = wide_in[:, in_columns : in_columns + norm_rows].astype(WIDE).T
    bias_vals = wide_in[:, in_columns + norm_rows : in_columns + norm_rows + bias_rows]
    bias_vals = bias_vals.astype(WIDE).reshape(-1)
    triple_bias = bias_vals[:triple_columns].reshape(span, heads_here, 3, head_dim)
    triple_bias = triple_bias.transpose(0, 2, 1, 3).reshape(1, triple_columns)

    normal0, inverse0 = standardize(hidden0)
    normed_one = (normal0 * norm_vals[0] + norm_vals[1]).astype(LOW)
    normed_two = (normal0 * norm_vals[2] + norm_vals[3]).astype(LOW)
    positions = sp_index * stretch + jnp.arange(stretch)
    tables = turn_tables(positions, turn_packs(span, wide), 3, wide, head_dim)
    packed = project_queries(normed_one, wide_in, triple_bias, tables, span, seq_here, wide)
    triple = lax.all_to_all(packed, "sp", split_axis=0, concat_axis=0, tiled=True)
    attended_heads, log_totals = attend_forward(triple, heads_here, ATTEND_ROWS, scale)
    attended = lax.all_to_all(attended_heads, "sp", split_axis=0, concat_axis=0, tiled=True)
    attended = attended.reshape(span, tokens_here, wide).transpose(1, 0, 2).reshape(tokens_here, width)
    up_values = (
        jnp.dot(
            normed_two, wide_in[:, triple_columns:in_columns], preferred_element_type=WIDE
        )
        + bias_vals[triple_columns:in_columns]
    )
    act_f, pull_gelu = jax.vjp(gelu_exact, up_values)
    joined = jnp.concatenate([attended, act_f.astype(LOW)], axis=-1)
    hidden1 = (
        hidden0 + jnp.dot(joined, wide_out, preferred_element_type=WIDE) + bias_vals[in_columns:]
    )
    normal1, inverse1 = standardize(hidden1)
    final = (normal1 * norm_vals[4] + norm_vals[5]).astype(LOW)
    rows_all = lax.all_gather(final.reshape(seq_here, stretch, width), "sp", axis=1, tiled=True)
    rows_all = rows_all.reshape(-1, width)
    grand = rows_all.shape[0]
    labels = targets.reshape(-1, 1) - offset
    powers, stats, lines = head_forward(rows_all, head_table, labels, vocab_local)
    merged = lax.all_gather(lines[0:3], "sp")
    highest = jnp.max(merged[:, 0], axis=0)
    summed = jnp.sum(merged[:, 1] * jnp.exp(merged[:, 0] - highest), axis=0)
    log_sum = highest + jnp.log(summed)
    token_loss = (log_sum - jnp.sum(merged[:, 2], axis=0)).reshape(seq_here, length)
    weight_all = 1.0 + (REPLAY_WEIGHT - 1.0) * stream_ids.astype(WIDE)
    total_weight = jnp.sum(weight_all)
    seq_weight = lax.dynamic_slice_in_dim(weight_all, dp_index * seq_here, seq_here, 0)
    loss_local = jnp.sum(seq_weight * jnp.mean(token_loss, axis=1))
    token_scale = jnp.broadcast_to(
        (seq_weight / (total_weight * length))[:, None], (seq_here, length)
    ).reshape(-1)
    guide = jnp.concatenate(
        [log_sum[None], token_scale[None], jnp.zeros((6, grand), WIDE)], axis=0
    )
    slopes, grad_rows = head_backward(stats, guide, labels, powers, head_table)
    final_grad = lax.psum_scatter(
        grad_rows.reshape(seq_here, length, width), "sp", scatter_dimension=1, tiled=True
    ).astype(WIDE)
    final_grad = final_grad.reshape(tokens_here, width)
    unembed_grad = lax.dot_general(
        slopes, rows_all, (((0,), (0,)), ((), ())), preferred_element_type=WIDE
    ).astype(LOW)
    final_grad, unembed_grad = lax.optimization_barrier((final_grad, unembed_grad))
    r_unembed = lax.psum_scatter(unembed_grad, "dp", scatter_dimension=1, tiled=True)

    g_gain_final = jnp.sum(final_grad * normal1, axis=0)
    g_shift_final = jnp.sum(final_grad, axis=0)
    d_hidden1 = standardize_pull(final_grad * norm_vals[4], normal1, inverse1)
    d_branch = d_hidden1.astype(LOW)
    g_out = lax.dot_general(
        joined, d_branch, (((0,), (0,)), ((), ())), preferred_element_type=WIDE
    ).astype(LOW)
    g_bias_out = jnp.sum(d_branch.astype(WIDE), axis=0)
    contract_last = (((1,), (1,)), ((), ()))
    d_attended = lax.dot_general(
        d_branch, wide_out[:width], contract_last, preferred_element_type=WIDE
    ).astype(LOW)
    d_attended = d_attended.reshape(seq_here, stretch, span, wide).transpose(2, 0, 1, 3)
    d_heads = lax.all_to_all(d_attended, "sp", split_axis=0, concat_axis=0, tiled=True)
    d_act = lax.dot_general(d_branch, wide_out[width:], contract_last, preferred_element_type=WIDE)
    d_up = pull_gelu(d_act)[0].astype(LOW)
    g_up = lax.dot_general(
        normed_two, d_up, (((0,), (0,)), ((), ())), preferred_element_type=WIDE
    ).astype(LOW)
    d_normed_two = lax.dot_general(
        d_up, wide_in[:, triple_columns:in_columns], contract_last, preferred_element_type=WIDE
    )
    d_heads, g_out, g_up, d_normed_two = lax.optimization_barrier(
        (d_heads, g_out, g_up, d_normed_two)
    )
    r_out = scattered(g_out)
    r_up = scattered(g_up)
    d_triple = attend_backward(
        triple, attended_heads, d_heads, log_totals, heads_here, ATTEND_ROWS, scale
    )
    d_triple = lax.all_to_all(d_triple, "sp", split_axis=0, concat_axis=0, tiled=True)
    d_joint = unturn(d_triple, tables)
    g_triple = lax.dot_general(
        normed_one, d_joint, (((0,), (0,)), ((), ())), preferred_element_type=WIDE
    ).astype(LOW)
    d_normed_one = lax.dot_general(
        d_joint, wide_in[:, :triple_columns], contract_last, preferred_element_type=WIDE
    )
    g_gain_one = jnp.sum(d_normed_one * normal0, axis=0)
    g_shift_one = jnp.sum(d_normed_one, axis=0)
    g_gain_two = jnp.sum(d_normed_two * normal0, axis=0)
    g_shift_two = jnp.sum(d_normed_two, axis=0)
    d_sum = d_normed_one * norm_vals[0] + d_normed_two * norm_vals[2]
    d_hidden0 = (d_hidden1 + standardize_pull(d_sum, normal0, inverse0)).astype(LOW)
    d_hidden0, r_unembed, r_out, r_up = lax.optimization_barrier(
        (d_hidden0, r_unembed, r_out, r_up)
    )
    grad_all = lax.all_to_all(d_hidden0, "dp", split_axis=1, concat_axis=0, tiled=True)
    grad_all = lax.all_gather(grad_all, "sp", axis=0, tiled=True)
    target_ids = jnp.where(in_slice, local_ids, vocab_local)
    r_embed = (
        jnp.zeros(embed_table.shape, WIDE).at[target_ids].add(grad_all.astype(WIDE), mode="drop")
    )

    g_bias_triple = jnp.sum(d_joint.astype(WIDE), axis=0).reshape(span, 3, heads_here, head_dim)
    g_bias = jnp.concatenate(
        [
            g_bias_triple.transpose(0, 2, 1, 3).reshape(-1),
            jnp.sum(d_up.astype(WIDE), axis=0),
            g_bias_out,
        ]
    )
    g_norm = jnp.stack(
        [g_gain_one, g_shift_one, g_gain_two, g_shift_two, g_gain_final, g_shift_final], axis=1
    )
    g_extra = jnp.concatenate([g_norm, g_bias.reshape(width, bias_rows)], axis=1).astype(LOW)
    g_extra = jnp.pad(g_extra, ((0, 0), (0, LANES - g_extra.shape[1])))
    r_triple = scattered(jnp.concatenate([g_triple, g_extra], axis=1))
    r_norm = r_triple[:, triple_columns : triple_columns + norm_rows].T
    r_bias = r_triple[
        :, triple_columns + norm_rows : triple_columns + norm_rows + bias_rows
    ].reshape(-1)
    r_triple = r_triple[:, :triple_columns].reshape(slab, span, 3, heads_here, head_dim)
    r_triple = r_triple.transpose(0, 1, 3, 2, 4).reshape(slab, triple_columns)
    r_in = jnp.concatenate([r_triple, r_up], axis=1)
    r_unembed = r_unembed[:vocab_local].astype(WIDE).T

    reduced = (r_embed, r_unembed, r_in, r_out, r_norm, r_bias)
    squares = jnp.float32(0.0)
    for grad_piece in reduced:
        squares = squares + jnp.sum(grad_piece * grad_piece)
    loss_term = jnp.where(sp_index == 0, loss_local, 0.0)
    totals = summed_over(jnp.stack([squares, loss_term]), ("sp", "dp"))
    squares_total, loss_total = totals[0], totals[1]
    grad_norm = jnp.sqrt(squares_total)
    mean_loss = loss_total / total_weight
    clip_factor = jnp.minimum(1.0, CLIP_LEVEL / (grad_norm + 1e-06))
    masters = (embed_table, unembed, proj_in, proj_out, norm_params, biases)
    firsts = (embed_first, unembed_first, proj_in_first, proj_out_first, norm_first, bias_first)
    seconds = (
        embed_second,
        unembed_second,
        proj_in_second,
        proj_out_second,
        norm_second,
        bias_second,
    )
    rates = (1.0, 0.05, 0.05, 0.1, 0.5, 0.5)
    decays = (WEIGHT_DECAY, WEIGHT_DECAY, WEIGHT_DECAY, WEIGHT_DECAY, 0.0, 0.0)
    results = []
    for index in range(6):
        results.extend(
            adam_update(
                masters[index],
                firsts[index],
                seconds[index],
                reduced[index],
                clip_factor,
                rates[index],
                decays[index],
            )
        )
    return (
        mean_loss,
        grad_norm,
        results[0],
        results[1],
        results[2],
        results[3],
        results[4],
        results[5],
        results[6],
        results[7],
        results[8],
        results[9],
        results[10],
        results[11],
        results[12],
        results[13],
        results[14],
        results[15],
        results[16],
        results[17],
    )


def solution(mesh):
    in_specs = (
        P("dp", None),
        P("dp", None),
        P(),
        P("sp", "dp"),
        P("sp", "dp"),
        P("sp", "dp"),
        P("dp", "sp"),
        P("dp", "sp"),
        P("dp", "sp"),
        P(("dp", "sp"), None),
        P(("dp", "sp"), None),
        P(("dp", "sp"), None),
        P(("dp", "sp"), None),
        P(("dp", "sp"), None),
        P(("dp", "sp"), None),
        P(None, ("dp", "sp")),
        P(None, ("dp", "sp")),
        P(None, ("dp", "sp")),
        P(("dp", "sp")),
        P(("dp", "sp")),
        P(("dp", "sp")),
    )
    out_specs = (
        P(),
        P(),
        P("sp", "dp"),
        P("sp", "dp"),
        P("sp", "dp"),
        P("dp", "sp"),
        P("dp", "sp"),
        P("dp", "sp"),
        P(("dp", "sp"), None),
        P(("dp", "sp"), None),
        P(("dp", "sp"), None),
        P(("dp", "sp"), None),
        P(("dp", "sp"), None),
        P(("dp", "sp"), None),
        P(None, ("dp", "sp")),
        P(None, ("dp", "sp")),
        P(None, ("dp", "sp")),
        P(("dp", "sp")),
        P(("dp", "sp")),
        P(("dp", "sp")),
    )
    return jax.shard_map(local, mesh=mesh, in_specs=in_specs, out_specs=out_specs, check_vma=False)
```

time: 3110 us -> 1820 us (0.59)
  matrix products: 836 us -> 161 us
  waiting for transfers between devices: 1520 us -> 991 us
  Pallas kernels: 0 us -> 239 us
  other arithmetic: 315 us -> 182 us
  blocking collectives: 198 us -> 82.2 us
  local copies, waits for them, and re-layouts: 166 us -> 108 us
    dot_general x69 -> x10, matrix products: 836 us -> 161 us  [the longest x1 64.5 us: local(): lax.dot_general(slopes, rows_all, (((0,), (0,)), ((), ())), preferred_ele...]
    reduce_scatter x6 -> x5, waiting for transfers between devices: 1030 us -> 475 us  [the longest x1 218 us: local(): lax.psum_scatter(unembed_grad, 'dp', scatter_dimension=1, tiled=True)]
    pallas_call x0 -> x6, Pallas kernels: none -> 239 us  [the longest x1 82.5 us: head_forward(): pl.pallas_call(partial(head_forward_kernel, real), grid=(total // count,)...]
    all_gather x6 -> x5, waiting for transfers between devices: 387 us -> 219 us  [the longest x1 165 us: local(): lax.all_gather(jnp.pad(unembed.T.astype(LOW), ((0, vocab_padded - vocab_l...]
    unnamed x14 -> x12, waiting for transfers between devices: 0.22 us -> 138 us
    reduce_sum x21 -> x9, other arithmetic: 94.7 us -> 6.79 us  [the longest x1 2.56 us: local(): jnp.sum(d_joint.astype(WIDE), axis=0).reshape(span, 3, heads_here, head_dim)]
    all_gather x5 -> x2, blocking collectives: 104 us -> 25.4 us  [the longest x1 15.1 us: local(): ids_all = lax.all_gather(token_ids, 'dp')]
    convert_element_type x19 -> x11, other arithmetic: 87.9 us -> 20.4 us  [the longest x3 6.07 us: scattered(): lax.psum_scatter(gradient, ('dp', 'sp'), scatter_dimension=0, tiled=True)]
  transfers between devices with their start and end apart: 17 -> 16, of which waited for: 14 -> 10; matrix products, arithmetic and copies ran while one was open for 11% -> 11% of each run, Pallas kernels for 0% -> 5%
where the time goes in v1:
time: 1820 us; the launch traced here: 1810 us
  waiting for transfers between devices  991 us (54%)
  Pallas kernels  239 us (13%)
  other arithmetic  182 us (10%)
  matrix products  161 us (9%)
  local copies, waits for them, and re-layouts  108 us (6%)
  blocking collectives  82.2 us (5%)
  between operations  27.3 us (2%)
  starting transfers between devices  21.1 us (1%)
    reduce_scatter x1, waiting for transfers between devices, local(): lax.psum_scatter(unembed_grad, 'dp', scatter_dimension=1, tiled=True)  218 us
    all_gather x1, waiting for transfers between devices, local(): lax.all_gather(jnp.pad(unembed.T.astype(LOW), ((0, vocab_padded - vocab_l...  165 us
    reduce_scatter x2, waiting for transfers between devices, scattered(): lax.psum_scatter(gradient, ('dp', 'sp'), scatter_dimension=0, tiled=True)  149 us
    unnamed x12, waiting for transfers between devices  138 us
    reduce_scatter x1, waiting for transfers between devices, local(): hidden0 = lax.psum_scatter(picked, 'sp', scatter_dimension=0, tiled=True)  101 us
    scatter-add x1, other arithmetic, local(): jnp.zeros(embed_table.shape, WIDE).at[target_ids]  83.6 us
    pallas_call x1, Pallas kernels, head_forward(): pl.pallas_call(partial(head_forward_kernel, real), grid=(total // count,)...  82.5 us
    all_to_all x1, waiting for transfers between devices, local(): lax.all_to_all(d_triple, 'sp', split_axis=0, concat_axis=0, tiled=True)  73.1 us
  transfers between devices with their start and end apart: 16, of which 10 were waited for; matrix products, arithmetic and copies ran while one was open for 11% of the time, Pallas kernels for 5%

profile of v1, /device:TPU:0, one launch (start us, length us, event | category | flops | bytes accessed | tf_op | source)
XLA Modules:
  0.0 1811.5 jit_solution(8872819386262089494)
XLA Ops:
  8.1 15.1 all-gather.4
  27.6 64.8 %gather_fusion = bf16[16384,256]{1,0:T(8,128)(2,1)} fusion(bf16[6288,256]{1,0:T(8,128)(2,1)S(1)} %convert_element_type.118, s32[16384]{0:T(1024)S(1)} %broadcast_clamp_fusion), kind=kCustom, calls=%fused_computation | custom fusion | bytes 16842752 | tf_op jit(solution)/shard_map/gather | solution.py:536
  110.8 101.5 %reduce-scatter.9.cloned.1.call-done = bf16[2048,256]{1,0:T(8,128)(2,1)} async-done(((bf16[16384,256]{1,0:T(8,128)(2,1)}), bf16[2048,256]{1,0:T(8,128)(2,1)}) %reduce-scatter.9.cloned.1.call-update) | async-done | bytes 1048592 | tf_op jit(solution)/shard_map/reduce_scatter | solution.py:539
  219.3 30.0 %all-to-all-done = bf16[4,512,256]{2,1,0:T(8,128)(2,1)S(1)} async-done(((bf16[4,512,256]{2,1,0:T(8,128)(2,1)}), bf16[4,512,256]{2,1,0:T(8,128)(2,1)S(1)}, u32[]{:S(2)}, u32[]{:S(2)}) %all-to-all-start) | async-done | bytes 1048608 | tf_op jit(solution)/shard_map/all_to_all | solution.py:540
  257.2 11.9 project_queries.1
  273.2 56.4 %all-to-all-done.1.query_ref.key_ref.value_ref = bf16[8,3,2,256,128]{4,3,2,1,0:T(8,128)(2,1)S(1)} async-done(((bf16[8,3,2,256,128]{4,3,2,1,0:T(8,128)(2,1)}), bf16[8,3,2,256,128]{4,3,2,1,0:T(8,128)(2,1)S(1)}, u32[]{:S(2)}, u32[]{:S(2)}) %all-to-all-start.1) | async-done | bytes 3145760 | tf_op jit(solution)/shard_map/all_to_all | solution.py:576
  331.3 23.8 %attend_forward.1 = (bf16[8,2,256,128]{3,2,1,0:T(8,128)(2,1)}, f32[2,8,2048]{2,1,0:T(8,128)}) custom-call(bf16[8,3,2,256,128]{4,3,2,1,0:T(8,128)(2,1)} %copy-done, bf16[8,3,2,256,128]{4,3,2,1,0:T(8,128)(2,1)} %copy-done, bf16[8,3,2,256,128]{4,3,2,1,0:T(8,128)(2,1)} %copy-done), custom_call_target="tpu_custom_call" | custom-call | flops 8388608 | bytes 524288 | tf_op jit(solution)/shard_map/attend_forward/pallas_call | solution.py:234
  359.0 27.3 %multiply_convert_fusion = (bf16[512,4096]{1,0:T(8,128)(2,1)}, f32[512,4096]{1,0:T(8,128)}, f32[512,4096]{1,0:T(8,128)}) fusion(f32[4096]{0:T(1024)S(1)} %add.294, bf16[1024,7296]{1,0:T(8,128)(2,1)} %all-gather.12.cloned.1.call-done.table_ref, f32[1024]{0:T(1024)S(1)} %get-tuple-element.168, f32[1024]{0:T(1024)S(1)} %get-tuple-element.169, ...), kind=kOutput, calls=%fused_computation.15 | convolution fusion | flops 4436000768 | bytes 31485952 | tf_op jit(solution)/shard_map/dot_general | solution.py:581
  404.0 164.5 %all-gather.18.cloned.1.call-done.table_ref = bf16[6400,1024]{1,0:T(8,128)(2,1)} async-done(((bf16[6400,256]{1,0:T(8,128)(2,1)}), bf16[6400,1024]{1,0:T(8,128)(2,1)}) %all-gather.18.cloned.1.call-update) | async-done | bytes 13107216 | tf_op jit(solution)/shard_map/all_gather | solution.py:558
  568.5 54.3 %all-gather.16.cloned.1.call-done = bf16[2,2048,1024]{2,1,0:T(8,128)(2,1)} async-done(((bf16[2,256,1024]{2,1,0:T(8,128)(2,1)}), bf16[2,2048,1024]{2,1,0:T(8,128)(2,1)}) %all-gather.16.cloned.1.call-update) | async-done | bytes 8388624 | tf_op jit(solution)/shard_map/all_gather | solution.py:593
  622.8 82.5 %head_forward.1 = (bf16[4096,6400]{1,0:T(8,128)(2,1)}, f32[4096,128]{1,0:T(8,128)}, f32[8,4096]{1,0:T(8,128)}) custom-call(bf16[4096,1024]{1,0:T(8,128)(2,1)} %bitcast.151, bf16[6400,1024]{1,0:T(8,128)(2,1)} %all-gather.18.cloned.1.call-done.table_ref, s32[4096,1]{1,0:T(8,128)} %bitcast.134), custom_call_target="tpu_custom_call" | custom-call | flops 53687091200 | bytes 73924608 | tf_op jit(solution)/shard_map/head_forward/pallas_call | solution.py:80
  718.7 71.5 %head_backward.1 = (bf16[4096,6400]{1,0:T(8,128)(2,1)}, bf16[4096,1024]{1,0:T(8,128)(2,1)}) custom-call(f32[4096,128]{1,0:T(8,128)} %get-tuple-element.38.stats_ref, f32[8,4096]{1,0:T(8,128)} %maximum_maximum_fusion.lines_ref, s32[4096,1]{1,0:T(8,128)} %bitcast.135, bf16[4096,6400]{1,0:T(8,128)(2,1)} %get-tuple-element.40.powers_ref, ...), custom_call_target="tpu_custom_call" | custom-call | flops 53687091200 | bytes 126353408 | tf_op jit(solution)/shard_map/head_backward/pallas_call | solution.py:135
  790.3 64.5 %convolution_convert_fusion = bf16[6400,1024]{1,0:T(8,128)(2,1)} fusion(bf16[4096,6400]{1,0:T(8,128)(2,1)} %get-tuple-element.42, bf16[4096,1024]{1,0:T(8,128)(2,1)} %bitcast.152), kind=kOutput, calls=%fused_computation.4 | convolution fusion | flops 53693644800 | bytes 73924608 | tf_op jit(solution)/shard_map/dot_general | solution.py:618
  866.4 14.4 fusion.86
  918.8 41.0 %attend_backward.1 = bf16[8,3,2,256,128]{4,3,2,1,0:T(8,128)(2,1)} custom-call(bf16[8,3,2,256,128]{4,3,2,1,0:T(8,128)(2,1)} %copy-done, bf16[8,3,2,256,128]{4,3,2,1,0:T(8,128)(2,1)} %copy-done, bf16[8,3,2,256,128]{4,3,2,1,0:T(8,128)(2,1)} %copy-done, bf16[8,2,256,128]{3,2,1,0:T(8,128)(2,1)} %get-tuple-element.37.out_ref, bf16[8,2,256,128]{3,2,1,0:T(8,128)(2,1)} %copy-done.8, ...), custom_call_target="tpu_custom_call" | custom-call | flops 8388608 | bytes 524288 | tf_op jit(solution)/shard_map/attend_backward/pallas_call | solution.py:333
  966.2 73.1 %all-to-all-done.4.triple_ref = bf16[8,3,2,256,128]{4,3,2,1,0:T(8,128)(2,1)} async-done(((bf16[8,3,2,256,128]{4,3,2,1,0:T(8,128)(2,1)}), bf16[8,3,2,256,128]{4,3,2,1,0:T(8,128)(2,1)}, u32[]{:S(2)}, u32[]{:S(2)}) %all-to-all-start.4) | async-done | bytes 3145760 | tf_op jit(solution)/shard_map/all_to_all | solution.py:654
  1079.9 149.1 %reduce-scatter.15.cloned.1.call-done = bf16[160,1024]{1,0:T(8,128)(2,1)} async-done(((bf16[5120,1024]{1,0:T(8,128)(2,1)}), bf16[160,1024]{1,0:T(8,128)(2,1)}) %reduce-scatter.15.cloned.1.call-update) | async-done | bytes 327696 | tf_op jit(solution)/shard_map/reduce_scatter | solution.py:485
  1230.9 217.6 %reduce-scatter.13.cloned.1.call-done = bf16[6400,256]{1,0:T(8,128)(2,1)} async-done(((bf16[6400,1024]{1,0:T(8,128)(2,1)}), bf16[6400,256]{1,0:T(8,128)(2,1)}) %reduce-scatter.13.cloned.1.call-update) | async-done | bytes 3276816 | tf_op jit(solution)/shard_map/reduce_scatter | solution.py:622
  1448.6 34.8 %all_to_all.52 = bf16[512,4,256]{2,0,1:T(8,128)(2,1)} all-to-all(bf16[512,4,256]{2,0,1:T(8,128)(2,1)S(1)} %bitcast.130), channel_id=1, replica_groups=mesh['dp'=4,'sp'=8] {'dp'}, dimensions={1} | all-to-all | bytes 2097152 | tf_op jit(solution)/shard_map/all_to_all | solution.py:671
  1485.9 136.4 %reduce-scatter.19.cloned.1.call-done = bf16[32,3200]{1,0:T(8,128)(2,1)} async-done(((bf16[1024,3200]{1,0:T(8,128)(2,1)}), bf16[32,3200]{1,0:T(8,128)(2,1)}) %reduce-scatter.19.cloned.1.call-update) | async-done | bytes 204816
  1645.3 83.6 %scatter_custom_fusion = f32[6288,256]{1,0:T(8,128)} fusion(s32[16384]{0:T(1024)} %bitcast.144, bf16[16384,256]{1,0:T(8,128)(2,1)} %all-gather.20.cloned.1.call-done, f32[]{:T(128)} %constant.64.clone.1), kind=kCustom, calls=%fused_computation.2 | custom fusion | flops 8388608 | bytes 14828032 | tf_op jit(solution)/shard_map/scatter-add | solution.py:675
  1738.8 11.8 all-reduce.3
  1773.6 13.8 multiply_subtract_fusion
  1787.5 13.8 add_subtract_fusion
  (273 shorter events, 226.8 us)
Async XLA Ops:
  8.0 204.2 %reduce-scatter.9.cloned.1.call-start = ((), (), s32[]{:S(2)}) async-start(), calls=%async_computation.12 | async-start | bytes 9437184 | tf_op jit(solution)/shard_map/reduce_scatter | solution.py:539
  100.5 149.9 %all-gather.12.cloned.1.call-start = ((), (), s32[]{:S(2)}) async-start(), calls=%async_computation.13 | async-start | bytes 15409152 | tf_op jit(solution)/shard_map/all_gather | solution.py:549
  104.0 283.7 %all-gather.14.cloned.1.call-start = ((), (), s32[]{:S(2)}) async-start(), calls=%async_computation.14 | async-start | bytes 10813440 | tf_op jit(solution)/shard_map/all_gather | solution.py:555
  104.8 463.7 %all-gather.18.cloned.1.call-start = ((), (), s32[]{:S(2)}) async-start(), calls=%async_computation.16 | async-start | bytes 16384000 | tf_op jit(solution)/shard_map/all_gather | solution.py:558
  212.2 37.1 %all-to-all-start = ((bf16[4,512,256]{2,1,0:T(8,128)(2,1)}), bf16[4,512,256]{2,1,0:T(8,128)(2,1)S(1)}, u32[]{:S(2)}, u32[]{:S(2)}) async-start(bf16[4,512,256]{2,1,0:T(8,128)(2,1)} %bitcast.138), calls=%async_computation.1 | async-start | bytes 2097152 | tf_op jit(solution)/shard_map/all_to_all | solution.py:540
  250.0 108.9 %copy-start.20 = (f32[512]{0:T(512)}, f32[512]{0:T(512)S(1)}, u32[]{:S(2)}) copy-start(f32[512]{0:T(512)S(1)} %broadcast_multiply_fusion.5) | copy-start | bytes 6148
  250.4 108.5 %copy-start.24 = (f32[512]{0:T(512)}, f32[512]{0:T(512)S(1)}, u32[]{:S(2)}) copy-start(f32[512]{0:T(512)S(1)} %add_rsqrt_fusion.1) | copy-start | bytes 6148
  255.8 103.1 %copy-start.33 = (f32[1024]{0:T(1024)}, f32[1024]{0:T(1024)S(1)}, u32[]{:S(2)}) copy-start(f32[1024]{0:T(1024)S(1)} %get-tuple-element.169) | copy-start | bytes 12292
  255.8 103.1 %copy-start.35 = (f32[1024]{0:T(1024)}, f32[1024]{0:T(1024)S(1)}, u32[]{:S(2)}) copy-start(f32[1024]{0:T(1024)S(1)} %get-tuple-element.168) | copy-start | bytes 12292
  255.8 142.2 %copy-start.16 = (f32[1024]{0:T(1024)}, f32[1024]{0:T(1024)S(1)}, u32[]{:S(2)}) copy-start(f32[1024]{0:T(1024)S(1)} %get-tuple-element.166) | copy-start | bytes 12292
  269.1 60.5 %all-to-all-start.1 = ((bf16[8,3,2,256,128]{4,3,2,1,0:T(8,128)(2,1)}), bf16[8,3,2,256,128]{4,3,2,1,0:T(8,128)(2,1)S(1)}, u32[]{:S(2)}, u32[]{:S(2)}) async-start(bf16[8,3,2,256,128]{4,3,2,1,0:T(8,128)(2,1)} %project_queries.1), calls=%async_computation.2 | async-start | bytes 6291456 | tf_op jit(solution)/shard_map/all_to_all | solution.py:576
  273.2 113.0 %copy-start.28 = (f32[4096]{0:T(1024)}, f32[4096]{0:T(1024)S(1)}, u32[]{:S(2)}) copy-start(f32[4096]{0:T(1024)S(1)} %add.294) | copy-start | bytes 49156
  355.1 31.3 %all-to-all-start.2 = ((bf16[8,2,256,128]{3,2,1,0:T(8,128)(2,1)}), bf16[8,2,256,128]{3,2,1,0:T(8,128)(2,1)S(1)}, u32[]{:S(2)}, u32[]{:S(2)}) async-start(bf16[8,2,256,128]{3,2,1,0:T(8,128)(2,1)} %get-tuple-element.37.out_ref), calls=%async_computation.3 | async-start | bytes 2097152 | tf_op jit(solution)/shard_map/all_to_all | solution.py:578
  358.6 264.2 %all-gather.16.cloned.1.call-start = ((), (), s32[]{:S(2)}) async-start(), calls=%async_computation.15 | async-start | bytes 9437184 | tf_op jit(solution)/shard_map/all_gather | solution.py:593
  400.3 461.4 %reduce-scatter.11.cloned.1.call-start = ((), (), s32[]{:S(2)}) async-start(), calls=%async_computation.17 | async-start | bytes 9437184 | tf_op jit(solution)/shard_map/reduce_scatter | solution.py:614
  894.3 22.9 %all-to-all-start.3 = ((bf16[8,2,256,128]{3,2,1,0:T(8,128)(2,1)}), bf16[8,2,256,128]{3,2,1,0:T(8,128)(2,1)S(1)}, u32[]{:S(2)}, u32[]{:S(2)}) async-start(bf16[8,2,256,128]{3,2,1,0:T(8,128)(2,1)} %bitcast.128), calls=%async_computation.5 | async-start | bytes 2097152 | tf_op jit(solution)/shard_map/all_to_all | solution.py:637
  897.9 180.2 %reduce-scatter.17.cloned.1.call-start = ((), (), s32[]{:S(2)}) async-start(), calls=%async_computation.20 | async-start | bytes 8650752 | tf_op jit(solution)/shard_map/reduce_scatter | solution.py:485
  917.3 311.8 %reduce-scatter.15.cloned.1.call-start = ((), (), s32[]{:S(2)}) async-start(), calls=%async_computation.19 | async-start | bytes 10813440 | tf_op jit(solution)/shard_map/reduce_scatter | solution.py:485
  918.2 530.3 %reduce-scatter.13.cloned.1.call-start = ((), (), s32[]{:S(2)}) async-start(), calls=%async_computation.18 | async-start | bytes 16384000 | tf_op jit(solution)/shard_map/reduce_scatter | solution.py:622
  959.8 79.5 %all-to-all-start.4 = ((bf16[8,3,2,256,128]{4,3,2,1,0:T(8,128)(2,1)}), bf16[8,3,2,256,128]{4,3,2,1,0:T(8,128)(2,1)}, u32[]{:S(2)}, u32[]{:S(2)}) async-start(bf16[8,3,2,256,128]{4,3,2,1,0:T(8,128)(2,1)} %attend_backward.1), calls=%async_computation.6 | async-start | bytes 6291456 | tf_op jit(solution)/shard_map/all_to_all | solution.py:654
  964.3 658.0 %reduce-scatter.19.cloned.1.call-start = ((), (), s32[]{:S(2)}) async-start(), calls=%async_computation.22 | async-start | bytes 6758400
  1075.2 570.1 %all-gather.20.cloned.1.call-start = ((), (), s32[]{:S(2)}) async-start(), calls=%async_computation.21 | async-start | bytes 9437184 | tf_op jit(solution)/shard_map/all_gather | solution.py:672
  1075.3 408.1 %copy-start.45 = (u32[32]{0:T(128)S(1)}, u32[32]{0:T(128)}, u32[]{:S(2)}) copy-start(u32[32]{0:T(128)} %constant.253) | copy-start | bytes 388
  1075.3 408.7 %copy-start.44 = (u32[32]{0:T(128)S(1)}, u32[32]{0:T(128)}, u32[]{:S(2)}) copy-start(u32[32]{0:T(128)} %constant.258) | copy-start | bytes 388
  (44 other events, 867.9 us)
Sparse Core Ops, SparseCore 0:
  100.6 111.5 reduce-scatter.8
  790.4 71.3 reduce-scatter.10
  1483.5 60.6 all-gather.19
Sparse Core Ops, SparseCore 1:
  104.5 113.6 all-gather.11
  221.4 110.1 all-gather.13
  333.6 234.8 all-gather.17
  570.5 52.3 all-gather.15
  917.3 157.5 reduce-scatter.16
  1077.3 151.7 reduce-scatter.14
  1231.3 217.2 reduce-scatter.12
  1450.7 171.5 reduce-scatter.18

commit v2 on v1

--- a/solution.py
+++ b/solution.py
@@ -33,7 +33,25 @@
     return lax.broadcasted_iota(jnp.int32, shape, 1)
 
 
-def head_forward_kernel(real, rows_ref, table_ref, label_ref, powers_ref, stats_ref, lines_ref):
+def fetch_table(parts, table_ref, arrivals):
+    @pl.when(pl.program_id(0) == 0)
+    def _():
+        share = table_ref.shape[1] // len(parts)
+        copies = [
+            pltpu.make_async_copy(
+                parts[k], table_ref.at[:, k * share : (k + 1) * share], arrivals.at[k]
+            )
+            for k in range(len(parts))
+        ]
+        for copy in copies:
+            copy.start()
+        for copy in copies:
+            copy.wait()
+
+
+def head_forward_kernel(teams, real, rows_ref, label_ref, *refs):
+    powers_ref, stats_ref, lines_ref, table_ref, arrivals = refs[teams:]
+    fetch_table(refs[:teams], table_ref, arrivals)
     padded = table_ref.shape[0]
     part = padded // CHUNKS
     rows = rows_ref[...]
@@ -73,18 +91,19 @@
     lines_ref[...] = jnp.transpose(stats)[0:8, :]
 
 
-def head_forward(rows, table, label, real):
+def head_forward(rows, tables, label, real):
     total, width = rows.shape
-    padded = table.shape[0]
+    padded = tables[0].shape[0]
+    teams = len(tables)
     count = min(HEAD_ROWS, total)
     return pl.pallas_call(
-        partial(head_forward_kernel, real),
+        partial(head_forward_kernel, teams, real),
         grid=(total // count,),
         in_specs=[
             pl.BlockSpec((count, width), lambda i: (i, 0)),
-            pl.BlockSpec((padded, width), lambda i: (0, 0), pipeline_mode=pl.Buffered(1)),
             pl.BlockSpec((count, 1), lambda i: (i, 0)),
-        ],
+        ]
+        + [pl.BlockSpec(memory_space=pl.ANY)] * teams,
         out_specs=[
             pl.BlockSpec((count, padded), lambda i: (i, 0)),
             pl.BlockSpec((count, LANES), lambda i: (i, 0)),
@@ -95,6 +114,7 @@
             jax.ShapeDtypeStruct((total, LANES), WIDE),
             jax.ShapeDtypeStruct((8, total), WIDE),
         ],
+        scratch_shapes=[pltpu.VMEM((padded, width), LOW), pltpu.SemaphoreType.DMA((teams,))],
         cost_estimate=pl.CostEstimate(
             flops=2 * total * width * padded,
             bytes_accessed=2 * (total * (width + padded) + width * padded),
@@ -102,10 +122,12 @@
         ),
         compiler_params=pltpu.CompilerParams(vmem_limit_bytes=VMEM_LIMIT),
         name="head_forward",
-    )(rows, table, label)
-
-
-def head_backward_kernel(stats_ref, lines_ref, label_ref, powers_ref, table_ref, slope_ref, grad_ref):
+    )(rows, label, *tables)
+
+
+def head_backward_kernel(teams, stats_ref, lines_ref, label_ref, powers_ref, *refs):
+    slope_ref, grad_ref, table_ref, arrivals = refs[teams:]
+    fetch_table(refs[:teams], table_ref, arrivals)
     padded = table_ref.shape[0]
     part = padded // CHUNKS
     stats = stats_ref[...]
@@ -128,20 +150,21 @@
     grad_ref[...] = total.astype(LOW)
 
 
-def head_backward(stats, lines, label, powers, table):
+def head_backward(stats, lines, label, powers, tables):
     total, padded = powers.shape
-    width = table.shape[1]
+    teams = len(tables)
+    width = teams * tables[0].shape[1]
     count = min(HEAD_ROWS, total)
     return pl.pallas_call(
-        head_backward_kernel,
+        partial(head_backward_kernel, teams),
         grid=(total // count,),
         in_specs=[
             pl.BlockSpec((count, LANES), lambda i: (i, 0)),
             pl.BlockSpec((8, count), lambda i: (0, i)),
             pl.BlockSpec((count, 1), lambda i: (i, 0)),
             pl.BlockSpec((count, padded), lambda i: (i, 0)),
-            pl.BlockSpec((padded, width), lambda i: (0, 0), pipeline_mode=pl.Buffered(1)),
-        ],
+        ]
+        + [pl.BlockSpec(memory_space=pl.ANY)] * teams,
         out_specs=[
             pl.BlockSpec((count, padded), lambda i: (i, 0)),
             pl.BlockSpec((count, width), lambda i: (i, 0)),
@@ -150,6 +173,7 @@
             jax.ShapeDtypeStruct((total, padded), LOW),
             jax.ShapeDtypeStruct((total, width), LOW),
         ],
+        scratch_shapes=[pltpu.VMEM((padded, width), LOW), pltpu.SemaphoreType.DMA((teams,))],
         cost_estimate=pl.CostEstimate(
             flops=2 * total * width * padded,
             bytes_accessed=2 * (total * (width + 2 * padded) + width * padded),
@@ -157,7 +181,7 @@
         ),
         compiler_params=pltpu.CompilerParams(vmem_limit_bytes=VMEM_LIMIT),
         name="head_backward",
-    )(stats, lines, label, powers, table)
+    )(stats, lines, label, powers, *tables)
 
 
 def attend_forward_kernel(heads, scale, query_ref, key_ref, value_ref, out_ref, lse_ref):
@@ -482,7 +506,31 @@
 
 
 def scattered(gradient):
-    return lax.psum_scatter(gradient, ("dp", "sp"), scatter_dimension=0, tiled=True).astype(WIDE)
+    dp, sp = lax.axis_size("dp"), lax.axis_size("sp")
+    rows, columns = gradient.shape
+    gradient = gradient.reshape(dp, sp, rows // (dp * sp), columns).transpose(1, 0, 2, 3)
+    gradient = gradient.reshape(rows, columns)
+    return lax.psum_scatter(gradient, "sp", scatter_dimension=0, tiled=True)
+
+
+def joined_teams(gradient):
+    dp = lax.axis_size("dp")
+    rows, columns = gradient.shape
+    gradient = lax.all_to_all(gradient, "dp", split_axis=0, concat_axis=0, tiled=True)
+    return jnp.sum(gradient.reshape(dp, rows // dp, columns).astype(WIDE), axis=0)
+
+
+def moved(array, axis, step):
+    size = lax.axis_size(axis)
+    return lax.ppermute(array, axis, [(i, (i + step) % size) for i in range(size)])
+
+
+def turned(values, teams, team):
+    share = values.shape[1] // teams
+    blocks = [values[:, b * share : (b + 1) * share] for b in range(teams)]
+    order = [blocks[(teams - 1 - m) % teams] for m in range(2 * teams - 1)]
+    row = jnp.concatenate(order, axis=1)
+    return lax.dynamic_slice_in_dim(row, (teams - 1 - team) * share, teams * share, 1)
 
 
 def local(
@@ -526,6 +574,25 @@
     tokens_here = seq_here * stretch
     offset = sp_index * vocab_local
 
+    bias_rows = biases.shape[0] // slab
+    norm_rows = norm_params.shape[0]
+    shard_triple = proj_in[:, :triple_columns].astype(LOW)
+    shard_triple = shard_triple.reshape(slab, span, heads_here, 3, head_dim).transpose(0, 1, 3, 2, 4)
+    shard_triple = shard_triple.reshape(slab, triple_columns)
+    extras = jnp.concatenate([norm_params.T, biases.reshape(slab, bias_rows)], axis=1).astype(LOW)
+    extras = jnp.pad(extras, ((0, 0), (0, LANES - extras.shape[1])))
+    shard_triple = jnp.concatenate([shard_triple, extras], axis=1)
+    vocab_step = CHUNKS * LANES
+    vocab_padded = -(-vocab_local // vocab_step) * vocab_step
+    own_table = jnp.pad(unembed.T.astype(LOW), ((0, vocab_padded - vocab_local), (0, 0)))
+    token_ids, shard_triple, own_table = lax.optimization_barrier(
+        (token_ids, shard_triple, own_table)
+    )
+    wide_triple = lax.all_gather(shard_triple, ("dp", "sp"), axis=0, tiled=True)
+    half = vocab_padded // 2
+    middle = teams // 2
+    far_first = moved(own_table[:half], "dp", middle)
+
     ids_all = lax.all_gather(token_ids, "dp")
     ids_all = ids_all.reshape(teams, seq_here, span, stretch).transpose(2, 0, 1, 3).reshape(-1)
     local_ids = ids_all - offset
@@ -536,33 +603,23 @@
         embed_table.astype(LOW).at[safe_ids].get(mode="promise_in_bounds"),
         jnp.zeros((), LOW),
     )
+    picked, wide_triple, far_first, own_table = lax.optimization_barrier(
+        (picked, wide_triple, far_first, own_table)
+    )
+    tables = {k: moved(own_table, "dp", k) for k in range(1, middle)}
+    wide_up = lax.all_gather(proj_in[:, triple_columns:].astype(LOW), ("dp", "sp"), axis=0, tiled=True)
+    wide_out = lax.all_gather(proj_out.astype(LOW), ("dp", "sp"), axis=0, tiled=True)
     hidden0 = lax.psum_scatter(picked, "sp", scatter_dimension=0, tiled=True)
-    hidden0 = lax.all_to_all(hidden0, "dp", split_axis=0, concat_axis=1, tiled=True).astype(WIDE)
-
-    bias_rows = biases.shape[0] // slab
-    norm_rows = norm_params.shape[0]
-    shard_triple = proj_in[:, :triple_columns].astype(LOW)
-    shard_triple = shard_triple.reshape(slab, span, heads_here, 3, head_dim).transpose(0, 1, 3, 2, 4)
-    shard_triple = shard_triple.reshape(slab, triple_columns)
-    extras = jnp.concatenate([norm_params.T, biases.reshape(slab, bias_rows)], axis=1).astype(LOW)
-    extras = jnp.pad(extras, ((0, 0), (0, LANES - extras.shape[1])))
-    wide_in = lax.all_gather(
-        jnp.concatenate([shard_triple, proj_in[:, triple_columns:].astype(LOW), extras], axis=1),
-        ("dp", "sp"),
-        axis=0,
-        tiled=True,
-    )
-    wide_out = lax.all_gather(proj_out.astype(LOW), ("dp", "sp"), axis=0, tiled=True)
-    vocab_step = CHUNKS * LANES
-    vocab_padded = -(-vocab_local // vocab_step) * vocab_step
-    head_table = lax.all_gather(
-        jnp.pad(unembed.T.astype(LOW), ((0, vocab_padded - vocab_local), (0, 0))),
-        "dp",
-        axis=1,
-        tiled=True,
-    )
-    norm_vals = wide_in[:, in_columns : in_columns + norm_rows].astype(WIDE).T
-    bias_vals = wide_in[:, in_columns + norm_rows : in_columns + norm_rows + bias_rows]
+    hidden0, tables = lax.optimization_barrier((hidden0, tables))
+    hidden0 = lax.all_to_all(hidden0, "dp", split_axis=0, concat_axis=1, tiled=True)
+    hidden0, later_table = lax.optimization_barrier((hidden0, own_table))
+    hidden0 = hidden0.astype(WIDE)
+    for k in range(middle + 1, teams):
+        tables[k] = moved(later_table, "dp", k)
+    norm_vals = wide_triple[:, triple_columns : triple_columns + norm_rows].astype(WIDE).T
+    bias_vals = wide_triple[
+        :, triple_columns + norm_rows : triple_columns + norm_rows + bias_rows
+    ]
     bias_vals = bias_vals.astype(WIDE).reshape(-1)
     triple_bias = bias_vals[:triple_columns].reshape(span, heads_here, 3, head_dim)
     triple_bias = triple_bias.transpose(0, 2, 1, 3).reshape(1, triple_columns)
@@ -571,16 +628,19 @@
     normed_one = (normal0 * norm_vals[0] + norm_vals[1]).astype(LOW)
     normed_two = (normal0 * norm_vals[2] + norm_vals[3]).astype(LOW)
     positions = sp_index * stretch + jnp.arange(stretch)
-    tables = turn_tables(positions, turn_packs(span, wide), 3, wide, head_dim)
-    packed = project_queries(normed_one, wide_in, triple_bias, tables, span, seq_here, wide)
+    angles = turn_tables(positions, turn_packs(span, wide), 3, wide, head_dim)
+    packed = project_queries(normed_one, wide_triple, triple_bias, angles, span, seq_here, wide)
     triple = lax.all_to_all(packed, "sp", split_axis=0, concat_axis=0, tiled=True)
+    triple, tables, later_table = lax.optimization_barrier((triple, tables, later_table))
+    far_last = moved(later_table[half:], "dp", middle)
     attended_heads, log_totals = attend_forward(triple, heads_here, ATTEND_ROWS, scale)
     attended = lax.all_to_all(attended_heads, "sp", split_axis=0, concat_axis=0, tiled=True)
+    attended, far_last = lax.optimization_barrier((attended, far_last))
+    tables[middle] = jnp.concatenate([far_first, far_last], axis=0)
+    tables = [own_table] + [tables[k] for k in range(1, teams)]
     attended = attended.reshape(span, tokens_here, wide).transpose(1, 0, 2).reshape(tokens_here, width)
     up_values = (
-        jnp.dot(
-            normed_two, wide_in[:, triple_columns:in_columns], preferred_element_type=WIDE
-        )
+        jnp.dot(normed_two, wide_up, preferred_element_type=WIDE)
         + bias_vals[triple_columns:in_columns]
     )
     act_f, pull_gelu = jax.vjp(gelu_exact, up_values)
@@ -590,11 +650,12 @@
     )
     normal1, inverse1 = standardize(hidden1)
     final = (normal1 * norm_vals[4] + norm_vals[5]).astype(LOW)
+    final = turned(final, teams, dp_index)
     rows_all = lax.all_gather(final.reshape(seq_here, stretch, width), "sp", axis=1, tiled=True)
     rows_all = rows_all.reshape(-1, width)
     grand = rows_all.shape[0]
     labels = targets.reshape(-1, 1) - offset
-    powers, stats, lines = head_forward(rows_all, head_table, labels, vocab_local)
+    powers, stats, lines = head_forward(rows_all, tables, labels, vocab_local)
     merged = lax.all_gather(lines[0:3], "sp")
     highest = jnp.max(merged[:, 0], axis=0)
     summed = jnp.sum(merged[:, 1] * jnp.exp(merged[:, 0] - highest), axis=0)
@@ -610,16 +671,24 @@
     guide = jnp.concatenate(
         [log_sum[None], token_scale[None], jnp.zeros((6, grand), WIDE)], axis=0
     )
-    slopes, grad_rows = head_backward(stats, guide, labels, powers, head_table)
+    slopes, grad_rows = head_backward(stats, guide, labels, powers, tables)
     final_grad = lax.psum_scatter(
         grad_rows.reshape(seq_here, length, width), "sp", scatter_dimension=1, tiled=True
     ).astype(WIDE)
     final_grad = final_grad.reshape(tokens_here, width)
-    unembed_grad = lax.dot_general(
-        slopes, rows_all, (((0,), (0,)), ((), ())), preferred_element_type=WIDE
-    ).astype(LOW)
-    final_grad, unembed_grad = lax.optimization_barrier((final_grad, unembed_grad))
-    r_unembed = lax.psum_scatter(unembed_grad, "dp", scatter_dimension=1, tiled=True)
+    share = width // teams
+    unembed_parts = [
+        lax.dot_general(
+            slopes,
+            rows_all[:, k * share : (k + 1) * share],
+            (((0,), (0,)), ((), ())),
+            preferred_element_type=WIDE,
+        ).astype(LOW)
+        for k in range(teams)
+    ]
+    arrived = [moved(unembed_parts[k], "dp", teams - k) for k in range(1, middle)]
+    final_grad, unembed_parts = lax.optimization_barrier((final_grad, unembed_parts))
+    final_grad = turned(final_grad, teams, dp_index)
 
     g_gain_final = jnp.sum(final_grad * normal1, axis=0)
     g_shift_final = jnp.sum(final_grad, axis=0)
@@ -641,34 +710,40 @@
         normed_two, d_up, (((0,), (0,)), ((), ())), preferred_element_type=WIDE
     ).astype(LOW)
     d_normed_two = lax.dot_general(
-        d_up, wide_in[:, triple_columns:in_columns], contract_last, preferred_element_type=WIDE
-    )
-    d_heads, g_out, g_up, d_normed_two = lax.optimization_barrier(
-        (d_heads, g_out, g_up, d_normed_two)
-    )
+        d_up, wide_up, contract_last, preferred_element_type=WIDE
+    )
+    d_heads, g_out, g_up, d_normed_two, arrived, unembed_parts = lax.optimization_barrier(
+        (d_heads, g_out, g_up, d_normed_two, arrived, unembed_parts)
+    )
+    far_first = moved(unembed_parts[middle][:half], "dp", middle)
     r_out = scattered(g_out)
     r_up = scattered(g_up)
     d_triple = attend_backward(
         triple, attended_heads, d_heads, log_totals, heads_here, ATTEND_ROWS, scale
     )
     d_triple = lax.all_to_all(d_triple, "sp", split_axis=0, concat_axis=0, tiled=True)
-    d_joint = unturn(d_triple, tables)
+    d_joint = unturn(d_triple, angles)
     g_triple = lax.dot_general(
         normed_one, d_joint, (((0,), (0,)), ((), ())), preferred_element_type=WIDE
     ).astype(LOW)
     d_normed_one = lax.dot_general(
-        d_joint, wide_in[:, :triple_columns], contract_last, preferred_element_type=WIDE
-    )
+        d_joint, wide_triple[:, :triple_columns], contract_last, preferred_element_type=WIDE
+    )
+    d_normed_one, far_first, unembed_parts = lax.optimization_barrier(
+        (d_normed_one, far_first, unembed_parts)
+    )
+    late = [moved(unembed_parts[k], "dp", teams - k) for k in range(middle + 1, teams)]
     g_gain_one = jnp.sum(d_normed_one * normal0, axis=0)
     g_shift_one = jnp.sum(d_normed_one, axis=0)
     g_gain_two = jnp.sum(d_normed_two * normal0, axis=0)
     g_shift_two = jnp.sum(d_normed_two, axis=0)
     d_sum = d_normed_one * norm_vals[0] + d_normed_two * norm_vals[2]
     d_hidden0 = (d_hidden1 + standardize_pull(d_sum, normal0, inverse0)).astype(LOW)
-    d_hidden0, r_unembed, r_out, r_up = lax.optimization_barrier(
-        (d_hidden0, r_unembed, r_out, r_up)
-    )
+    d_hidden0, r_out, r_up = lax.optimization_barrier((d_hidden0, r_out, r_up))
     grad_all = lax.all_to_all(d_hidden0, "dp", split_axis=1, concat_axis=0, tiled=True)
+    grad_all, late, far_part = lax.optimization_barrier((grad_all, late, unembed_parts[middle]))
+    far_last = moved(far_part[half:], "dp", middle)
+    r_unembed = [unembed_parts[0], *arrived, *late, jnp.concatenate([far_first, far_last], axis=0)]
     grad_all = lax.all_gather(grad_all, "sp", axis=0, tiled=True)
     target_ids = jnp.where(in_slice, local_ids, vocab_local)
     r_embed = (
@@ -689,6 +764,7 @@
     g_extra = jnp.concatenate([g_norm, g_bias.reshape(width, bias_rows)], axis=1).astype(LOW)
     g_extra = jnp.pad(g_extra, ((0, 0), (0, LANES - g_extra.shape[1])))
     r_triple = scattered(jnp.concatenate([g_triple, g_extra], axis=1))
+    r_triple, r_up, r_out = joined_teams(r_triple), joined_teams(r_up), joined_teams(r_out)
     r_norm = r_triple[:, triple_columns : triple_columns + norm_rows].T
     r_bias = r_triple[
         :, triple_columns + norm_rows : triple_columns + norm_rows + bias_rows
@@ -696,7 +772,7 @@
     r_triple = r_triple[:, :triple_columns].reshape(slab, span, 3, heads_here, head_dim)
     r_triple = r_triple.transpose(0, 1, 3, 2, 4).reshape(slab, triple_columns)
     r_in = jnp.concatenate([r_triple, r_up], axis=1)
-    r_unembed = r_unembed[:vocab_local].astype(WIDE).T
+    r_unembed = sum(part[:vocab_local].astype(WIDE) for part in r_unembed).T
 
     reduced = (r_embed, r_unembed, r_in, r_out, r_norm, r_bias)
     squares = jnp.float32(0.0)

time: 1820 us -> 1550 us (0.85)
  waiting for transfers between devices: 991 us -> 540 us
  blocking collectives: 82.2 us -> 177 us
  matrix products: 161 us -> 195 us
  local copies, waits for them, and re-layouts: 108 us -> 135 us
  starting transfers between devices: 21.1 us -> 41.1 us
    reduce_scatter x3, waiting for transfers between devices: 367 us -> 32.2 us  [scattered(): return lax.psum_scatter(gradient, 'sp', scatter_dimension=0, tiled=True)]
    ppermute x0 -> x8, waiting for transfers between devices: none -> 177 us  [moved(): lax.ppermute(array, axis, [(i, (i + step) % size) for i in range(size)])]
    unnamed x12 -> x10, waiting for transfers between devices: 138 us -> 0.17 us
    all_gather x2, waiting for transfers between devices: 165 us -> 45.2 us  [the longest x1 45.1 us: local(): lax.all_gather(proj_in[:, triple_columns:].astype(LOW), ('dp', 'sp'), axi...]
    reduce_scatter x1, waiting for transfers between devices: 101 us -> 0.01 us  [local(): hidden0 = lax.psum_scatter(picked, 'sp', scatter_dimension=0, tiled=True)]
    all_gather x1, blocking collectives: 15.1 us -> 92.1 us  [local(): ids_all = lax.all_gather(token_ids, 'dp')]
    all_to_all x0 -> x2, waiting for transfers between devices: none -> 72.9 us  [the longest x1 51.6 us: joined_teams(): lax.all_to_all(gradient, 'dp', split_axis=0, concat_axis=0, tiled=True)]
    all_gather x1, waiting for transfers between devices: 0.01 us -> 63.9 us  [local(): lax.all_gather(proj_out.astype(LOW), ('dp', 'sp'), axis=0, tiled=True)]
  transfers between devices with their start and end apart: 16 -> 25, of which waited for: 10 -> 16; matrix products, arithmetic and copies ran while one was open for 11% -> 22% of each run, Pallas kernels for 5% -> 6%
where the time goes in v2:
time: 1550 us; the launch traced here: 1540 us
  waiting for transfers between devices  540 us (35%)
  Pallas kernels  242 us (16%)
  matrix products  195 us (13%)
  other arithmetic  186 us (12%)
  blocking collectives  177 us (11%)
  local copies, waits for them, and re-layouts  135 us (9%)
  starting transfers between devices  41.1 us (3%)
  between operations  26.4 us (2%)
    ppermute x8, waiting for transfers between devices, moved(): lax.ppermute(array, axis, [(i, (i + step) % size) for i in range(size)])  177 us
    dot_general x4, matrix products, local(): lax.dot_general(slopes, rows_all[:, k * share:(k + 1) * share], (((0,), (...  101 us
    all_gather x1, blocking collectives, local(): ids_all = lax.all_gather(token_ids, 'dp')  92.1 us
    scatter-add x1, other arithmetic, local(): jnp.zeros(embed_table.shape, WIDE).at[target_ids]  83.6 us
    pallas_call x1, Pallas kernels, head_forward(): pl.pallas_call(partial(head_forward_kernel, teams, real), grid=(total //...  83.2 us
    pallas_call x1, Pallas kernels, head_backward(): pl.pallas_call(partial(head_backward_kernel, teams), grid=(total // count...  73.9 us
    gather x1, local copies, waits for them, and re-layouts, local(): embed_table.astype(LOW).at[safe_ids].get(mode='promise_in_bounds')  64.8 us
    all_gather x1, waiting for transfers between devices, local(): lax.all_gather(proj_out.astype(LOW), ('dp', 'sp'), axis=0, tiled=True)  63.9 us
  transfers between devices with their start and end apart: 25, of which 16 were waited for; matrix products, arithmetic and copies ran while one was open for 22% of the time, Pallas kernels for 6%

profile of v2, /device:TPU:0, one launch (start us, length us, event | category | flops | bytes accessed | tf_op | source)
XLA Modules:
  0.0 1541.7 jit_solution(16866401774207332578)
XLA Ops:
  24.7 92.1 %all-gather.4 = s32[4,2,2048]{2,1,0:T(2,128)S(1)} all-gather(s32[1,2,2048]{2,1,0:T(2,128)S(1)} %bitcast.171), channel_id=2, replica_groups=mesh['dp'=4,'sp'=8] {'dp'}, dimensions={0}, use_global_device_ids=true | all-gather | bytes 81920 | tf_op jit(solution)/shard_map/all_gather | solution.py:596
  121.1 64.8 %gather_fusion = bf16[16384,256]{1,0:T(8,128)(2,1)} fusion(bf16[6288,256]{1,0:T(8,128)(2,1)S(1)} %convert_element_type.127, s32[16384]{0:T(1024)S(1)} %broadcast_clamp_fusion), kind=kCustom, calls=%fused_computation | custom fusion | bytes 16842752 | tf_op jit(solution)/shard_map/gather | solution.py:603
  196.7 73.7 %collective-permute-done.1.refs_1_ = bf16[6400,256]{1,0:T(8,128)(2,1)} collective-permute-done((bf16[6400,256]{1,0:T(8,128)(2,1)}, bf16[6400,256]{1,0:T(8,128)(2,1)}, u32[]{:S(2)}, u32[]{:S(2)}) %collective-permute-start.1) | collective-permute-done | bytes 3276832 | tf_op jit(solution)/shard_map/ppermute | solution.py:525
  323.7 37.5 %all-to-all-done.1.query_ref.key_ref.value_ref = bf16[8,3,2,256,128]{4,3,2,1,0:T(8,128)(2,1)S(1)} async-done(((bf16[8,3,2,256,128]{4,3,2,1,0:T(8,128)(2,1)}), bf16[8,3,2,256,128]{4,3,2,1,0:T(8,128)(2,1)S(1)}, u32[]{:S(2)}, u32[]{:S(2)}) %all-to-all-start.1) | async-done | bytes 3145760 | tf_op jit(solution)/shard_map/all_to_all | solution.py:633
  361.2 26.0 %collective-permute-done.2.refs_3_ = bf16[6400,256]{1,0:T(8,128)(2,1)} collective-permute-done((bf16[6400,256]{1,0:T(8,128)(2,1)}, bf16[6400,256]{1,0:T(8,128)(2,1)}, u32[]{:S(2)}, u32[]{:S(2)}) %collective-permute-start.2) | collective-permute-done | bytes 3276832 | tf_op jit(solution)/shard_map/ppermute | solution.py:525
  417.9 45.1 %all-gather.14.cloned.1.call-done = bf16[1024,4096]{1,0:T(8,128)(2,1)} async-done(((bf16[32,4096]{1,0:T(8,128)(2,1)}), bf16[1024,4096]{1,0:T(8,128)(2,1)}) %all-gather.14.cloned.1.call-update) | async-done | bytes 8388624 | tf_op jit(solution)/shard_map/all_gather | solution.py:610
  463.1 27.9 %multiply_convert_fusion = (bf16[512,4096]{1,0:T(8,128)(2,1)}, f32[512,4096]{1,0:T(8,128)}, f32[512,4096]{1,0:T(8,128)}) fusion(f32[4096]{0:T(1024)S(1)} %add.305, bf16[1024,4096]{1,0:T(8,128)(2,1)} %all-gather.14.cloned.1.call-done, bf16[512,1024]{1,0:T(8,128)(2,1)} %bitcast.134, f32[1024]{0:T(1024)S(1)} %get-tuple-element.168, ...), kind=kOutput, calls=%fused_computation.18 | convolution fusion | flops 4436525056 | bytes 30437376 | tf_op jit(solution)/shard_map/dot_general | solution.py:643
  492.1 63.9 %all-gather.16.cloned.1.call-done = bf16[5120,1024]{1,0:T(8,128)(2,1)} async-done(((bf16[160,1024]{1,0:T(8,128)(2,1)}), bf16[5120,1024]{1,0:T(8,128)(2,1)}) %all-gather.16.cloned.1.call-update) | async-done | bytes 10485776 | tf_op jit(solution)/shard_map/all_gather | solution.py:611
  575.8 46.1 %all-gather.18.cloned.1.call-done = bf16[2,2048,1024]{2,1,0:T(8,128)(2,1)} async-done(((bf16[2,256,1024]{2,1,0:T(8,128)(2,1)}), bf16[2,2048,1024]{2,1,0:T(8,128)(2,1)}) %all-gather.18.cloned.1.call-update) | async-done | bytes 8388624 | tf_op jit(solution)/shard_map/all_gather | solution.py:654
  621.8 83.2 %head_forward.1 = (bf16[4096,6400]{1,0:T(8,128)(2,1)}, f32[4096,128]{1,0:T(8,128)}, f32[8,4096]{1,0:T(8,128)}) custom-call(bf16[4096,1024]{1,0:T(8,128)(2,1)} %bitcast.172, s32[4096,1]{1,0:T(8,128)} %bitcast.153, bf16[6400,256]{1,0:T(8,128)(2,1)} %pad.13.refs_0_, bf16[6400,256]{1,0:T(8,128)(2,1)} %collective-permute-done.1.refs_1_, ...), custom_call_target="tpu_custom_call" | custom-call | flops 53687091200 | bytes 73924608 | tf_op jit(solution)/shard_map/head_forward/pallas_call | solution.py:99
  718.0 73.9 %head_backward.1 = (bf16[4096,6400]{1,0:T(8,128)(2,1)}, bf16[4096,1024]{1,0:T(8,128)(2,1)}) custom-call(f32[4096,128]{1,0:T(8,128)} %get-tuple-element.85.stats_ref, f32[8,4096]{1,0:T(8,128)} %maximum_maximum_fusion.lines_ref, s32[4096,1]{1,0:T(8,128)} %bitcast.154, bf16[4096,6400]{1,0:T(8,128)(2,1)} %get-tuple-element.87.powers_ref, ...), custom_call_target="tpu_custom_call" | custom-call | flops 53687091200 | bytes 126353408 | tf_op jit(solution)/shard_map/head_backward/pallas_call | solution.py:158
  791.9 27.1 %convolution_convert_fusion.3 = bf16[6400,256]{1,0:T(8,128)(2,1)} fusion(bf16[4096,6400]{1,0:T(8,128)(2,1)} %get-tuple-element.89, bf16[4096,1024]{1,0:T(8,128)(2,1)} %bitcast.173), kind=kOutput, calls=%fused_computation.12 | convolution fusion | flops 13423411200 | bytes 57802752 | tf_op jit(solution)/shard_map/dot_general | solution.py:681
  822.4 24.9 %convolution_convert_fusion.1 = bf16[6400,256]{1,0:T(8,128)(2,1)} fusion(bf16[4096,6400]{1,0:T(8,128)(2,1)} %get-tuple-element.89, bf16[4096,1024]{1,0:T(8,128)(2,1)} %bitcast.174), kind=kOutput, calls=%fused_computation.10 | convolution fusion | flops 13423411200 | bytes 57802752 | tf_op jit(solution)/shard_map/dot_general | solution.py:681
  847.3 24.7 %convolution_convert_fusion.2 = bf16[6400,256]{1,0:T(8,128)(2,1)} fusion(bf16[4096,6400]{1,0:T(8,128)(2,1)} %get-tuple-element.89, bf16[4096,1024]{1,0:T(8,128)(2,1)} %bitcast.175), kind=kOutput, calls=%fused_computation.11 | convolution fusion | flops 13423411200 | bytes 57802752 | tf_op jit(solution)/shard_map/dot_general | solution.py:681
  872.1 23.9 %convolution_convert_fusion.4 = bf16[6400,256]{1,0:T(8,128)(2,1)} fusion(bf16[4096,6400]{1,0:T(8,128)(2,1)} %get-tuple-element.89, bf16[4096,1024]{1,0:T(8,128)(2,1)} %bitcast.176), kind=kOutput, calls=%fused_computation.13 | convolution fusion | flops 13423411200 | bytes 57802752 | tf_op jit(solution)/shard_map/dot_general | solution.py:681
  969.3 41.3 %attend_backward.1 = bf16[8,3,2,256,128]{4,3,2,1,0:T(8,128)(2,1)} custom-call(bf16[8,3,2,256,128]{4,3,2,1,0:T(8,128)(2,1)} %copy-done, bf16[8,3,2,256,128]{4,3,2,1,0:T(8,128)(2,1)} %copy-done, bf16[8,3,2,256,128]{4,3,2,1,0:T(8,128)(2,1)} %copy-done, bf16[8,2,256,128]{3,2,1,0:T(8,128)(2,1)} %get-tuple-element.78.out_ref, bf16[8,2,256,128]{3,2,1,0:T(8,128)(2,1)} %copy-done.7, ...), custom_call_target="tpu_custom_call" | custom-call | flops 8388608 | bytes 524288 | tf_op jit(solution)/shard_map/attend_backward/pallas_call | solution.py:357
  1018.3 42.6 %all-to-all-done.4.triple_ref = bf16[8,3,2,256,128]{4,3,2,1,0:T(8,128)(2,1)} async-done(((bf16[8,3,2,256,128]{4,3,2,1,0:T(8,128)(2,1)}), bf16[8,3,2,256,128]{4,3,2,1,0:T(8,128)(2,1)}, u32[]{:S(2)}, u32[]{:S(2)}) %all-to-all-start.4) | async-done | bytes 3145760 | tf_op jit(solution)/shard_map/all_to_all | solution.py:724
  1111.5 29.6 %reduce-scatter.10.cloned.1.call-done = bf16[640,1024]{1,0:T(8,128)(2,1)} async-done(((bf16[5120,1024]{1,0:T(8,128)(2,1)}), bf16[640,1024]{1,0:T(8,128)(2,1)}) %reduce-scatter.10.cloned.1.call-update) | async-done | bytes 1310736 | tf_op jit(solution)/shard_map/reduce_scatter | solution.py:513
  1148.0 34.6 %collective-permute-done.6 = bf16[6400,256]{1,0:T(8,128)(2,1)} collective-permute-done((bf16[6400,256]{1,0:T(8,128)(2,1)}, bf16[6400,256]{1,0:T(8,128)(2,1)}, u32[]{:S(2)}, u32[]{:S(2)}) %collective-permute-start.6) | collective-permute-done | bytes 3276832 | tf_op jit(solution)/shard_map/ppermute | solution.py:525
  1207.6 25.2 %all_to_all.85 = bf16[4,32,3200]{2,1,0:T(8,128)(2,1)S(1)} all-to-all(bf16[4,32,3200]{2,1,0:T(8,128)(2,1)} %bitcast.159), channel_id=1, replica_groups=mesh['dp'=4,'sp'=8] {'dp'}, dimensions={0} | all-to-all | bytes 1638400 | tf_op jit(solution)/shard_map/all_to_all | solution.py:519
  1232.8 27.9 %all_to_all.86 = bf16[4,32,4096]{2,1,0:T(8,128)(2,1)} all-to-all(bf16[4,32,4096]{2,1,0:T(8,128)(2,1)S(1)} %bitcast.157), channel_id=1, replica_groups=mesh['dp'=4,'sp'=8] {'dp'}, dimensions={0} | all-to-all | bytes 2097152 | tf_op jit(solution)/shard_map/all_to_all | solution.py:519
  1279.5 51.6 %all-to-all-done.8 = bf16[4,160,1024]{2,1,0:T(8,128)(2,1)S(1)} async-done(((bf16[4,160,1024]{2,1,0:T(8,128)(2,1)}), bf16[4,160,1024]{2,1,0:T(8,128)(2,1)S(1)}, u32[]{:S(2)}, u32[]{:S(2)}) %all-to-all-start.8) | async-done | bytes 1310752 | tf_op jit(solution)/shard_map/all_to_all | solution.py:519
  1332.1 33.2 %collective-permute-done.7 = bf16[3200,256]{1,0:T(8,128)(2,1)} collective-permute-done((bf16[3200,256]{1,0:T(8,128)(2,1)}, bf16[3200,256]{1,0:T(8,128)(2,1)}, u32[]{:S(2)}, u32[]{:S(2)}) %collective-permute-start.7) | collective-permute-done | bytes 1638432 | tf_op jit(solution)/shard_map/ppermute | solution.py:525
  1373.3 83.6 %scatter_custom_fusion = f32[6288,256]{1,0:T(8,128)} fusion(s32[16384]{0:T(1024)} %bitcast.165, bf16[16384,256]{1,0:T(8,128)(2,1)} %all-gather.20.cloned.1.call-done, f32[]{:T(128)} %constant.66.clone.1), kind=kCustom, calls=%fused_computation.2 | custom fusion | flops 8388608 | bytes 14828032 | tf_op jit(solution)/shard_map/scatter-add | solution.py:750
  (329 shorter events, 410.7 us)
Async XLA Ops:
  7.2 186.8 %all-gather.12.cloned.1.call-start = ((), (), s32[]{:S(2)}) async-start(), calls=%async_computation.14 | async-start | bytes 6758400 | tf_op jit(solution)/shard_map/all_gather | solution.py:591
  17.8 252.6 %reduce-scatter.6.cloned.1.call-start = ((), (), s32[]{:S(2)}) async-start(), calls=%async_computation.15 | async-start | bytes 9437184 | tf_op jit(solution)/shard_map/reduce_scatter | solution.py:612
  20.6 173.4 %collective-permute-start = (bf16[3200,256]{1,0:T(8,128)(2,1)}, bf16[3200,256]{1,0:T(8,128)(2,1)}, u32[]{:S(2)}, u32[]{:S(2)}) collective-permute-start(bf16[3200,256]{1,0:T(8,128)(2,1)} %slice.145), channel_id=1, source_target_pairs={{0,16},{8,24},{16,0},{24,8},{1,17},{9,25},{17,1},{25,9},{2,18},{10... | collective-permute-start | bytes 4915208 | tf_op jit(solution)/shard_map/ppermute | solution.py:525
  194.1 269.0 %all-gather.14.cloned.1.call-start = ((), (), s32[]{:S(2)}) async-start(), calls=%async_computation.16 | async-start | bytes 8650752 | tf_op jit(solution)/shard_map/all_gather | solution.py:610
  195.8 360.2 %all-gather.16.cloned.1.call-start = ((), (), s32[]{:S(2)}) async-start(), calls=%async_computation.17 | async-start | bytes 10813440 | tf_op jit(solution)/shard_map/all_gather | solution.py:611
  196.6 73.8 %collective-permute-start.1 = (bf16[6400,256]{1,0:T(8,128)(2,1)}, bf16[6400,256]{1,0:T(8,128)(2,1)}, u32[]{:S(2)}, u32[]{:S(2)}) collective-permute-start(bf16[6400,256]{1,0:T(8,128)(2,1)} %pad.13.refs_0_), channel_id=1, source_target_pairs={{0,8},{8,16},{16,24},{24,0},{1,9},{9,17},{17,25},{25,1},{2,10},{10... | collective-permute-start | bytes 9830408 | tf_op jit(solution)/shard_map/ppermute | solution.py:525
  270.4 33.2 %all-to-all-start = ((bf16[4,512,256]{2,1,0:T(8,128)(2,1)}), bf16[4,512,256]{2,1,0:T(8,128)(2,1)S(1)}, u32[]{:S(2)}, u32[]{:S(2)}) async-start(bf16[4,512,256]{2,1,0:T(8,128)(2,1)} %bitcast.158), calls=%async_computation.1 | async-start | bytes 2097152 | tf_op jit(solution)/shard_map/all_to_all | solution.py:614
  303.7 83.5 %collective-permute-start.2 = (bf16[6400,256]{1,0:T(8,128)(2,1)}, bf16[6400,256]{1,0:T(8,128)(2,1)}, u32[]{:S(2)}, u32[]{:S(2)}) collective-permute-start(bf16[6400,256]{1,0:T(8,128)(2,1)} %pad.13.refs_0_), channel_id=1, source_target_pairs={{0,24},{8,0},{16,8},{24,16},{1,25},{9,1},{17,9},{25,17},{2,26},{10... | collective-permute-start | bytes 9830408 | tf_op jit(solution)/shard_map/ppermute | solution.py:525
  319.3 41.9 %all-to-all-start.1 = ((bf16[8,3,2,256,128]{4,3,2,1,0:T(8,128)(2,1)}), bf16[8,3,2,256,128]{4,3,2,1,0:T(8,128)(2,1)S(1)}, u32[]{:S(2)}, u32[]{:S(2)}) async-start(bf16[8,3,2,256,128]{4,3,2,1,0:T(8,128)(2,1)} %project_queries.1), calls=%async_computation.2 | async-start | bytes 6291456 | tf_op jit(solution)/shard_map/all_to_all | solution.py:633
  389.9 101.9 %collective-permute-start.3 = (bf16[3200,256]{1,0:T(8,128)(2,1)}, bf16[3200,256]{1,0:T(8,128)(2,1)}, u32[]{:S(2)}, u32[]{:S(2)}) collective-permute-start(bf16[3200,256]{1,0:T(8,128)(2,1)} %slice.151), channel_id=1, source_target_pairs={{0,16},{8,24},{16,0},{24,8},{1,17},{9,25},{17,1},{25,9},{2,18},{10... | collective-permute-start | bytes 4915208 | tf_op jit(solution)/shard_map/ppermute | solution.py:525
  413.7 77.2 %all-to-all-start.2 = ((bf16[8,2,256,128]{3,2,1,0:T(8,128)(2,1)}), bf16[8,2,256,128]{3,2,1,0:T(8,128)(2,1)S(1)}, u32[]{:S(2)}, u32[]{:S(2)}) async-start(bf16[8,2,256,128]{3,2,1,0:T(8,128)(2,1)} %get-tuple-element.78.out_ref), calls=%async_computation.3 | async-start | bytes 2097152 | tf_op jit(solution)/shard_map/all_to_all | solution.py:637
  417.3 204.5 %all-gather.18.cloned.1.call-start = ((), (), s32[]{:S(2)}) async-start(), calls=%async_computation.18 | async-start | bytes 9437184 | tf_op jit(solution)/shard_map/all_gather | solution.py:654
  568.9 327.1 %reduce-scatter.8.cloned.1.call-start = ((), (), s32[]{:S(2)}) async-start(), calls=%async_computation.19 | async-start | bytes 9437184 | tf_op jit(solution)/shard_map/reduce_scatter | solution.py:675
  819.0 130.3 %collective-permute-start.4 = (bf16[6400,256]{1,0:T(8,128)(2,1)}, bf16[6400,256]{1,0:T(8,128)(2,1)}, u32[]{:S(2)}, u32[]{:S(2)}) collective-permute-start(bf16[6400,256]{1,0:T(8,128)(2,1)} %convolution_convert_fusion.3), channel_id=1, source_target_pairs={{0,24},{8,0},{16,8},{24,16},{1,25},{9,1},{17,9},{25,17},{2,26},{10... | collective-permute-start | bytes 9830408 | tf_op jit(solution)/shard_map/ppermute | solution.py:525
  930.1 181.4 %reduce-scatter.12.cloned.1.call-start = ((), (), s32[]{:S(2)}) async-start(), calls=%async_computation.21 | async-start | bytes 9437184 | tf_op jit(solution)/shard_map/reduce_scatter | solution.py:513
  957.5 183.6 %reduce-scatter.10.cloned.1.call-start = ((), (), s32[]{:S(2)}) async-start(), calls=%async_computation.20 | async-start | bytes 11796480 | tf_op jit(solution)/shard_map/reduce_scatter | solution.py:513
  1010.6 50.4 %all-to-all-start.4 = ((bf16[8,3,2,256,128]{4,3,2,1,0:T(8,128)(2,1)}), bf16[8,3,2,256,128]{4,3,2,1,0:T(8,128)(2,1)}, u32[]{:S(2)}, u32[]{:S(2)}) async-start(bf16[8,3,2,256,128]{4,3,2,1,0:T(8,128)(2,1)} %attend_backward.1), calls=%async_computation.6 | async-start | bytes 6291456 | tf_op jit(solution)/shard_map/all_to_all | solution.py:724
  1015.2 192.4 %reduce-scatter.14.cloned.1.call-start = ((), (), s32[]{:S(2)}) async-start(), calls=%async_computation.23 | async-start | bytes 7372800 | tf_op jit(solution)/shard_map/reduce_scatter | solution.py:513
  1017.9 71.8 %collective-permute-start.5 = (bf16[3200,256]{1,0:T(8,128)(2,1)}, bf16[3200,256]{1,0:T(8,128)(2,1)}, u32[]{:S(2)}, u32[]{:S(2)}) collective-permute-start(bf16[3200,256]{1,0:T(8,128)(2,1)} %slice.177), channel_id=1, source_target_pairs={{0,16},{8,24},{16,0},{24,8},{1,17},{9,25},{17,1},{25,9},{2,18},{10... | collective-permute-start | bytes 4915208 | tf_op jit(solution)/shard_map/ppermute | solution.py:525
  1106.6 76.0 %collective-permute-start.6 = (bf16[6400,256]{1,0:T(8,128)(2,1)}, bf16[6400,256]{1,0:T(8,128)(2,1)}, u32[]{:S(2)}, u32[]{:S(2)}) collective-permute-start(bf16[6400,256]{1,0:T(8,128)(2,1)} %convolution_convert_fusion.1), channel_id=1, source_target_pairs={{0,8},{8,16},{16,24},{24,0},{1,9},{9,17},{17,25},{25,1},{2,10},{10... | collective-permute-start | bytes 9830408 | tf_op jit(solution)/shard_map/ppermute | solution.py:525
  1143.3 60.6 %all-to-all-start.5 = ((bf16[512,4,256]{2,0,1:T(8,128)(2,1)}), bf16[512,4,256]{2,0,1:T(8,128)(2,1)S(1)}, u32[]{:S(2)}, u32[]{:S(2)}) async-start(bf16[512,4,256]{2,0,1:T(8,128)(2,1)} %bitcast.123), calls=%async_computation.9 | async-start | bytes 2097152 | tf_op jit(solution)/shard_map/all_to_all | solution.py:743
  1148.0 225.3 %all-gather.20.cloned.1.call-start = ((), (), s32[]{:S(2)}) async-start(), calls=%async_computation.22 | async-start | bytes 9437184 | tf_op jit(solution)/shard_map/all_gather | solution.py:747
  1260.8 70.4 %all-to-all-start.8 = ((bf16[4,160,1024]{2,1,0:T(8,128)(2,1)}), bf16[4,160,1024]{2,1,0:T(8,128)(2,1)S(1)}, u32[]{:S(2)}, u32[]{:S(2)}) async-start(bf16[4,160,1024]{2,1,0:T(8,128)(2,1)} %bitcast.38), calls=%async_computation.13 | async-start | bytes 2621440 | tf_op jit(solution)/shard_map/all_to_all | solution.py:519
  1267.5 97.9 %collective-permute-start.7 = (bf16[3200,256]{1,0:T(8,128)(2,1)}, bf16[3200,256]{1,0:T(8,128)(2,1)}, u32[]{:S(2)}, u32[]{:S(2)}) collective-permute-start(bf16[3200,256]{1,0:T(8,128)(2,1)} %slice.181), channel_id=1, source_target_pairs={{0,16},{8,24},{16,0},{24,8},{1,17},{9,25},{17,1},{25,9},{2,18},{10... | collective-permute-start | bytes 4915208 | tf_op jit(solution)/shard_map/ppermute | solution.py:525
  (59 other events, 2235.1 us)
Sparse Core Ops, SparseCore 0:
  18.0 123.0 all-gather.11
  194.2 70.6 reduce-scatter.5
  268.3 194.7 all-gather.13
  466.3 89.6 all-gather.15
  569.0 52.7 all-gather.17
  792.0 71.3 reduce-scatter.7
  957.6 77.9 reduce-scatter.11
  1039.1 101.8 reduce-scatter.9
  1144.5 63.0 reduce-scatter.13
  1209.9 54.2 all-gather.19

commit v3 on v2

--- a/solution.py
+++ b/solution.py
@@ -505,6 +505,12 @@
     return vector
 
 
+def gathered(shard):
+    rows = lax.all_gather(shard, "dp")
+    rows = lax.all_gather(rows, "sp", axis=1, tiled=True)
+    return rows.reshape(-1, shard.shape[1])
+
+
 def scattered(gradient):
     dp, sp = lax.axis_size("dp"), lax.axis_size("sp")
     rows, columns = gradient.shape
@@ -591,9 +597,9 @@
     wide_triple = lax.all_gather(shard_triple, ("dp", "sp"), axis=0, tiled=True)
     half = vocab_padded // 2
     middle = teams // 2
+    ids_all = lax.all_gather(token_ids, "dp")
+    ids_all, own_table = lax.optimization_barrier((ids_all, own_table))
     far_first = moved(own_table[:half], "dp", middle)
-
-    ids_all = lax.all_gather(token_ids, "dp")
     ids_all = ids_all.reshape(teams, seq_here, span, stretch).transpose(2, 0, 1, 3).reshape(-1)
     local_ids = ids_all - offset
     in_slice = (local_ids >= 0) & (local_ids < vocab_local)
@@ -603,14 +609,17 @@
         embed_table.astype(LOW).at[safe_ids].get(mode="promise_in_bounds"),
         jnp.zeros((), LOW),
     )
+    shard_up, shard_out = proj_in[:, triple_columns:].astype(LOW), proj_out.astype(LOW)
     picked, wide_triple, far_first, own_table = lax.optimization_barrier(
         (picked, wide_triple, far_first, own_table)
     )
     tables = {k: moved(own_table, "dp", k) for k in range(1, middle)}
-    wide_up = lax.all_gather(proj_in[:, triple_columns:].astype(LOW), ("dp", "sp"), axis=0, tiled=True)
-    wide_out = lax.all_gather(proj_out.astype(LOW), ("dp", "sp"), axis=0, tiled=True)
     hidden0 = lax.psum_scatter(picked, "sp", scatter_dimension=0, tiled=True)
-    hidden0, tables = lax.optimization_barrier((hidden0, tables))
+    hidden0, tables, shard_up, shard_out = lax.optimization_barrier(
+        (hidden0, tables, shard_up, shard_out)
+    )
+    wide_up = gathered(shard_up)
+    wide_out = gathered(shard_out)
     hidden0 = lax.all_to_all(hidden0, "dp", split_axis=0, concat_axis=1, tiled=True)
     hidden0, later_table = lax.optimization_barrier((hidden0, own_table))
     hidden0 = hidden0.astype(WIDE)
@@ -677,17 +686,22 @@
     ).astype(WIDE)
     final_grad = final_grad.reshape(tokens_here, width)
     share = width // teams
-    unembed_parts = [
+    inner = rows_all[:, share : (middle + 1) * share]
+    outer = jnp.concatenate([rows_all[:, :share], rows_all[:, (middle + 1) * share :]], axis=1)
+    inner, outer = [
         lax.dot_general(
-            slopes,
-            rows_all[:, k * share : (k + 1) * share],
-            (((0,), (0,)), ((), ())),
-            preferred_element_type=WIDE,
+            slopes, side, (((0,), (0,)), ((), ())), preferred_element_type=WIDE
         ).astype(LOW)
-        for k in range(teams)
+        for side in (inner, outer)
     ]
-    arrived = [moved(unembed_parts[k], "dp", teams - k) for k in range(1, middle)]
-    final_grad, unembed_parts = lax.optimization_barrier((final_grad, unembed_parts))
+    arrived = [
+        moved(inner[:, (k - 1) * share : k * share], "dp", teams - k) for k in range(1, middle)
+    ]
+    far = inner[:, (middle - 1) * share :]
+    quarter = vocab_padded // 4
+    far = [far[q * quarter : (q + 1) * quarter] for q in range(4)]
+    far[0] = moved(far[0], "dp", middle)
+    final_grad, inner, outer = lax.optimization_barrier((final_grad, inner, outer))
     final_grad = turned(final_grad, teams, dp_index)
 
     g_gain_final = jnp.sum(final_grad * normal1, axis=0)
@@ -712,15 +726,17 @@
     d_normed_two = lax.dot_general(
         d_up, wide_up, contract_last, preferred_element_type=WIDE
     )
-    d_heads, g_out, g_up, d_normed_two, arrived, unembed_parts = lax.optimization_barrier(
-        (d_heads, g_out, g_up, d_normed_two, arrived, unembed_parts)
-    )
-    far_first = moved(unembed_parts[middle][:half], "dp", middle)
+    d_heads, g_out, g_up, d_normed_two, arrived, far = lax.optimization_barrier(
+        (d_heads, g_out, g_up, d_normed_two, arrived, far)
+    )
+    far[1] = moved(far[1], "dp", middle)
     r_out = scattered(g_out)
     r_up = scattered(g_up)
     d_triple = attend_backward(
         triple, attended_heads, d_heads, log_totals, heads_here, ATTEND_ROWS, scale
     )
+    d_triple, far = lax.optimization_barrier((d_triple, far))
+    far[2] = moved(far[2], "dp", middle)
     d_triple = lax.all_to_all(d_triple, "sp", split_axis=0, concat_axis=0, tiled=True)
     d_joint = unturn(d_triple, angles)
     g_triple = lax.dot_general(
@@ -729,22 +745,28 @@
     d_normed_one = lax.dot_general(
         d_joint, wide_triple[:, :triple_columns], contract_last, preferred_element_type=WIDE
     )
-    d_normed_one, far_first, unembed_parts = lax.optimization_barrier(
-        (d_normed_one, far_first, unembed_parts)
-    )
-    late = [moved(unembed_parts[k], "dp", teams - k) for k in range(middle + 1, teams)]
+    d_normed_one, far, outer = lax.optimization_barrier((d_normed_one, far, outer))
+    own_part = outer[:, :share]
+    late = [
+        (k, outer[:, (k - middle) * share : (k - middle + 1) * share])
+        for k in range(middle + 1, teams)
+    ]
+    late_first = [moved(part[:half], "dp", teams - k) for k, part in late]
     g_gain_one = jnp.sum(d_normed_one * normal0, axis=0)
     g_shift_one = jnp.sum(d_normed_one, axis=0)
     g_gain_two = jnp.sum(d_normed_two * normal0, axis=0)
     g_shift_two = jnp.sum(d_normed_two, axis=0)
     d_sum = d_normed_one * norm_vals[0] + d_normed_two * norm_vals[2]
     d_hidden0 = (d_hidden1 + standardize_pull(d_sum, normal0, inverse0)).astype(LOW)
-    d_hidden0, r_out, r_up = lax.optimization_barrier((d_hidden0, r_out, r_up))
     grad_all = lax.all_to_all(d_hidden0, "dp", split_axis=1, concat_axis=0, tiled=True)
-    grad_all, late, far_part = lax.optimization_barrier((grad_all, late, unembed_parts[middle]))
-    far_last = moved(far_part[half:], "dp", middle)
-    r_unembed = [unembed_parts[0], *arrived, *late, jnp.concatenate([far_first, far_last], axis=0)]
+    late_rest = [part[half:] for k, part in late]
+    grad_all, r_out, r_up, late_first, late_rest = lax.optimization_barrier(
+        (grad_all, r_out, r_up, late_first, late_rest)
+    )
+    late_rest = [moved(late_rest[j], "dp", teams - late[j][0]) for j in range(len(late))]
     grad_all = lax.all_gather(grad_all, "sp", axis=0, tiled=True)
+    grad_all, late_rest, far = lax.optimization_barrier((grad_all, late_rest, far))
+    far[3] = moved(far[3], "dp", middle)
     target_ids = jnp.where(in_slice, local_ids, vocab_local)
     r_embed = (
         jnp.zeros(embed_table.shape, WIDE).at[target_ids].add(grad_all.astype(WIDE), mode="drop")
@@ -765,6 +787,11 @@
     g_extra = jnp.pad(g_extra, ((0, 0), (0, LANES - g_extra.shape[1])))
     r_triple = scattered(jnp.concatenate([g_triple, g_extra], axis=1))
     r_triple, r_up, r_out = joined_teams(r_triple), joined_teams(r_up), joined_teams(r_out)
+    r_embed, far, late_first, late_rest, arrived, r_out, own_part = lax.optimization_barrier(
+        (r_embed, far, late_first, late_rest, arrived, r_out, own_part)
+    )
+    late = [jnp.concatenate(pair, axis=0) for pair in zip(late_first, late_rest)]
+    r_unembed = [own_part, *arrived, *late, jnp.concatenate(far, axis=0)]
     r_norm = r_triple[:, triple_columns : triple_columns + norm_rows].T
     r_bias = r_triple[
         :, triple_columns + norm_rows : triple_columns + norm_rows + bias_rows

time: 1550 us -> 1460 us (0.942)
  waiting for transfers between devices: 540 us -> 477 us
  matrix products: 195 us -> 162 us
    all_to_all x0 -> x2, blocking collectives: none -> 113 us  [the longest x1 57.6 us: local(): lax.all_to_all(d_hidden0, 'dp', split_axis=1, concat_axis=0, tiled=True)]
    all_gather x1, blocking collectives: 92.1 us -> 14.9 us  [local(): ids_all = lax.all_gather(token_ids, 'dp')]
    ppermute x8 -> x11, waiting for transfers between devices: 177 us -> 118 us  [moved(): lax.ppermute(array, axis, [(i, (i + step) % size) for i in range(size)])]
    all_to_all x2 -> x0, waiting for transfers between devices: 58.8 us -> none  [the longest x1 37.5 us: local(): lax.all_to_all(packed, 'sp', split_axis=0, concat_axis=0, tiled=True)]
    all_gather x2 -> x4, waiting for transfers between devices: 109 us -> 61.8 us  [the longest x2 61.7 us: gathered(): rows = lax.all_gather(shard, 'dp')]
    all_to_all x1 -> x2, waiting for transfers between devices: 51.6 us -> 94.5 us  [joined_teams(): lax.all_to_all(gradient, 'dp', split_axis=0, concat_axis=0, tiled=True)]
    dot_general x4 -> x2, matrix products: 101 us -> 68.1 us  [local(): lax.dot_general(slopes, side, (((0,), (0,)), ((), ())), preferred_element...]
    all_gather x1, waiting for transfers between devices: 0.02 us -> 29.5 us  [local(): wide_triple = lax.all_gather(shard_triple, ('dp', 'sp'), axis=0, tiled=True)]
  transfers between devices with their start and end apart: 25 -> 29, of which waited for: 16 -> 15; matrix products, arithmetic and copies ran while one was open for 22% -> 26% of each run, Pallas kernels for 6% -> 6%
where the time goes in v3:
time: 1460 us; the launch traced here: 1450 us
  waiting for transfers between devices  477 us (33%)
  Pallas kernels  242 us (17%)
  blocking collectives  186 us (13%)
  other arithmetic  184 us (13%)
  matrix products  162 us (11%)
  local copies, waits for them, and re-layouts  131 us (9%)
  starting transfers between devices  41.7 us (3%)
  between operations  26.5 us (2%)
    ppermute x11, waiting for transfers between devices, moved(): lax.ppermute(array, axis, [(i, (i + step) % size) for i in range(size)])  118 us
    all_to_all x2, waiting for transfers between devices, joined_teams(): lax.all_to_all(gradient, 'dp', split_axis=0, concat_axis=0, tiled=True)  94.5 us
    scatter-add x1, other arithmetic, local(): jnp.zeros(embed_table.shape, WIDE).at[target_ids]  83.6 us
    pallas_call x1, Pallas kernels, head_forward(): pl.pallas_call(partial(head_forward_kernel, teams, real), grid=(total //...  83.2 us
    pallas_call x1, Pallas kernels, head_backward(): pl.pallas_call(partial(head_backward_kernel, teams), grid=(total // count...  73.8 us
    dot_general x2, matrix products, local(): lax.dot_general(slopes, side, (((0,), (0,)), ((), ())), preferred_element...  68.1 us
    gather x1, local copies, waits for them, and re-layouts, local(): embed_table.astype(LOW).at[safe_ids].get(mode='promise_in_bounds')  64.8 us
    all_gather x2, waiting for transfers between devices, gathered(): rows = lax.all_gather(shard, 'dp')  61.7 us
  transfers between devices with their start and end apart: 29, of which 15 were waited for; matrix products, arithmetic and copies ran while one was open for 26% of the time, Pallas kernels for 6%

profile of v3, /device:TPU:0, one launch (start us, length us, event | category | flops | bytes accessed | tf_op | source)
XLA Modules:
  0.0 1449.4 jit_solution(7595609695731522573)
XLA Ops:
  41.0 64.8 %gather_fusion = bf16[16384,256]{1,0:T(8,128)(2,1)} fusion(bf16[6288,256]{1,0:T(8,128)(2,1)S(1)} %convert_element_type.121, s32[16384]{0:T(1024)S(1)} %broadcast_clamp_fusion), kind=kCustom, calls=%fused_computation | custom fusion | bytes 16842752 | tf_op jit(solution)/shard_map/gather | solution.py:609
  119.2 29.5 %all-gather.16.cloned.1.call-done.table_ref = bf16[1024,3200]{1,0:T(8,128)(2,1)} async-done(((bf16[32,3200]{1,0:T(8,128)(2,1)}), bf16[1024,3200]{1,0:T(8,128)(2,1)}) %all-gather.16.cloned.1.call-update) | async-done | bytes 6553616 | tf_op jit(solution)/shard_map/all_gather | solution.py:597
  153.9 70.0 %collective-permute-done.1.refs_1_ = bf16[6400,256]{1,0:T(8,128)(2,1)} collective-permute-done((bf16[6400,256]{1,0:T(8,128)(2,1)S(1)}, bf16[6400,256]{1,0:T(8,128)(2,1)}, u32[]{:S(2)}, u32[]{:S(2)}) %collective-permute-start.1) | collective-permute-done | bytes 3276832 | tf_op jit(solution)/shard_map/ppermute | solution.py:531
  224.5 27.9 %all-gather.26.cloned.1.call-done = bf16[128,4096]{1,0:T(8,128)(2,1)} async-done(((bf16[32,4096]{1,0:T(8,128)(2,1)}), bf16[128,4096]{1,0:T(8,128)(2,1)}) %all-gather.26.cloned.1.call-update) | async-done | bytes 1048592 | tf_op jit(solution)/shard_map/all_gather | solution.py:509
  252.4 33.9 %all-gather.28.cloned.1.call-done = bf16[640,1024]{1,0:T(8,128)(2,1)} async-done(((bf16[160,1024]{1,0:T(8,128)(2,1)}), bf16[640,1024]{1,0:T(8,128)(2,1)}) %all-gather.28.cloned.1.call-update) | async-done | bytes 1310736 | tf_op jit(solution)/shard_map/all_gather | solution.py:509
  296.9 18.2 %all-to-all-done = bf16[4,512,256]{2,1,0:T(8,128)(2,1)S(1)} async-done(((bf16[4,512,256]{2,1,0:T(8,128)(2,1)}), bf16[4,512,256]{2,1,0:T(8,128)(2,1)S(1)}, u32[]{:S(2)}, u32[]{:S(2)}) %all-to-all-start) | async-done | bytes 1048608 | tf_op jit(solution)/shard_map/all_to_all | solution.py:623
  330.8 55.7 %all_to_all.85.query_ref.key_ref.value_ref = bf16[8,3,2,256,128]{4,3,2,1,0:T(8,128)(2,1)} all-to-all(bf16[8,3,2,256,128]{4,3,2,1,0:T(8,128)(2,1)} %project_queries.1), channel_id=1, replica_groups=mesh['dp'=4,'sp'=8] {'sp'}, dimensions={0} | all-to-all | bytes 6291456 | tf_op jit(solution)/shard_map/all_to_all | solution.py:642
  390.1 23.8 %attend_forward.1 = (bf16[8,2,256,128]{3,2,1,0:T(8,128)(2,1)}, f32[2,8,2048]{2,1,0:T(8,128)}) custom-call(bf16[8,3,2,256,128]{4,3,2,1,0:T(8,128)(2,1)} %all_to_all.85.query_ref.key_ref.value_ref, bf16[8,3,2,256,128]{4,3,2,1,0:T(8,128)(2,1)} %all_to_all.85.query_ref.key_ref.value_ref, bf16[8,3,2,256,128]{4,3,2,1,0:T(8,128)(2,1)} %all_to_all.85.query_ref.key_ref.value_ref), custom_call_target="tpu_custom_call" | custom-call | flops 8388608 | bytes 524288 | tf_op jit(solution)/shard_map/attend_forward/pallas_call | solution.py:258
  435.1 24.9 %collective-permute-done.3 = bf16[3200,256]{1,0:T(8,128)(2,1)} collective-permute-done((bf16[3200,256]{1,0:T(8,128)(2,1)}, bf16[3200,256]{1,0:T(8,128)(2,1)}, u32[]{:S(2)}, u32[]{:S(2)}) %collective-permute-start.3) | collective-permute-done | bytes 1638432 | tf_op jit(solution)/shard_map/ppermute | solution.py:531
  460.5 27.9 %multiply_convert_fusion = (bf16[512,4096]{1,0:T(8,128)(2,1)}, f32[512,4096]{1,0:T(8,128)}, f32[512,4096]{1,0:T(8,128)}) fusion(f32[4096]{0:T(1024)S(1)} %add.305, bf16[1024,4096]{1,0:T(8,128)(2,1)} %bitcast.186, bf16[512,1024]{1,0:T(8,128)(2,1)S(1)} %bitcast.134, f32[1024]{0:T(1024)S(1)} %get-tuple-element.216, f32[1024]{0:T(1024)S(1)} %get-tuple-element.217, ...), kind=kOutput, calls=%fused_computation.16 | convolution fusion | flops 4436525056 | bytes 30437376 | tf_op jit(solution)/shard_map/dot_general | solution.py:652
  508.4 47.1 %all-gather.22.cloned.1.call-done = bf16[2,2048,1024]{2,1,0:T(8,128)(2,1)} async-done(((bf16[2,256,1024]{2,1,0:T(8,128)(2,1)}), bf16[2,2048,1024]{2,1,0:T(8,128)(2,1)}) %all-gather.22.cloned.1.call-update) | async-done | bytes 8388624 | tf_op jit(solution)/shard_map/all_gather | solution.py:663
  555.5 83.2 %head_forward.1 = (bf16[4096,6400]{1,0:T(8,128)(2,1)}, f32[4096,128]{1,0:T(8,128)}, f32[8,4096]{1,0:T(8,128)}) custom-call(bf16[4096,1024]{1,0:T(8,128)(2,1)} %bitcast.156, s32[4096,1]{1,0:T(8,128)} %bitcast.161, bf16[6400,256]{1,0:T(8,128)(2,1)} %copy-done.4, bf16[6400,256]{1,0:T(8,128)(2,1)} %collective-permute-done.1.refs_1_, ...), custom_call_target="tpu_custom_call" | custom-call | flops 53687091200 | bytes 73924608 | tf_op jit(solution)/shard_map/head_forward/pallas_call | solution.py:99
  651.7 73.8 %head_backward.1 = (bf16[4096,6400]{1,0:T(8,128)(2,1)}, bf16[4096,1024]{1,0:T(8,128)(2,1)}) custom-call(f32[4096,128]{1,0:T(8,128)} %get-tuple-element.113.stats_ref, f32[8,4096]{1,0:T(8,128)} %maximum_maximum_fusion.lines_ref, s32[4096,1]{1,0:T(8,128)} %bitcast.162, bf16[4096,6400]{1,0:T(8,128)(2,1)} %get-tuple-element.115.powers_ref, ...), custom_call_target="tpu_custom_call" | custom-call | flops 53687091200 | bytes 126353408 | tf_op jit(solution)/shard_map/head_backward/pallas_call | solution.py:158
  725.6 34.4 %convolution_convert_fusion.1 = bf16[6400,512]{1,0:T(8,128)(2,1)S(1)} fusion(bf16[4096,6400]{1,0:T(8,128)(2,1)} %get-tuple-element.117, bf16[4096,1024]{1,0:T(8,128)(2,1)} %bitcast.157), kind=kOutput, calls=%fused_computation.8 | convolution fusion | flops 26846822400 | bytes 63176704 | tf_op jit(solution)/shard_map/dot_general | solution.py:692
  767.4 33.7 %convolution_convert_fusion = bf16[6400,512]{1,0:T(8,128)(2,1)} fusion(bf16[4096,6400]{1,0:T(8,128)(2,1)} %get-tuple-element.117, bf16[4096,256]{1,0:T(8,128)(2,1)S(1)} %get-tuple-element.251, bf16[4096,256]{1,0:T(8,128)(2,1)S(1)} %get-tuple-element.250), kind=kOutput, calls=%fused_computation.7 | convolution fusion | flops 26855211008 | bytes 63176704 | tf_op jit(solution)/shard_map/dot_general | solution.py:692
  891.8 41.3 %attend_backward.1 = bf16[8,3,2,256,128]{4,3,2,1,0:T(8,128)(2,1)} custom-call(bf16[8,3,2,256,128]{4,3,2,1,0:T(8,128)(2,1)} %all_to_all.85.query_ref.key_ref.value_ref, bf16[8,3,2,256,128]{4,3,2,1,0:T(8,128)(2,1)} %all_to_all.85.query_ref.key_ref.value_ref, bf16[8,3,2,256,128]{4,3,2,1,0:T(8,128)(2,1)} %all_to_all.85.query_ref.key_ref.value_ref, ...), custom_call_target="tpu_custom_call" | custom-call | flops 8388608 | bytes 524288 | tf_op jit(solution)/shard_map/attend_backward/pallas_call | solution.py:357
  941.1 44.3 %all-to-all-done.4.triple_ref = bf16[8,3,2,256,128]{4,3,2,1,0:T(8,128)(2,1)} async-done(((bf16[8,3,2,256,128]{4,3,2,1,0:T(8,128)(2,1)}), bf16[8,3,2,256,128]{4,3,2,1,0:T(8,128)(2,1)}, u32[]{:S(2)}, u32[]{:S(2)}) %all-to-all-start.4) | async-done | bytes 3145760 | tf_op jit(solution)/shard_map/all_to_all | solution.py:740
  1027.6 57.6 %all_to_all.86 = bf16[512,4,256]{2,0,1:T(8,128)(2,1)} all-to-all(bf16[512,4,256]{2,0,1:T(8,128)(2,1)S(1)} %bitcast.153), channel_id=1, replica_groups=mesh['dp'=4,'sp'=8] {'dp'}, dimensions={1} | all-to-all | bytes 2097152 | tf_op jit(solution)/shard_map/all_to_all | solution.py:761
  1085.2 44.9 %reduce-scatter.14.cloned.1.call-done = bf16[128,3200]{1,0:T(8,128)(2,1)} async-done(((bf16[1024,3200]{1,0:T(8,128)(2,1)}), bf16[128,3200]{1,0:T(8,128)(2,1)}) %reduce-scatter.14.cloned.1.call-update) | async-done | bytes 819216 | tf_op jit(solution)/shard_map/reduce_scatter | solution.py:519
  1130.1 25.2 %all_to_all.87 = bf16[4,32,3200]{2,1,0:T(8,128)(2,1)S(1)} all-to-all(bf16[4,32,3200]{2,1,0:T(8,128)(2,1)} %bitcast.170), channel_id=1, replica_groups=mesh['dp'=4,'sp'=8] {'dp'}, dimensions={0} | all-to-all | bytes 1638400 | tf_op jit(solution)/shard_map/all_to_all | solution.py:525
  1160.8 57.9 %all-to-all-done.8 = bf16[4,32,4096]{2,1,0:T(8,128)(2,1)S(1)} async-done(((bf16[4,32,4096]{2,1,0:T(8,128)(2,1)}), bf16[4,32,4096]{2,1,0:T(8,128)(2,1)S(1)}, u32[]{:S(2)}, u32[]{:S(2)}) %all-to-all-start.8) | async-done | bytes 1048608 | tf_op jit(solution)/shard_map/all_to_all | solution.py:525
  1236.4 36.6 %all-to-all-done.6 = bf16[4,160,1024]{2,1,0:T(8,128)(2,1)S(1)} async-done(((bf16[4,160,1024]{2,1,0:T(8,128)(2,1)}), bf16[4,160,1024]{2,1,0:T(8,128)(2,1)S(1)}, u32[]{:S(2)}, u32[]{:S(2)}) %all-to-all-start.6) | async-done | bytes 1310752 | tf_op jit(solution)/shard_map/all_to_all | solution.py:525
  1273.3 83.6 %scatter_custom_fusion = f32[6288,256]{1,0:T(8,128)} fusion(s32[16384]{0:T(1024)} %bitcast.176, bf16[16384,256]{1,0:T(8,128)(2,1)} %all-gather.24.cloned.1.call-done, f32[]{:T(128)} %constant.66.clone.1), kind=kCustom, calls=%fused_computation.2 | custom fusion | flops 8388608 | bytes 14828032 | tf_op jit(solution)/shard_map/scatter-add | solution.py:772
  1408.6 17.3 %add_subtract_fusion = (f32[6288,256]{1,0:T(8,128)}, f32[6288,256]{1,0:T(8,128)}, f32[6288,256]{1,0:T(8,128)}) fusion(f32[6288,256]{1,0:T(8,128)} %param.24, f32[6288,256]{1,0:T(8,128)} %scatter_custom_fusion, f32[]{:T(128)S(6)} %min.13, f32[6288,256]{1,0:T(8,128)} %param.25, f32[6288,256]{1,0:T(8,128)} %param.26), kind=kLoop, calls=%fused_computation.38 | loop fusion | flops 24145920 | bytes 45072388 | tf_op jit(solution)/shard_map/sub | solution.py:499
  (343 shorter events, 365.2 us)
Async XLA Ops:
  7.2 141.5 %all-gather.16.cloned.1.call-start = ((), (), s32[]{:S(2)}) async-start(), calls=%async_computation.14 | async-start | bytes 6758400 | tf_op jit(solution)/shard_map/all_gather | solution.py:597
  19.7 204.1 %reduce-scatter.6.cloned.1.call-start = ((), (), s32[]{:S(2)}) async-start(), calls=%async_computation.15 | async-start | bytes 9437184 | tf_op jit(solution)/shard_map/reduce_scatter | solution.py:617
  36.0 83.2 %collective-permute-start = (bf16[3200,256]{1,0:T(8,128)(2,1)}, bf16[3200,256]{1,0:T(8,128)(2,1)}, u32[]{:S(2)}, u32[]{:S(2)}) collective-permute-start(bf16[3200,256]{1,0:T(8,128)(2,1)} %slice.168), channel_id=1, source_target_pairs={{0,16},{8,24},{16,0},{24,8},{1,17},{9,25},{17,1},{25,9},{2,18},{10... | collective-permute-start | bytes 4915208 | tf_op jit(solution)/shard_map/ppermute | solution.py:531
  148.8 103.6 %all-gather.26.cloned.1.call-start = ((), (), s32[]{:S(2)}) async-start(), calls=%async_computation.24 | async-start | bytes 1310720 | tf_op jit(solution)/shard_map/all_gather | solution.py:509
  148.8 75.0 %collective-permute-start.1 = (bf16[6400,256]{1,0:T(8,128)(2,1)S(1)}, bf16[6400,256]{1,0:T(8,128)(2,1)}, u32[]{:S(2)}, u32[]{:S(2)}) collective-permute-start(bf16[6400,256]{1,0:T(8,128)(2,1)S(1)} %copy-done.5), channel_id=1, source_target_pairs={{0,8},{8,16},{16,24},{24,0},{1,9},{9,17},{17,25},{25,1},{2,10},{10... | collective-permute-start | bytes 9830408 | tf_op jit(solution)/shard_map/ppermute | solution.py:531
  223.9 62.4 %all-gather.28.cloned.1.call-start = ((), (), s32[]{:S(2)}) async-start(), calls=%async_computation.25 | async-start | bytes 1638400 | tf_op jit(solution)/shard_map/all_gather | solution.py:509
  224.4 236.0 %all-gather.18.cloned.1.call-start = ((), (), s32[]{:S(2)}) async-start(), calls=%async_computation.16 | async-start | bytes 9437184 | tf_op jit(solution)/shard_map/all_gather | solution.py:510
  252.4 236.0 %all-gather.20.cloned.1.call-start = ((), (), s32[]{:S(2)}) async-start(), calls=%async_computation.17 | async-start | bytes 11796480 | tf_op jit(solution)/shard_map/all_gather | solution.py:510
  315.3 72.3 %collective-permute-start.2 = (bf16[6400,256]{1,0:T(8,128)(2,1)}, bf16[6400,256]{1,0:T(8,128)(2,1)}, u32[]{:S(2)}, u32[]{:S(2)}) collective-permute-start(bf16[6400,256]{1,0:T(8,128)(2,1)} %copy-done.4), channel_id=1, source_target_pairs={{0,24},{8,0},{16,8},{24,16},{1,25},{9,1},{17,9},{25,17},{2,26},{10... | collective-permute-start | bytes 9830408 | tf_op jit(solution)/shard_map/ppermute | solution.py:531
  388.8 71.3 %collective-permute-start.3 = (bf16[3200,256]{1,0:T(8,128)(2,1)}, bf16[3200,256]{1,0:T(8,128)(2,1)}, u32[]{:S(2)}, u32[]{:S(2)}) collective-permute-start(bf16[3200,256]{1,0:T(8,128)(2,1)} %slice.175), channel_id=1, source_target_pairs={{0,16},{8,24},{16,0},{24,8},{1,17},{9,25},{17,1},{25,9},{2,18},{10... | collective-permute-start | bytes 4915208 | tf_op jit(solution)/shard_map/ppermute | solution.py:531
  417.5 138.0 %all-gather.22.cloned.1.call-start = ((), (), s32[]{:S(2)}) async-start(), calls=%async_computation.18 | async-start | bytes 9437184 | tf_op jit(solution)/shard_map/all_gather | solution.py:663
  501.3 299.8 %reduce-scatter.8.cloned.1.call-start = ((), (), s32[]{:S(2)}) async-start(), calls=%async_computation.19 | async-start | bytes 9437184 | tf_op jit(solution)/shard_map/reduce_scatter | solution.py:684
  761.9 109.6 %collective-permute-start.4 = (bf16[6400,256]{1,0:T(8,128)(2,1)}, bf16[6400,256]{1,0:T(8,128)(2,1)}, u32[]{:S(2)}, u32[]{:S(2)}) collective-permute-start(bf16[6400,256]{1,0:T(8,128)(2,1)} %slice.241), channel_id=1, source_target_pairs={{0,24},{8,0},{16,8},{24,16},{1,25},{9,1},{17,9},{25,17},{2,26},{10... | collective-permute-start | bytes 9830408 | tf_op jit(solution)/shard_map/ppermute | solution.py:531
  767.1 104.4 %collective-permute-start.5 = (bf16[1600,256]{1,0:T(8,128)(2,1)}, bf16[1600,256]{1,0:T(8,128)(2,1)}, u32[]{:S(2)}, u32[]{:S(2)}) collective-permute-start(bf16[1600,256]{1,0:T(8,128)(2,1)} %get-tuple-element.257), channel_id=1, source_target_pairs={{0,16},{8,24},{16,0},{24,8},{1,17},{9,25},{17,1},{25,9},{2,18},{10... | collective-permute-start | bytes 2457608 | tf_op jit(solution)/shard_map/ppermute | solution.py:531
  835.2 250.0 %reduce-scatter.12.cloned.1.call-start = ((), (), s32[]{:S(2)}) async-start(), calls=%async_computation.21 | async-start | bytes 9437184 | tf_op jit(solution)/shard_map/reduce_scatter | solution.py:519
  879.7 205.5 %reduce-scatter.10.cloned.1.call-start = ((), (), s32[]{:S(2)}) async-start(), calls=%async_computation.20 | async-start | bytes 11796480 | tf_op jit(solution)/shard_map/reduce_scatter | solution.py:519
  937.6 192.4 %reduce-scatter.14.cloned.1.call-start = ((), (), s32[]{:S(2)}) async-start(), calls=%async_computation.23 | async-start | bytes 7372800 | tf_op jit(solution)/shard_map/reduce_scatter | solution.py:519
  938.1 66.5 %collective-permute-start.7 = (bf16[1600,256]{1,0:T(8,128)(2,1)}, bf16[1600,256]{1,0:T(8,128)(2,1)}, u32[]{:S(2)}, u32[]{:S(2)}) collective-permute-start(bf16[1600,256]{1,0:T(8,128)(2,1)} %get-tuple-element.128), channel_id=1, source_target_pairs={{0,16},{8,24},{16,0},{24,8},{1,17},{9,25},{17,1},{25,9},{2,18},{10... | collective-permute-start | bytes 2457608 | tf_op jit(solution)/shard_map/ppermute | solution.py:531
  1021.4 202.3 %all-gather.24.cloned.1.call-start = ((), (), s32[]{:S(2)}) async-start(), calls=%async_computation.22 | async-start | bytes 9437184 | tf_op jit(solution)/shard_map/all_gather | solution.py:767
  1025.0 60.1 %collective-permute-start.8 = (bf16[3200,256]{1,0:T(8,128)(2,1)S(1)}, bf16[3200,256]{1,0:T(8,128)(2,1)}, u32[]{:S(2)}, u32[]{:S(2)}) collective-permute-start(bf16[3200,256]{1,0:T(8,128)(2,1)S(1)} %get-tuple-element.253), channel_id=1, source_target_pairs={{0,8},{8,16},{16,24},{24,0},{1,9},{9,17},{17,25},{25,1},{2,10},{10... | collective-permute-start | bytes 4915208 | tf_op jit(solution)/shard_map/ppermute | solution.py:531
  1155.3 63.4 %all-to-all-start.8 = ((bf16[4,32,4096]{2,1,0:T(8,128)(2,1)}), bf16[4,32,4096]{2,1,0:T(8,128)(2,1)S(1)}, u32[]{:S(2)}, u32[]{:S(2)}) async-start(bf16[4,32,4096]{2,1,0:T(8,128)(2,1)} %bitcast.167), calls=%async_computation.13 | async-start | bytes 2097152 | tf_op jit(solution)/shard_map/all_to_all | solution.py:525
  1158.8 64.8 %collective-permute-start.9 = (bf16[3200,256]{1,0:T(8,128)(2,1)}, bf16[3200,256]{1,0:T(8,128)(2,1)}, u32[]{:S(2)}, u32[]{:S(2)}) collective-permute-start(bf16[3200,256]{1,0:T(8,128)(2,1)} %get-tuple-element.137), channel_id=1, source_target_pairs={{0,8},{8,16},{16,24},{24,0},{1,9},{9,17},{17,25},{25,1},{2,10},{10... | collective-permute-start | bytes 4915208 | tf_op jit(solution)/shard_map/ppermute | solution.py:531
  1219.7 53.3 %all-to-all-start.6 = ((bf16[4,160,1024]{2,1,0:T(8,128)(2,1)}), bf16[4,160,1024]{2,1,0:T(8,128)(2,1)S(1)}, u32[]{:S(2)}, u32[]{:S(2)}) async-start(bf16[4,160,1024]{2,1,0:T(8,128)(2,1)} %bitcast.163), calls=%async_computation.10 | async-start | bytes 2621440 | tf_op jit(solution)/shard_map/all_to_all | solution.py:525
  1223.7 133.2 %collective-permute-start.10 = (bf16[1600,256]{1,0:T(8,128)(2,1)}, bf16[1600,256]{1,0:T(8,128)(2,1)}, u32[]{:S(2)}, u32[]{:S(2)}) collective-permute-start(bf16[1600,256]{1,0:T(8,128)(2,1)} %get-tuple-element.146), channel_id=1, source_target_pairs={{0,16},{8,24},{16,0},{24,8},{1,17},{9,25},{17,1},{25,9},{2,18},{10... | collective-permute-start | bytes 2457608 | tf_op jit(solution)/shard_map/ppermute | solution.py:531
  (63 other events, 2389.4 us)
Sparse Core Ops, SparseCore 0:
  19.9 128.8 all-gather.15
  152.2 69.9 reduce-scatter.5
  224.4 27.9 all-gather.25
  254.4 31.8 all-gather.27
  288.0 54.1 all-gather.17
  344.0 83.3 all-gather.19
  501.5 54.0 all-gather.21
  725.7 71.3 reduce-scatter.7
  879.8 90.9 reduce-scatter.11
  974.2 89.3 reduce-scatter.9
  1067.0 63.0 reduce-scatter.13
  1131.8 54.2 all-gather.23

commit v4 on v3

--- a/solution.py
+++ b/solution.py
@@ -505,10 +505,24 @@
     return vector
 
 
-def gathered(shard):
-    rows = lax.all_gather(shard, "dp")
+def turned_blocks(blocks, team, axis):
+    teams = len(blocks)
+    order = [blocks[(teams - 1 - m) % teams] for m in range(2 * teams - 1)]
+    share = blocks[0].shape[axis]
+    joined = jnp.concatenate(order, axis=axis)
+    return lax.dynamic_slice_in_dim(joined, (teams - 1 - team) * share, teams * share, axis)
+
+
+def team_rows(shard):
+    teams = lax.axis_size("dp")
+    blocks = [shard] + [moved(shard, "dp", k) for k in range(1, teams)]
+    rows = turned_blocks(blocks, lax.axis_index("dp"), 0)
+    return rows.reshape(teams, *shard.shape)
+
+
+def gathered(rows):
     rows = lax.all_gather(rows, "sp", axis=1, tiled=True)
-    return rows.reshape(-1, shard.shape[1])
+    return rows.reshape(-1, rows.shape[-1])
 
 
 def scattered(gradient):
@@ -520,10 +534,7 @@
 
 
 def joined_teams(gradient):
-    dp = lax.axis_size("dp")
-    rows, columns = gradient.shape
-    gradient = lax.all_to_all(gradient, "dp", split_axis=0, concat_axis=0, tiled=True)
-    return jnp.sum(gradient.reshape(dp, rows // dp, columns).astype(WIDE), axis=0)
+    return lax.psum_scatter(gradient, "dp", scatter_dimension=0, tiled=True)
 
 
 def moved(array, axis, step):
@@ -534,9 +545,7 @@
 def turned(values, teams, team):
     share = values.shape[1] // teams
     blocks = [values[:, b * share : (b + 1) * share] for b in range(teams)]
-    order = [blocks[(teams - 1 - m) % teams] for m in range(2 * teams - 1)]
-    row = jnp.concatenate(order, axis=1)
-    return lax.dynamic_slice_in_dim(row, (teams - 1 - team) * share, teams * share, 1)
+    return turned_blocks(blocks, team, 1)
 
 
 def local(
@@ -591,15 +600,18 @@
     vocab_step = CHUNKS * LANES
     vocab_padded = -(-vocab_local // vocab_step) * vocab_step
     own_table = jnp.pad(unembed.T.astype(LOW), ((0, vocab_padded - vocab_local), (0, 0)))
-    token_ids, shard_triple, own_table = lax.optimization_barrier(
-        (token_ids, shard_triple, own_table)
-    )
+    shard_up, shard_out = proj_in[:, triple_columns:].astype(LOW), proj_out.astype(LOW)
+    token_ids, shard_triple = lax.optimization_barrier((token_ids, shard_triple))
     wide_triple = lax.all_gather(shard_triple, ("dp", "sp"), axis=0, tiled=True)
     half = vocab_padded // 2
     middle = teams // 2
     ids_all = lax.all_gather(token_ids, "dp")
-    ids_all, own_table = lax.optimization_barrier((ids_all, own_table))
-    far_first = moved(own_table[:half], "dp", middle)
+    ids_all, own_table, shard_up, shard_out = lax.optimization_barrier(
+        (ids_all, own_table, shard_up, shard_out)
+    )
+    quarter = vocab_padded // 4
+    far_first = moved(own_table[:quarter], "dp", middle)
+    rows_up, rows_out = team_rows(shard_up), team_rows(shard_out)
     ids_all = ids_all.reshape(teams, seq_here, span, stretch).transpose(2, 0, 1, 3).reshape(-1)
     local_ids = ids_all - offset
     in_slice = (local_ids >= 0) & (local_ids < vocab_local)
@@ -609,17 +621,16 @@
         embed_table.astype(LOW).at[safe_ids].get(mode="promise_in_bounds"),
         jnp.zeros((), LOW),
     )
-    shard_up, shard_out = proj_in[:, triple_columns:].astype(LOW), proj_out.astype(LOW)
-    picked, wide_triple, far_first, own_table = lax.optimization_barrier(
-        (picked, wide_triple, far_first, own_table)
+    picked, wide_triple, far_first, own_table, rows_up, rows_out = lax.optimization_barrier(
+        (picked, wide_triple, far_first, own_table, rows_up, rows_out)
     )
     tables = {k: moved(own_table, "dp", k) for k in range(1, middle)}
     hidden0 = lax.psum_scatter(picked, "sp", scatter_dimension=0, tiled=True)
-    hidden0, tables, shard_up, shard_out = lax.optimization_barrier(
-        (hidden0, tables, shard_up, shard_out)
-    )
-    wide_up = gathered(shard_up)
-    wide_out = gathered(shard_out)
+    hidden0, tables, rows_up, rows_out = lax.optimization_barrier(
+        (hidden0, tables, rows_up, rows_out)
+    )
+    wide_up = gathered(rows_up)
+    wide_out = gathered(rows_out)
     hidden0 = lax.all_to_all(hidden0, "dp", split_axis=0, concat_axis=1, tiled=True)
     hidden0, later_table = lax.optimization_barrier((hidden0, own_table))
     hidden0 = hidden0.astype(WIDE)
@@ -641,12 +652,11 @@
     packed = project_queries(normed_one, wide_triple, triple_bias, angles, span, seq_here, wide)
     triple = lax.all_to_all(packed, "sp", split_axis=0, concat_axis=0, tiled=True)
     triple, tables, later_table = lax.optimization_barrier((triple, tables, later_table))
-    far_last = moved(later_table[half:], "dp", middle)
+    far_next = moved(later_table[quarter:half], "dp", middle)
     attended_heads, log_totals = attend_forward(triple, heads_here, ATTEND_ROWS, scale)
     attended = lax.all_to_all(attended_heads, "sp", split_axis=0, concat_axis=0, tiled=True)
-    attended, far_last = lax.optimization_barrier((attended, far_last))
-    tables[middle] = jnp.concatenate([far_first, far_last], axis=0)
-    tables = [own_table] + [tables[k] for k in range(1, teams)]
+    attended, far_next, later_table = lax.optimization_barrier((attended, far_next, later_table))
+    far_last = moved(later_table[half:], "dp", middle)
     attended = attended.reshape(span, tokens_here, wide).transpose(1, 0, 2).reshape(tokens_here, width)
     up_values = (
         jnp.dot(normed_two, wide_up, preferred_element_type=WIDE)
@@ -661,6 +671,9 @@
     final = (normal1 * norm_vals[4] + norm_vals[5]).astype(LOW)
     final = turned(final, teams, dp_index)
     rows_all = lax.all_gather(final.reshape(seq_here, stretch, width), "sp", axis=1, tiled=True)
+    rows_all, far_last = lax.optimization_barrier((rows_all, far_last))
+    tables[middle] = jnp.concatenate([far_first, far_next, far_last], axis=0)
+    tables = [own_table] + [tables[k] for k in range(1, teams)]
     rows_all = rows_all.reshape(-1, width)
     grand = rows_all.shape[0]
     labels = targets.reshape(-1, 1) - offset
@@ -698,7 +711,6 @@
         moved(inner[:, (k - 1) * share : k * share], "dp", teams - k) for k in range(1, middle)
     ]
     far = inner[:, (middle - 1) * share :]
-    quarter = vocab_padded // 4
     far = [far[q * quarter : (q + 1) * quarter] for q in range(4)]
     far[0] = moved(far[0], "dp", middle)
     final_grad, inner, outer = lax.optimization_barrier((final_grad, inner, outer))
@@ -735,8 +747,13 @@
     d_triple = attend_backward(
         triple, attended_heads, d_heads, log_totals, heads_here, ATTEND_ROWS, scale
     )
-    d_triple, far = lax.optimization_barrier((d_triple, far))
+    d_triple, far, outer = lax.optimization_barrier((d_triple, far, outer))
     far[2] = moved(far[2], "dp", middle)
+    late = [
+        (k, outer[:, (k - middle) * share : (k - middle + 1) * share])
+        for k in range(middle + 1, teams)
+    ]
+    late_first = [moved(part[:half], "dp", teams - k) for k, part in late]
     d_triple = lax.all_to_all(d_triple, "sp", split_axis=0, concat_axis=0, tiled=True)
     d_joint = unturn(d_triple, angles)
     g_triple = lax.dot_general(
@@ -745,13 +762,12 @@
     d_normed_one = lax.dot_general(
         d_joint, wide_triple[:, :triple_columns], contract_last, preferred_element_type=WIDE
     )
-    d_normed_one, far, outer = lax.optimization_barrier((d_normed_one, far, outer))
+    late_rest = [part[half:] for k, part in late]
+    d_normed_one, far, outer, late_first, late_rest = lax.optimization_barrier(
+        (d_normed_one, far, outer, late_first, late_rest)
+    )
     own_part = outer[:, :share]
-    late = [
-        (k, outer[:, (k - middle) * share : (k - middle + 1) * share])
-        for k in range(middle + 1, teams)
-    ]
-    late_first = [moved(part[:half], "dp", teams - k) for k, part in late]
+    late_rest = [moved(late_rest[j], "dp", teams - late[j][0]) for j in range(len(late))]
     g_gain_one = jnp.sum(d_normed_one * normal0, axis=0)
     g_shift_one = jnp.sum(d_normed_one, axis=0)
     g_gain_two = jnp.sum(d_normed_two * normal0, axis=0)
@@ -759,19 +775,13 @@
     d_sum = d_normed_one * norm_vals[0] + d_normed_two * norm_vals[2]
     d_hidden0 = (d_hidden1 + standardize_pull(d_sum, normal0, inverse0)).astype(LOW)
     grad_all = lax.all_to_all(d_hidden0, "dp", split_axis=1, concat_axis=0, tiled=True)
-    late_rest = [part[half:] for k, part in late]
-    grad_all, r_out, r_up, late_first, late_rest = lax.optimization_barrier(
-        (grad_all, r_out, r_up, late_first, late_rest)
-    )
-    late_rest = [moved(late_rest[j], "dp", teams - late[j][0]) for j in range(len(late))]
+    grad_all, r_out, r_up = lax.optimization_barrier((grad_all, r_out, r_up))
     grad_all = lax.all_gather(grad_all, "sp", axis=0, tiled=True)
-    grad_all, late_rest, far = lax.optimization_barrier((grad_all, late_rest, far))
+    grad_all, late_rest, far, r_out, r_up = lax.optimization_barrier(
+        (grad_all, late_rest, far, r_out, r_up)
+    )
     far[3] = moved(far[3], "dp", middle)
     target_ids = jnp.where(in_slice, local_ids, vocab_local)
-    r_embed = (
-        jnp.zeros(embed_table.shape, WIDE).at[target_ids].add(grad_all.astype(WIDE), mode="drop")
-    )
-
     g_bias_triple = jnp.sum(d_joint.astype(WIDE), axis=0).reshape(span, 3, heads_here, head_dim)
     g_bias = jnp.concatenate(
         [
@@ -786,10 +796,17 @@
     g_extra = jnp.concatenate([g_norm, g_bias.reshape(width, bias_rows)], axis=1).astype(LOW)
     g_extra = jnp.pad(g_extra, ((0, 0), (0, LANES - g_extra.shape[1])))
     r_triple = scattered(jnp.concatenate([g_triple, g_extra], axis=1))
+    grad_all, r_triple = lax.optimization_barrier((grad_all, r_triple))
+    r_embed = (
+        jnp.zeros(embed_table.shape, WIDE).at[target_ids].add(grad_all.astype(WIDE), mode="drop")
+    )
     r_triple, r_up, r_out = joined_teams(r_triple), joined_teams(r_up), joined_teams(r_out)
-    r_embed, far, late_first, late_rest, arrived, r_out, own_part = lax.optimization_barrier(
-        (r_embed, far, late_first, late_rest, arrived, r_out, own_part)
-    )
+    r_embed, far, late_first, late_rest, arrived, own_part, r_triple, r_up, r_out = (
+        lax.optimization_barrier(
+            (r_embed, far, late_first, late_rest, arrived, own_part, r_triple, r_up, r_out)
+        )
+    )
+    r_triple, r_up, r_out = r_triple.astype(WIDE), r_up.astype(WIDE), r_out.astype(WIDE)
     late = [jnp.concatenate(pair, axis=0) for pair in zip(late_first, late_rest)]
     r_unembed = [own_part, *arrived, *late, jnp.concatenate(far, axis=0)]
     r_norm = r_triple[:, triple_columns : triple_columns + norm_rows].T

time: 1460 us -> 1380 us (0.945)
  waiting for transfers between devices: 477 us -> 421 us
  blocking collectives: 186 us -> 134 us
  local copies, waits for them, and re-layouts: 131 us -> 158 us
    ppermute x11 -> x18, waiting for transfers between devices: 118 us -> 233 us  [moved(): lax.ppermute(array, axis, [(i, (i + step) % size) for i in range(size)])]
    all_to_all x2 -> x0, waiting for transfers between devices: 94.5 us -> none  [joined_teams(): lax.all_to_all(gradient, 'dp', split_axis=0, concat_axis=0, tiled=True)]
    unnamed x12 -> x15, waiting for transfers between devices: 0.71 us -> 64.2 us
    all_gather x2 -> x0, waiting for transfers between devices: 61.7 us -> none  [gathered(): rows = lax.all_gather(shard, 'dp')]
    all_gather x1, waiting for transfers between devices: 0.02 us -> 54.3 us  [local(): grad_all = lax.all_gather(grad_all, 'sp', axis=0, tiled=True)]
    all_gather x1, waiting for transfers between devices: 47.1 us -> 0.01 us  [local(): lax.all_gather(final.reshape(seq_here, stretch, width), 'sp', axis=1, til...]
    reduce_scatter x3 -> x2, waiting for transfers between devices: 44.9 us -> 0.01 us  [scattered(): return lax.psum_scatter(gradient, 'sp', scatter_dimension=0, tiled=True)]
    all_gather x1, waiting for transfers between devices: 29.5 us -> 0.01 us  [local(): wide_triple = lax.all_gather(shard_triple, ('dp', 'sp'), axis=0, tiled=True)]
  transfers between devices with their start and end apart: 29 -> 35, of which waited for: 15 -> 13; matrix products, arithmetic and copies ran while one was open for 26% -> 29% of each run, Pallas kernels for 6% -> 6%
where the time goes in v4:
time: 1380 us; the launch traced here: 1370 us
  waiting for transfers between devices  421 us (31%)
  Pallas kernels  242 us (18%)
  other arithmetic  185 us (13%)
  matrix products  162 us (12%)
  local copies, waits for them, and re-layouts  158 us (11%)
  blocking collectives  134 us (10%)
  starting transfers between devices  38.8 us (3%)
  between operations  26.4 us (2%)
    ppermute x18, waiting for transfers between devices, moved(): lax.ppermute(array, axis, [(i, (i + step) % size) for i in range(size)])  233 us
    scatter-add x1, other arithmetic, local(): jnp.zeros(embed_table.shape, WIDE).at[target_ids]  83.8 us
    pallas_call x1, Pallas kernels, head_forward(): pl.pallas_call(partial(head_forward_kernel, teams, real), grid=(total //...  83.2 us
    pallas_call x1, Pallas kernels, head_backward(): pl.pallas_call(partial(head_backward_kernel, teams), grid=(total // count...  73.9 us
    gather x1, local copies, waits for them, and re-layouts, local(): embed_table.astype(LOW).at[safe_ids].get(mode='promise_in_bounds')  70 us
    dot_general x2, matrix products, local(): lax.dot_general(slopes, side, (((0,), (0,)), ((), ())), preferred_element...  68.5 us
    unnamed x15, waiting for transfers between devices  64.2 us
    all_to_all x1, blocking collectives, local(): lax.all_to_all(packed, 'sp', split_axis=0, concat_axis=0, tiled=True)  56.6 us
  transfers between devices with their start and end apart: 35, of which 13 were waited for; matrix products, arithmetic and copies ran while one was open for 29% of the time, Pallas kernels for 6%

profile of v4, /device:TPU:0, one launch (start us, length us, event | category | flops | bytes accessed | tf_op | source)
XLA Modules:
  0.0 1368.6 jit_solution(16793978107754592231)
XLA Ops:
  12.1 15.1 %all-gather.4 = s32[4,2,2048]{2,1,0:T(2,128)S(1)} all-gather(s32[1,2,2048]{2,1,0:T(2,128)} %bitcast.178), channel_id=2, replica_groups=mesh['dp'=4,'sp'=8] {'dp'}, dimensions={0}, use_global_device_ids=true | all-gather | bytes 81920 | tf_op jit(solution)/shard_map/all_gather | solution.py:608
  48.0 70.0 %gather_fusion = bf16[16384,256]{1,0:T(8,128)(2,1)} fusion(bf16[6288,256]{1,0:T(8,128)(2,1)S(1)} %convert_element_type.122, s32[16384]{0:T(1024)} %broadcast_clamp_fusion), kind=kCustom, calls=%fused_computation | custom fusion | bytes 16842752 | tf_op jit(solution)/shard_map/gather | solution.py:621
  150.0 18.3 %collective-permute-done = bf16[1600,256]{1,0:T(8,128)(2,1)} collective-permute-done((bf16[1600,256]{1,0:T(8,128)(2,1)}, bf16[1600,256]{1,0:T(8,128)(2,1)}, u32[]{:S(2)}, u32[]{:S(2)}) %collective-permute-start) | collective-permute-done | bytes 819232 | tf_op jit(solution)/shard_map/ppermute | solution.py:542
  168.4 74.7 %collective-permute-done.7.refs_1_ = bf16[6400,256]{1,0:T(8,128)(2,1)} collective-permute-done((bf16[6400,256]{1,0:T(8,128)(2,1)S(1)}, bf16[6400,256]{1,0:T(8,128)(2,1)}, u32[]{:S(2)}, u32[]{:S(2)}) %collective-permute-start.7) | collective-permute-done | bytes 3276832 | tf_op jit(solution)/shard_map/ppermute | solution.py:542
  254.3 18.3 %all-to-all-done = bf16[4,512,256]{2,1,0:T(8,128)(2,1)S(1)} async-done(((bf16[4,512,256]{2,1,0:T(8,128)(2,1)}), bf16[4,512,256]{2,1,0:T(8,128)(2,1)S(1)}, u32[]{:S(2)}, u32[]{:S(2)}) %all-to-all-start) | async-done | bytes 1048608 | tf_op jit(solution)/shard_map/all_to_all | solution.py:634
  288.3 56.6 %all_to_all.58.query_ref.key_ref.value_ref = bf16[8,3,2,256,128]{4,3,2,1,0:T(8,128)(2,1)} all-to-all(bf16[8,3,2,256,128]{4,3,2,1,0:T(8,128)(2,1)} %project_queries.1), channel_id=1, replica_groups=mesh['dp'=4,'sp'=8] {'sp'}, dimensions={0} | all-to-all | bytes 6291456 | tf_op jit(solution)/shard_map/all_to_all | solution.py:653
  345.0 23.8 %attend_forward.1 = (bf16[8,2,256,128]{3,2,1,0:T(8,128)(2,1)}, f32[2,8,2048]{2,1,0:T(8,128)}) custom-call(bf16[8,3,2,256,128]{4,3,2,1,0:T(8,128)(2,1)} %all_to_all.58.query_ref.key_ref.value_ref, bf16[8,3,2,256,128]{4,3,2,1,0:T(8,128)(2,1)} %all_to_all.58.query_ref.key_ref.value_ref, bf16[8,3,2,256,128]{4,3,2,1,0:T(8,128)(2,1)} %all_to_all.58.query_ref.key_ref.value_ref), custom_call_target="tpu_custom_call" | custom-call | flops 8388608 | bytes 524288 | tf_op jit(solution)/shard_map/attend_forward/pallas_call | solution.py:258
  375.5 38.9 %collective-permute-done.9 = bf16[1600,256]{1,0:T(8,128)(2,1)} collective-permute-done((bf16[1600,256]{1,0:T(8,128)(2,1)}, bf16[1600,256]{1,0:T(8,128)(2,1)}, u32[]{:S(2)}, u32[]{:S(2)}) %collective-permute-start.9) | collective-permute-done | bytes 819232 | tf_op jit(solution)/shard_map/ppermute | solution.py:542
  414.8 27.9 %multiply_convert_fusion = (bf16[512,4096]{1,0:T(8,128)(2,1)}, f32[512,4096]{1,0:T(8,128)}, f32[512,4096]{1,0:T(8,128)}) fusion(f32[4096]{0:T(1024)S(1)} %add.319, bf16[1024,4096]{1,0:T(8,128)(2,1)} %bitcast.182, bf16[512,1024]{1,0:T(8,128)(2,1)S(1)} %bitcast.132, f32[1024]{0:T(1024)S(1)} %get-tuple-element.282, f32[1024]{0:T(1024)S(1)} %get-tuple-element.283, ...), kind=kOutput, calls=%fused_computation.16 | convolution fusion | flops 4436525056 | bytes 30437376 | tf_op jit(solution)/shard_map/dot_general | solution.py:662
  464.4 65.1 %collective-permute-done.10 = bf16[3200,256]{1,0:T(8,128)(2,1)S(1)} collective-permute-done((bf16[3200,256]{1,0:T(8,128)(2,1)}, bf16[3200,256]{1,0:T(8,128)(2,1)S(1)}, u32[]{:S(2)}, u32[]{:S(2)}) %collective-permute-start.10) | collective-permute-done | bytes 1638432 | tf_op jit(solution)/shard_map/ppermute | solution.py:542
  530.8 83.2 %head_forward.1 = (bf16[4096,6400]{1,0:T(8,128)(2,1)}, f32[4096,128]{1,0:T(8,128)}, f32[8,4096]{1,0:T(8,128)}) custom-call(bf16[4096,1024]{1,0:T(8,128)(2,1)} %bitcast.157, s32[4096,1]{1,0:T(8,128)} %bitcast.162, bf16[6400,256]{1,0:T(8,128)(2,1)} %pad.13.refs_0_, bf16[6400,256]{1,0:T(8,128)(2,1)} %collective-permute-done.7.refs_1_, ...), custom_call_target="tpu_custom_call" | custom-call | flops 53687091200 | bytes 73924608 | tf_op jit(solution)/shard_map/head_forward/pallas_call | solution.py:99
  627.1 73.9 %head_backward.1 = (bf16[4096,6400]{1,0:T(8,128)(2,1)}, bf16[4096,1024]{1,0:T(8,128)(2,1)}) custom-call(f32[4096,128]{1,0:T(8,128)} %get-tuple-element.132.stats_ref, f32[8,4096]{1,0:T(8,128)} %maximum_maximum_fusion.lines_ref, s32[4096,1]{1,0:T(8,128)} %bitcast.163, bf16[4096,6400]{1,0:T(8,128)(2,1)} %get-tuple-element.134.powers_ref, ...), custom_call_target="tpu_custom_call" | custom-call | flops 53687091200 | bytes 126353408 | tf_op jit(solution)/shard_map/head_backward/pallas_call | solution.py:158
  701.0 34.6 %convolution_convert_fusion.1 = bf16[6400,512]{1,0:T(8,128)(2,1)S(1)} fusion(bf16[4096,6400]{1,0:T(8,128)(2,1)} %get-tuple-element.136, bf16[4096,1024]{1,0:T(8,128)(2,1)} %bitcast.158), kind=kOutput, calls=%fused_computation.8 | convolution fusion | flops 26846822400 | bytes 63176704 | tf_op jit(solution)/shard_map/dot_general | solution.py:705
  742.0 33.9 %convolution_convert_fusion = bf16[6400,512]{1,0:T(8,128)(2,1)} fusion(bf16[4096,6400]{1,0:T(8,128)(2,1)} %get-tuple-element.136, bf16[4096,256]{1,0:T(8,128)(2,1)S(1)} %get-tuple-element.317, bf16[4096,256]{1,0:T(8,128)(2,1)S(1)} %get-tuple-element.316), kind=kOutput, calls=%fused_computation.7 | convolution fusion | flops 26855211008 | bytes 63176704 | tf_op jit(solution)/shard_map/dot_general | solution.py:705
  781.0 13.5 fusion.116
  829.0 16.2 %collective-permute-done.12 = bf16[1600,256]{1,0:T(8,128)(2,1)} collective-permute-done((bf16[1600,256]{1,0:T(8,128)(2,1)}, bf16[1600,256]{1,0:T(8,128)(2,1)}, u32[]{:S(2)}, u32[]{:S(2)}) %collective-permute-start.12) | collective-permute-done | bytes 819232 | tf_op jit(solution)/shard_map/ppermute | solution.py:542
  866.0 41.5 %attend_backward.1 = bf16[8,3,2,256,128]{4,3,2,1,0:T(8,128)(2,1)} custom-call(bf16[8,3,2,256,128]{4,3,2,1,0:T(8,128)(2,1)} %all_to_all.58.query_ref.key_ref.value_ref, bf16[8,3,2,256,128]{4,3,2,1,0:T(8,128)(2,1)} %all_to_all.58.query_ref.key_ref.value_ref, bf16[8,3,2,256,128]{4,3,2,1,0:T(8,128)(2,1)} %all_to_all.58.query_ref.key_ref.value_ref, ...), custom_call_target="tpu_custom_call" | custom-call | flops 8388608 | bytes 524288 | tf_op jit(solution)/shard_map/attend_backward/pallas_call | solution.py:357
  921.2 38.8 %all-to-all-done.4.triple_ref = bf16[8,3,2,256,128]{4,3,2,1,0:T(8,128)(2,1)} async-done(((bf16[8,3,2,256,128]{4,3,2,1,0:T(8,128)(2,1)}), bf16[8,3,2,256,128]{4,3,2,1,0:T(8,128)(2,1)}, u32[]{:S(2)}, u32[]{:S(2)}) %all-to-all-start.4) | async-done | bytes 3145760 | tf_op jit(solution)/shard_map/all_to_all | solution.py:757
  1012.5 29.7 %all_to_all.59 = bf16[512,4,256]{2,0,1:T(8,128)(2,1)} all-to-all(bf16[512,4,256]{2,0,1:T(8,128)(2,1)S(1)} %bitcast.153), channel_id=1, replica_groups=mesh['dp'=4,'sp'=8] {'dp'}, dimensions={1} | all-to-all | bytes 2097152 | tf_op jit(solution)/shard_map/all_to_all | solution.py:777
  1042.5 62.3 %reduce-scatter.25.cloned.1.call-done = bf16[128,3200]{1,0:T(8,128)(2,1)} async-done(((bf16[1024,3200]{1,0:T(8,128)(2,1)}), bf16[128,3200]{1,0:T(8,128)(2,1)}) %reduce-scatter.25.cloned.1.call-update) | async-done | bytes 819216
  1106.5 54.3 %all-gather.20.cloned.1.call-done = bf16[16384,256]{1,0:T(8,128)(2,1)} async-done(((bf16[2048,256]{1,0:T(8,128)(2,1)}), bf16[16384,256]{1,0:T(8,128)(2,1)}) %all-gather.20.cloned.1.call-update) | async-done | bytes 8388624 | tf_op jit(solution)/shard_map/all_gather | solution.py:779
  1168.6 83.8 %scatter_custom_fusion = f32[6288,256]{1,0:T(8,128)} fusion(s32[16384]{0:T(1024)} %bitcast.172, bf16[16384,256]{1,0:T(8,128)(2,1)} %all-gather.20.cloned.1.call-done, f32[]{:T(128)} %constant.70.clone.1), kind=kCustom, calls=%fused_computation.2 | custom fusion | flops 8388608 | bytes 14828032 | tf_op jit(solution)/shard_map/scatter-add | solution.py:801
  1328.0 17.3 %add_subtract_fusion = (f32[6288,256]{1,0:T(8,128)}, f32[6288,256]{1,0:T(8,128)}, f32[6288,256]{1,0:T(8,128)}) fusion(f32[6288,256]{1,0:T(8,128)} %param.24, f32[6288,256]{1,0:T(8,128)} %scatter_custom_fusion, f32[]{:T(128)S(6)} %min.13, f32[6288,256]{1,0:T(8,128)} %param.25, f32[6288,256]{1,0:T(8,128)} %param.26), kind=kLoop, calls=%fused_computation.38 | loop fusion | flops 24145920 | bytes 45072388 | tf_op jit(solution)/shard_map/sub | solution.py:499
  1345.9 13.6 multiply_subtract_fusion
  (377 shorter events, 336.9 us)
Async XLA Ops:
  7.2 161.1 %all-gather.12.cloned.1.call-start = ((), (), s32[]{:S(2)}) async-start(), calls=%async_computation.14 | async-start | bytes 6758400 | tf_op jit(solution)/shard_map/all_gather | solution.py:605
  33.0 108.8 %collective-permute-start.4 = (bf16[160,1024]{1,0:T(8,128)(2,1)}, bf16[160,1024]{1,0:T(8,128)(2,1)}, u32[]{:S(2)}, u32[]{:S(2)}) collective-permute-start(bf16[160,1024]{1,0:T(8,128)(2,1)} %convert_element_type.121), channel_id=1, source_target_pairs={{0,24},{8,0},{16,8},{24,16},{1,25},{9,1},{17,9},{25,17},{2,26},{10... | collective-permute-start | bytes 983048 | tf_op jit(solution)/shard_map/ppermute | solution.py:542
  36.5 106.3 %collective-permute-start.5 = (bf16[160,1024]{1,0:T(8,128)(2,1)}, bf16[160,1024]{1,0:T(8,128)(2,1)}, u32[]{:S(2)}, u32[]{:S(2)}) collective-permute-start(bf16[160,1024]{1,0:T(8,128)(2,1)} %convert_element_type.121), channel_id=1, source_target_pairs={{0,16},{8,24},{16,0},{24,8},{1,17},{9,25},{17,1},{25,9},{2,18},{10... | collective-permute-start | bytes 983048 | tf_op jit(solution)/shard_map/ppermute | solution.py:542
  36.5 107.3 %collective-permute-start.6 = (bf16[160,1024]{1,0:T(8,128)(2,1)}, bf16[160,1024]{1,0:T(8,128)(2,1)}, u32[]{:S(2)}, u32[]{:S(2)}) collective-permute-start(bf16[160,1024]{1,0:T(8,128)(2,1)} %convert_element_type.121), channel_id=1, source_target_pairs={{0,8},{8,16},{16,24},{24,0},{1,9},{9,17},{17,25},{25,1},{2,10},{10... | collective-permute-start | bytes 983048 | tf_op jit(solution)/shard_map/ppermute | solution.py:542
  37.1 90.6 %collective-permute-start.1 = (bf16[32,4096]{1,0:T(8,128)(2,1)S(1)}, bf16[32,4096]{1,0:T(8,128)(2,1)}, u32[]{:S(2)}, u32[]{:S(2)}) collective-permute-start(bf16[32,4096]{1,0:T(8,128)(2,1)S(1)} %slice.224), channel_id=1, source_target_pairs={{0,24},{8,0},{16,8},{24,16},{1,25},{9,1},{17,9},{25,17},{2,26},{10... | collective-permute-start | bytes 786440 | tf_op jit(solution)/shard_map/ppermute | solution.py:542
  40.3 88.3 %collective-permute-start.2 = (bf16[32,4096]{1,0:T(8,128)(2,1)S(1)}, bf16[32,4096]{1,0:T(8,128)(2,1)}, u32[]{:S(2)}, u32[]{:S(2)}) collective-permute-start(bf16[32,4096]{1,0:T(8,128)(2,1)S(1)} %slice.224), channel_id=1, source_target_pairs={{0,16},{8,24},{16,0},{24,8},{1,17},{9,25},{17,1},{25,9},{2,18},{10... | collective-permute-start | bytes 786440 | tf_op jit(solution)/shard_map/ppermute | solution.py:542
  41.5 201.7 %reduce-scatter.13.cloned.1.call-start = ((), (), s32[]{:S(2)}) async-start(), calls=%async_computation.15 | async-start | bytes 9437184 | tf_op jit(solution)/shard_map/reduce_scatter | solution.py:628
  168.3 246.4 %all-gather.14.cloned.1.call-start = ((), (), s32[]{:S(2)}) async-start(), calls=%async_computation.16 | async-start | bytes 9437184 | tf_op jit(solution)/shard_map/all_gather | solution.py:524
  168.4 74.8 %collective-permute-start.7 = (bf16[6400,256]{1,0:T(8,128)(2,1)S(1)}, bf16[6400,256]{1,0:T(8,128)(2,1)}, u32[]{:S(2)}, u32[]{:S(2)}) collective-permute-start(bf16[6400,256]{1,0:T(8,128)(2,1)S(1)} %copy-done.4), channel_id=1, source_target_pairs={{0,8},{8,16},{16,24},{24,0},{1,9},{9,17},{17,25},{25,1},{2,10},{10... | collective-permute-start | bytes 9830408 | tf_op jit(solution)/shard_map/ppermute | solution.py:542
  243.2 199.5 %all-gather.16.cloned.1.call-start = ((), (), s32[]{:S(2)}) async-start(), calls=%async_computation.17 | async-start | bytes 11796480 | tf_op jit(solution)/shard_map/all_gather | solution.py:524
  372.6 156.9 %all-gather.18.cloned.1.call-start = ((), (), s32[]{:S(2)}) async-start(), calls=%async_computation.18 | async-start | bytes 9437184 | tf_op jit(solution)/shard_map/all_gather | solution.py:673
  454.8 321.1 %reduce-scatter.15.cloned.1.call-start = ((), (), s32[]{:S(2)}) async-start(), calls=%async_computation.19 | async-start | bytes 9437184 | tf_op jit(solution)/shard_map/reduce_scatter | solution.py:697
  456.7 72.7 %collective-permute-start.10 = (bf16[3200,256]{1,0:T(8,128)(2,1)}, bf16[3200,256]{1,0:T(8,128)(2,1)S(1)}, u32[]{:S(2)}, u32[]{:S(2)}) collective-permute-start(bf16[3200,256]{1,0:T(8,128)(2,1)} %slice.189), channel_id=1, source_target_pairs={{0,16},{8,24},{16,0},{24,8},{1,17},{9,25},{17,1},{25,9},{2,18},{10... | collective-permute-start | bytes 4915208 | tf_op jit(solution)/shard_map/ppermute | solution.py:542
  737.5 107.7 %collective-permute-start.11 = (bf16[6400,256]{1,0:T(8,128)(2,1)}, bf16[6400,256]{1,0:T(8,128)(2,1)}, u32[]{:S(2)}, u32[]{:S(2)}) collective-permute-start(bf16[6400,256]{1,0:T(8,128)(2,1)} %slice.245), channel_id=1, source_target_pairs={{0,24},{8,0},{16,8},{24,16},{1,25},{9,1},{17,9},{25,17},{2,26},{10... | collective-permute-start | bytes 9830408 | tf_op jit(solution)/shard_map/ppermute | solution.py:542
  741.7 103.6 %collective-permute-start.12 = (bf16[1600,256]{1,0:T(8,128)(2,1)}, bf16[1600,256]{1,0:T(8,128)(2,1)}, u32[]{:S(2)}, u32[]{:S(2)}) collective-permute-start(bf16[1600,256]{1,0:T(8,128)(2,1)} %get-tuple-element.323), channel_id=1, source_target_pairs={{0,16},{8,24},{16,0},{24,8},{1,17},{9,25},{17,1},{25,9},{2,18},{10... | collective-permute-start | bytes 2457608 | tf_op jit(solution)/shard_map/ppermute | solution.py:542
  809.8 232.4 %reduce-scatter.19.cloned.1.call-start = ((), (), s32[]{:S(2)}) async-start(), calls=%async_computation.21 | async-start | bytes 9437184 | tf_op jit(solution)/shard_map/reduce_scatter | solution.py:533
  853.4 188.8 %reduce-scatter.17.cloned.1.call-start = ((), (), s32[]{:S(2)}) async-start(), calls=%async_computation.20 | async-start | bytes 11796480 | tf_op jit(solution)/shard_map/reduce_scatter | solution.py:533
  912.0 192.8 %reduce-scatter.25.cloned.1.call-start = ((), (), s32[]{:S(2)}) async-start(), calls=%async_computation.25 | async-start | bytes 7372800
  915.4 76.2 %collective-permute-start.15 = (bf16[3200,256]{1,0:T(8,128)(2,1)S(1)}, bf16[3200,256]{1,0:T(8,128)(2,1)}, u32[]{:S(2)}, u32[]{:S(2)}) collective-permute-start(bf16[3200,256]{1,0:T(8,128)(2,1)S(1)} %get-tuple-element.319), channel_id=1, source_target_pairs={{0,8},{8,16},{16,24},{24,0},{1,9},{9,17},{17,25},{25,1},{2,10},{10... | collective-permute-start | bytes 4915208 | tf_op jit(solution)/shard_map/ppermute | solution.py:542
  1008.6 152.3 %all-gather.20.cloned.1.call-start = ((), (), s32[]{:S(2)}) async-start(), calls=%async_computation.22 | async-start | bytes 9437184 | tf_op jit(solution)/shard_map/all_gather | solution.py:779
  1042.2 210.2 %reduce-scatter.27.cloned.1.call-start = ((), (), s32[]{:S(2)}) async-start(), calls=%async_computation.26 | async-start | bytes 1024000
  1162.3 91.5 %reduce-scatter.21.cloned.1.call-start = ((), (), s32[]{:S(2)}) async-start(), calls=%async_computation.23 | async-start | bytes 1310720 | tf_op jit(solution)/shard_map/reduce_scatter | solution.py:537
  1162.9 104.4 %reduce-scatter.23.cloned.1.call-start = ((), (), s32[]{:S(2)}) async-start(), calls=%async_computation.24 | async-start | bytes 1638400 | tf_op jit(solution)/shard_map/reduce_scatter | solution.py:537
  1163.6 90.1 %collective-permute-start.17 = (bf16[1600,256]{1,0:T(8,128)(2,1)S(1)}, bf16[1600,256]{1,0:T(8,128)(2,1)S(1)}, u32[]{:S(2)}, u32[]{:S(2)}) collective-permute-start(bf16[1600,256]{1,0:T(8,128)(2,1)S(1)} %copy-done.18), channel_id=1, source_target_pairs={{0,16},{8,24},{16,0},{24,8},{1,17},{9,25},{17,1},{25,9},{2,18},{10... | collective-permute-start | bytes 2457608 | tf_op jit(solution)/shard_map/ppermute | solution.py:542
  (71 other events, 2660.9 us)
Sparse Core Ops, SparseCore 0:
  41.6 74.4 all-gather.11
  168.4 70.3 reduce-scatter.12
  243.3 52.4 all-gather.13
  298.1 82.7 all-gather.15
  454.9 53.3 all-gather.17
  701.1 70.5 reduce-scatter.14
  853.5 92.0 reduce-scatter.18
  949.1 89.1 reduce-scatter.16
  1041.7 63.0 reduce-scatter.24
  1106.5 54.2 all-gather.19
  1163.7 41.4 reduce-scatter.26
  1207.4 27.8 reduce-scatter.20
  1237.6 29.6 reduce-scatter.22

commit v5 on v4

--- a/solution.py
+++ b/solution.py
@@ -655,24 +655,26 @@
     far_next = moved(later_table[quarter:half], "dp", middle)
     attended_heads, log_totals = attend_forward(triple, heads_here, ATTEND_ROWS, scale)
     attended = lax.all_to_all(attended_heads, "sp", split_axis=0, concat_axis=0, tiled=True)
-    attended, far_next, later_table = lax.optimization_barrier((attended, far_next, later_table))
-    far_last = moved(later_table[half:], "dp", middle)
     attended = attended.reshape(span, tokens_here, wide).transpose(1, 0, 2).reshape(tokens_here, width)
     up_values = (
         jnp.dot(normed_two, wide_up, preferred_element_type=WIDE)
         + bias_vals[triple_columns:in_columns]
     )
     act_f, pull_gelu = jax.vjp(gelu_exact, up_values)
-    joined = jnp.concatenate([attended, act_f.astype(LOW)], axis=-1)
+    act, far_next, later_table = lax.optimization_barrier((act_f.astype(LOW), far_next, later_table))
+    far_third = moved(later_table[half : half + quarter], "dp", middle)
+    joined = jnp.concatenate([attended, act], axis=-1)
     hidden1 = (
         hidden0 + jnp.dot(joined, wide_out, preferred_element_type=WIDE) + bias_vals[in_columns:]
     )
     normal1, inverse1 = standardize(hidden1)
     final = (normal1 * norm_vals[4] + norm_vals[5]).astype(LOW)
     final = turned(final, teams, dp_index)
+    final, far_third, later_table = lax.optimization_barrier((final, far_third, later_table))
+    far_last = moved(later_table[half + quarter :], "dp", middle)
     rows_all = lax.all_gather(final.reshape(seq_here, stretch, width), "sp", axis=1, tiled=True)
     rows_all, far_last = lax.optimization_barrier((rows_all, far_last))
-    tables[middle] = jnp.concatenate([far_first, far_next, far_last], axis=0)
+    tables[middle] = jnp.concatenate([far_first, far_next, far_third, far_last], axis=0)
     tables = [own_table] + [tables[k] for k in range(1, teams)]
     rows_all = rows_all.reshape(-1, width)
     grand = rows_all.shape[0]
@@ -712,7 +714,6 @@
     ]
     far = inner[:, (middle - 1) * share :]
     far = [far[q * quarter : (q + 1) * quarter] for q in range(4)]
-    far[0] = moved(far[0], "dp", middle)
     final_grad, inner, outer = lax.optimization_barrier((final_grad, inner, outer))
     final_grad = turned(final_grad, teams, dp_index)
 
@@ -748,12 +749,11 @@
         triple, attended_heads, d_heads, log_totals, heads_here, ATTEND_ROWS, scale
     )
     d_triple, far, outer = lax.optimization_barrier((d_triple, far, outer))
-    far[2] = moved(far[2], "dp", middle)
+    far[0] = moved(far[0], "dp", middle)
     late = [
         (k, outer[:, (k - middle) * share : (k - middle + 1) * share])
         for k in range(middle + 1, teams)
     ]
-    late_first = [moved(part[:half], "dp", teams - k) for k, part in late]
     d_triple = lax.all_to_all(d_triple, "sp", split_axis=0, concat_axis=0, tiled=True)
     d_joint = unturn(d_triple, angles)
     g_triple = lax.dot_general(
@@ -762,12 +762,12 @@
     d_normed_one = lax.dot_general(
         d_joint, wide_triple[:, :triple_columns], contract_last, preferred_element_type=WIDE
     )
-    late_rest = [part[half:] for k, part in late]
-    d_normed_one, far, outer, late_first, late_rest = lax.optimization_barrier(
-        (d_normed_one, far, outer, late_first, late_rest)
-    )
+    late_steps = [teams - k for k, part in late]
+    late = [part for k, part in late]
+    d_normed_one, far, outer, late = lax.optimization_barrier((d_normed_one, far, outer, late))
     own_part = outer[:, :share]
-    late_rest = [moved(late_rest[j], "dp", teams - late[j][0]) for j in range(len(late))]
+    late = [moved(part, "dp", step) for part, step in zip(late, late_steps)]
+    far[2] = moved(far[2], "dp", middle)
     g_gain_one = jnp.sum(d_normed_one * normal0, axis=0)
     g_shift_one = jnp.sum(d_normed_one, axis=0)
     g_gain_two = jnp.sum(d_normed_two * normal0, axis=0)
@@ -777,8 +777,8 @@
     grad_all = lax.all_to_all(d_hidden0, "dp", split_axis=1, concat_axis=0, tiled=True)
     grad_all, r_out, r_up = lax.optimization_barrier((grad_all, r_out, r_up))
     grad_all = lax.all_gather(grad_all, "sp", axis=0, tiled=True)
-    grad_all, late_rest, far, r_out, r_up = lax.optimization_barrier(
-        (grad_all, late_rest, far, r_out, r_up)
+    grad_all, late, far, r_out, r_up = lax.optimization_barrier(
+        (grad_all, late, far, r_out, r_up)
     )
     far[3] = moved(far[3], "dp", middle)
     target_ids = jnp.where(in_slice, local_ids, vocab_local)
@@ -800,14 +800,17 @@
     r_embed = (
         jnp.zeros(embed_table.shape, WIDE).at[target_ids].add(grad_all.astype(WIDE), mode="drop")
     )
-    r_triple, r_up, r_out = joined_teams(r_triple), joined_teams(r_up), joined_teams(r_out)
-    r_embed, far, late_first, late_rest, arrived, own_part, r_triple, r_up, r_out = (
-        lax.optimization_barrier(
-            (r_embed, far, late_first, late_rest, arrived, own_part, r_triple, r_up, r_out)
-        )
-    )
-    r_triple, r_up, r_out = r_triple.astype(WIDE), r_up.astype(WIDE), r_out.astype(WIDE)
-    late = [jnp.concatenate(pair, axis=0) for pair in zip(late_first, late_rest)]
+    team_parts = [part.reshape(teams, slab, -1) for part in (r_triple, r_up, r_out)]
+    r_layer = joined_teams(jnp.concatenate(team_parts, axis=2).reshape(teams * slab, -1))
+    r_embed, far, late, arrived, own_part, r_layer = lax.optimization_barrier(
+        (r_embed, far, late, arrived, own_part, r_layer)
+    )
+    r_layer = r_layer.astype(WIDE)
+    up_start = triple_columns + LANES
+    out_start = up_start + hidden_units
+    r_up = r_layer[:, up_start:out_start]
+    r_out = r_layer[:, out_start:].reshape(-1, width)
+    r_triple = r_layer[:, :up_start]
     r_unembed = [own_part, *arrived, *late, jnp.concatenate(far, axis=0)]
     r_norm = r_triple[:, triple_columns : triple_columns + norm_rows].T
     r_bias = r_triple[

time: 1380 us -> 1350 us (0.978)
  waiting for transfers between devices: 421 us -> 386 us
  blocking collectives: 134 us -> 106 us
  local copies, waits for them, and re-layouts: 158 us -> 179 us
    all_gather x1, waiting for transfers between devices: 54.3 us -> 13.3 us  [local(): grad_all = lax.all_gather(grad_all, 'sp', axis=0, tiled=True)]
    ppermute x18, waiting for transfers between devices: 233 us -> 192 us  [moved(): lax.ppermute(array, axis, [(i, (i + step) % size) for i in range(size)])]
    all_to_all x1 -> x0, blocking collectives: 29.7 us -> none  [local(): lax.all_to_all(d_hidden0, 'dp', split_axis=1, concat_axis=0, tiled=True)]
    all_to_all x0 -> x1, waiting for transfers between devices: none -> 22 us  [local(): lax.all_to_all(d_hidden0, 'dp', split_axis=1, concat_axis=0, tiled=True)]
    reshape x1 -> x3, local copies, waits for them, and re-layouts: 3.26 us -> 23.2 us  [scattered(): gradient.reshape(dp, sp, rows // (dp * sp), columns).transpose(1, 0, 2, 3)]
    transpose x2 -> x0, local copies, waits for them, and re-layouts: 19.3 us -> none  [scattered(): gradient.reshape(dp, sp, rows // (dp * sp), columns).transpose(1, 0, 2, 3)]
    all_gather x1, waiting for transfers between devices: 0.01 us -> 16.3 us  [local(): lax.all_gather(final.reshape(seq_here, stretch, width), 'sp', axis=1, til...]
    all_to_all x1, waiting for transfers between devices: 0.01 us -> 13.9 us  [local(): lax.all_to_all(attended_heads, 'sp', split_axis=0, concat_axis=0, tiled=T...]
  transfers between devices with their start and end apart: 35 -> 34, of which waited for: 13 -> 15; matrix products, arithmetic and copies ran while one was open for 29% -> 32% of each run, Pallas kernels for 6% -> 6%
where the time goes in v5:
time: 1350 us; the launch traced here: 1340 us
  waiting for transfers between devices  386 us (29%)
  Pallas kernels  242 us (18%)
  other arithmetic  190 us (14%)
  local copies, waits for them, and re-layouts  179 us (13%)
  matrix products  161 us (12%)
  blocking collectives  106 us (8%)
  starting transfers between devices  48 us (4%)
  between operations  26.3 us (2%)
    ppermute x18, waiting for transfers between devices, moved(): lax.ppermute(array, axis, [(i, (i + step) % size) for i in range(size)])  192 us
    scatter-add x1, other arithmetic, local(): jnp.zeros(embed_table.shape, WIDE).at[target_ids]  83.7 us
    pallas_call x1, Pallas kernels, head_forward(): pl.pallas_call(partial(head_forward_kernel, teams, real), grid=(total //...  83.2 us
    pallas_call x1, Pallas kernels, head_backward(): pl.pallas_call(partial(head_backward_kernel, teams), grid=(total // count...  73.9 us
    gather x1, local copies, waits for them, and re-layouts, local(): embed_table.astype(LOW).at[safe_ids].get(mode='promise_in_bounds')  70.1 us
    dot_general x2, matrix products, local(): lax.dot_general(slopes, side, (((0,), (0,)), ((), ())), preferred_element...  68.3 us
    unnamed x14, waiting for transfers between devices  63.2 us
    all_to_all x1, blocking collectives, local(): lax.all_to_all(packed, 'sp', split_axis=0, concat_axis=0, tiled=True)  56.6 us
  transfers between devices with their start and end apart: 34, of which 15 were waited for; matrix products, arithmetic and copies ran while one was open for 32% of the time, Pallas kernels for 6%

profile of v5, /device:TPU:0, one launch (start us, length us, event | category | flops | bytes accessed | tf_op | source)
XLA Modules:
  0.0 1339.2 jit_solution(17250420595678231425)
XLA Ops:
  12.1 15.1 %all-gather.4 = s32[4,2,2048]{2,1,0:T(2,128)S(1)} all-gather(s32[1,2,2048]{2,1,0:T(2,128)} %bitcast.177), channel_id=2, replica_groups=mesh['dp'=4,'sp'=8] {'dp'}, dimensions={0}, use_global_device_ids=true | all-gather | bytes 81920 | tf_op jit(solution)/shard_map/all_gather | solution.py:608
  48.0 70.1 %gather_fusion = bf16[16384,256]{1,0:T(8,128)(2,1)} fusion(bf16[6288,256]{1,0:T(8,128)(2,1)S(1)} %convert_element_type.116, s32[16384]{0:T(1024)} %broadcast_clamp_fusion), kind=kCustom, calls=%fused_computation | custom fusion | bytes 16842752 | tf_op jit(solution)/shard_map/gather | solution.py:621
  150.0 18.3 %collective-permute-done = bf16[1600,256]{1,0:T(8,128)(2,1)} collective-permute-done((bf16[1600,256]{1,0:T(8,128)(2,1)}, bf16[1600,256]{1,0:T(8,128)(2,1)}, u32[]{:S(2)}, u32[]{:S(2)}) %collective-permute-start) | collective-permute-done | bytes 819232 | tf_op jit(solution)/shard_map/ppermute | solution.py:542
  168.5 74.7 %collective-permute-done.7.refs_1_ = bf16[6400,256]{1,0:T(8,128)(2,1)} collective-permute-done((bf16[6400,256]{1,0:T(8,128)(2,1)S(1)}, bf16[6400,256]{1,0:T(8,128)(2,1)}, u32[]{:S(2)}, u32[]{:S(2)}) %collective-permute-start.7) | collective-permute-done | bytes 3276832 | tf_op jit(solution)/shard_map/ppermute | solution.py:542
  254.4 18.3 %all-to-all-done = bf16[4,512,256]{2,1,0:T(8,128)(2,1)S(1)} async-done(((bf16[4,512,256]{2,1,0:T(8,128)(2,1)}), bf16[4,512,256]{2,1,0:T(8,128)(2,1)S(1)}, u32[]{:S(2)}, u32[]{:S(2)}) %all-to-all-start) | async-done | bytes 1048608 | tf_op jit(solution)/shard_map/all_to_all | solution.py:634
  288.3 56.6 %all_to_all.58.query_ref.key_ref.value_ref = bf16[8,3,2,256,128]{4,3,2,1,0:T(8,128)(2,1)} all-to-all(bf16[8,3,2,256,128]{4,3,2,1,0:T(8,128)(2,1)} %project_queries.1), channel_id=1, replica_groups=mesh['dp'=4,'sp'=8] {'sp'}, dimensions={0} | all-to-all | bytes 6291456 | tf_op jit(solution)/shard_map/all_to_all | solution.py:653
  345.1 23.8 %attend_forward.1 = (bf16[8,2,256,128]{3,2,1,0:T(8,128)(2,1)}, f32[2,8,2048]{2,1,0:T(8,128)}) custom-call(bf16[8,3,2,256,128]{4,3,2,1,0:T(8,128)(2,1)} %all_to_all.58.query_ref.key_ref.value_ref, bf16[8,3,2,256,128]{4,3,2,1,0:T(8,128)(2,1)} %all_to_all.58.query_ref.key_ref.value_ref, bf16[8,3,2,256,128]{4,3,2,1,0:T(8,128)(2,1)} %all_to_all.58.query_ref.key_ref.value_ref), custom_call_target="tpu_custom_call" | custom-call | flops 8388608 | bytes 524288 | tf_op jit(solution)/shard_map/attend_forward/pallas_call | solution.py:258
  375.6 13.9 %all-to-all-done.2 = bf16[8,2,256,128]{3,2,1,0:T(8,128)(2,1)S(1)} async-done(((bf16[8,2,256,128]{3,2,1,0:T(8,128)(2,1)}), bf16[8,2,256,128]{3,2,1,0:T(8,128)(2,1)S(1)}, u32[]{:S(2)}, u32[]{:S(2)}) %all-to-all-start.2) | async-done | bytes 1048608 | tf_op jit(solution)/shard_map/all_to_all | solution.py:657
  390.6 27.3 %multiply_convert_fusion = (bf16[512,4096]{1,0:T(8,128)(2,1)S(1)}, f32[512,4096]{1,0:T(8,128)}, f32[512,4096]{1,0:T(8,128)}) fusion(f32[4096]{0:T(1024)S(1)} %add.315, bf16[1024,4096]{1,0:T(8,128)(2,1)} %bitcast.181, bf16[512,1024]{1,0:T(8,128)(2,1)S(1)} %bitcast.134, f32[1024]{0:T(1024)S(1)} %get-tuple-element.320, f32[1024]{0:T(1024)S(1)} %get-tuple-element.321, ...), kind=kOutput, calls=%fused_computation.16 | convolution fusion | flops 4436525056 | bytes 30437376 | tf_op jit(solution)/shard_map/dot_general | solution.py:660
  436.9 19.1 %collective-permute-done.10 = bf16[1600,256]{1,0:T(8,128)(2,1)S(1)} collective-permute-done((bf16[1600,256]{1,0:T(8,128)(2,1)}, bf16[1600,256]{1,0:T(8,128)(2,1)S(1)}, u32[]{:S(2)}, u32[]{:S(2)}) %collective-permute-start.10) | collective-permute-done | bytes 819232 | tf_op jit(solution)/shard_map/ppermute | solution.py:542
  464.7 31.3 %collective-permute-done.11 = bf16[1600,256]{1,0:T(8,128)(2,1)S(1)} collective-permute-done((bf16[1600,256]{1,0:T(8,128)(2,1)}, bf16[1600,256]{1,0:T(8,128)(2,1)S(1)}, u32[]{:S(2)}, u32[]{:S(2)}) %collective-permute-start.11) | collective-permute-done | bytes 819232 | tf_op jit(solution)/shard_map/ppermute | solution.py:542
  496.0 16.3 %all-gather.18.cloned.1.call-done = bf16[2,2048,1024]{2,1,0:T(8,128)(2,1)} async-done(((bf16[2,256,1024]{2,1,0:T(8,128)(2,1)}), bf16[2,2048,1024]{2,1,0:T(8,128)(2,1)}) %all-gather.18.cloned.1.call-update) | async-done | bytes 8388624 | tf_op jit(solution)/shard_map/all_gather | solution.py:675
  513.2 83.2 %head_forward.1 = (bf16[4096,6400]{1,0:T(8,128)(2,1)}, f32[4096,128]{1,0:T(8,128)}, f32[8,4096]{1,0:T(8,128)}) custom-call(bf16[4096,1024]{1,0:T(8,128)(2,1)} %bitcast.158, s32[4096,1]{1,0:T(8,128)} %bitcast.163, bf16[6400,256]{1,0:T(8,128)(2,1)} %pad.13.refs_0_, bf16[6400,256]{1,0:T(8,128)(2,1)} %collective-permute-done.7.refs_1_, ...), custom_call_target="tpu_custom_call" | custom-call | flops 53687091200 | bytes 73924608 | tf_op jit(solution)/shard_map/head_forward/pallas_call | solution.py:99
  609.4 73.9 %head_backward.1 = (bf16[4096,6400]{1,0:T(8,128)(2,1)}, bf16[4096,1024]{1,0:T(8,128)(2,1)}) custom-call(f32[4096,128]{1,0:T(8,128)} %get-tuple-element.134.stats_ref, f32[8,4096]{1,0:T(8,128)} %maximum_maximum_fusion.lines_ref, s32[4096,1]{1,0:T(8,128)} %bitcast.164, bf16[4096,6400]{1,0:T(8,128)(2,1)} %get-tuple-element.136.powers_ref, ...), custom_call_target="tpu_custom_call" | custom-call | flops 53687091200 | bytes 126353408 | tf_op jit(solution)/shard_map/head_backward/pallas_call | solution.py:158
  683.3 34.4 %convolution_convert_fusion.1 = bf16[6400,512]{1,0:T(8,128)(2,1)S(1)} fusion(bf16[4096,6400]{1,0:T(8,128)(2,1)} %get-tuple-element.138, bf16[4096,1024]{1,0:T(8,128)(2,1)} %bitcast.159), kind=kOutput, calls=%fused_computation.8 | convolution fusion | flops 26846822400 | bytes 63176704 | tf_op jit(solution)/shard_map/dot_general | solution.py:707
  725.1 33.9 %convolution_convert_fusion = bf16[6400,512]{1,0:T(8,128)(2,1)} fusion(bf16[4096,6400]{1,0:T(8,128)(2,1)} %get-tuple-element.138, bf16[4096,256]{1,0:T(8,128)(2,1)S(1)} %get-tuple-element.355, bf16[4096,256]{1,0:T(8,128)(2,1)S(1)} %get-tuple-element.354), kind=kOutput, calls=%fused_computation.7 | convolution fusion | flops 26855211008 | bytes 63176704 | tf_op jit(solution)/shard_map/dot_general | solution.py:707
  782.9 13.5 %fusion.108 = (bf16[4096]{0:T(1024)(128)(2,1)S(1)}, bf16[512,4096]{1,0:T(8,128)(2,1)S(1)}) fusion(f32[512,4096]{1,0:T(8,128)} %get-tuple-element.351, bf16[512,1024]{1,0:T(8,128)(2,1)S(1)} %get-tuple-element.345, bf16[5120,1024]{1,0:T(8,128)(2,1)} %bitcast.180, f32[512,4096]{1,0:T(8,128)} %get-tuple-element.380, f32[4096]{0:T(1024)S(1)} %copy-done.39), kind=kOutput, calls=%fused_computation.247 | convolution fusion | flops 4328517632 | bytes 30433280 | tf_op jit(solution)/shard_map/dot_general | solution.py:734
  833.4 41.4 %attend_backward.1 = bf16[8,3,2,256,128]{4,3,2,1,0:T(8,128)(2,1)} custom-call(bf16[8,3,2,256,128]{4,3,2,1,0:T(8,128)(2,1)} %all_to_all.58.query_ref.key_ref.value_ref, bf16[8,3,2,256,128]{4,3,2,1,0:T(8,128)(2,1)} %all_to_all.58.query_ref.key_ref.value_ref, bf16[8,3,2,256,128]{4,3,2,1,0:T(8,128)(2,1)} %all_to_all.58.query_ref.key_ref.value_ref, ...), custom_call_target="tpu_custom_call" | custom-call | flops 8388608 | bytes 524288 | tf_op jit(solution)/shard_map/attend_backward/pallas_call | solution.py:357
  886.5 37.4 %all-to-all-done.4.triple_ref = bf16[8,3,2,256,128]{4,3,2,1,0:T(8,128)(2,1)} async-done(((bf16[8,3,2,256,128]{4,3,2,1,0:T(8,128)(2,1)}), bf16[8,3,2,256,128]{4,3,2,1,0:T(8,128)(2,1)}, u32[]{:S(2)}, u32[]{:S(2)}) %all-to-all-start.4) | async-done | bytes 3145760 | tf_op jit(solution)/shard_map/all_to_all | solution.py:757
  971.5 22.0 %all-to-all-done.5 = bf16[512,4,256]{2,0,1:T(8,128)(2,1)S(1)} async-done(((bf16[512,4,256]{2,0,1:T(8,128)(2,1)}), bf16[512,4,256]{2,0,1:T(8,128)(2,1)S(1)}, u32[]{:S(2)}, u32[]{:S(2)}) %all-to-all-start.5) | async-done | bytes 1048608 | tf_op jit(solution)/shard_map/all_to_all | solution.py:777
  1006.7 62.5 %reduce-scatter.21.cloned.1.call-done = bf16[128,3200]{1,0:T(8,128)(2,1)} async-done(((bf16[1024,3200]{1,0:T(8,128)(2,1)}), bf16[128,3200]{1,0:T(8,128)(2,1)}) %reduce-scatter.21.cloned.1.call-update) | async-done | bytes 819216
  1071.0 41.5 %collective-permute-done.16 = bf16[1600,256]{1,0:T(8,128)(2,1)} collective-permute-done((bf16[1600,256]{1,0:T(8,128)(2,1)S(1)}, bf16[1600,256]{1,0:T(8,128)(2,1)}, u32[]{:S(2)}, u32[]{:S(2)}) %collective-permute-start.16) | collective-permute-done | bytes 819232 | tf_op jit(solution)/shard_map/ppermute | solution.py:542
  1138.1 83.7 %scatter_custom_fusion = f32[6288,256]{1,0:T(8,128)} fusion(s32[16384]{0:T(1024)} %bitcast.171, bf16[16384,256]{1,0:T(8,128)(2,1)} %all-gather.20.cloned.1.call-done, f32[]{:T(128)} %constant.70.clone.1), kind=kCustom, calls=%fused_computation.2 | custom fusion | flops 8388608 | bytes 14828032 | tf_op jit(solution)/shard_map/scatter-add | solution.py:801
  1297.2 17.3 %add_subtract_fusion = (f32[6288,256]{1,0:T(8,128)}, f32[6288,256]{1,0:T(8,128)}, f32[6288,256]{1,0:T(8,128)}) fusion(f32[6288,256]{1,0:T(8,128)} %param.24, f32[6288,256]{1,0:T(8,128)} %scatter_custom_fusion, f32[]{:T(128)S(6)} %min.13, f32[6288,256]{1,0:T(8,128)} %param.25, f32[6288,256]{1,0:T(8,128)} %param.26), kind=kLoop, calls=%fused_computation.38 | loop fusion | flops 24145920 | bytes 45072388 | tf_op jit(solution)/shard_map/sub | solution.py:499
  (373 shorter events, 383.7 us)
Async XLA Ops:
  7.2 161.1 %all-gather.12.cloned.1.call-start = ((), (), s32[]{:S(2)}) async-start(), calls=%async_computation.12 | async-start | bytes 6758400 | tf_op jit(solution)/shard_map/all_gather | solution.py:605
  33.0 108.8 %collective-permute-start.4 = (bf16[160,1024]{1,0:T(8,128)(2,1)}, bf16[160,1024]{1,0:T(8,128)(2,1)}, u32[]{:S(2)}, u32[]{:S(2)}) collective-permute-start(bf16[160,1024]{1,0:T(8,128)(2,1)} %convert_element_type.115), channel_id=1, source_target_pairs={{0,24},{8,0},{16,8},{24,16},{1,25},{9,1},{17,9},{25,17},{2,26},{10... | collective-permute-start | bytes 983048 | tf_op jit(solution)/shard_map/ppermute | solution.py:542
  36.5 106.3 %collective-permute-start.5 = (bf16[160,1024]{1,0:T(8,128)(2,1)}, bf16[160,1024]{1,0:T(8,128)(2,1)}, u32[]{:S(2)}, u32[]{:S(2)}) collective-permute-start(bf16[160,1024]{1,0:T(8,128)(2,1)} %convert_element_type.115), channel_id=1, source_target_pairs={{0,16},{8,24},{16,0},{24,8},{1,17},{9,25},{17,1},{25,9},{2,18},{10... | collective-permute-start | bytes 983048 | tf_op jit(solution)/shard_map/ppermute | solution.py:542
  36.5 107.3 %collective-permute-start.6 = (bf16[160,1024]{1,0:T(8,128)(2,1)}, bf16[160,1024]{1,0:T(8,128)(2,1)}, u32[]{:S(2)}, u32[]{:S(2)}) collective-permute-start(bf16[160,1024]{1,0:T(8,128)(2,1)} %convert_element_type.115), channel_id=1, source_target_pairs={{0,8},{8,16},{16,24},{24,0},{1,9},{9,17},{17,25},{25,1},{2,10},{10... | collective-permute-start | bytes 983048 | tf_op jit(solution)/shard_map/ppermute | solution.py:542
  37.1 90.6 %collective-permute-start.1 = (bf16[32,4096]{1,0:T(8,128)(2,1)S(1)}, bf16[32,4096]{1,0:T(8,128)(2,1)}, u32[]{:S(2)}, u32[]{:S(2)}) collective-permute-start(bf16[32,4096]{1,0:T(8,128)(2,1)S(1)} %slice.233), channel_id=1, source_target_pairs={{0,24},{8,0},{16,8},{24,16},{1,25},{9,1},{17,9},{25,17},{2,26},{10... | collective-permute-start | bytes 786440 | tf_op jit(solution)/shard_map/ppermute | solution.py:542
  40.3 88.4 %collective-permute-start.2 = (bf16[32,4096]{1,0:T(8,128)(2,1)S(1)}, bf16[32,4096]{1,0:T(8,128)(2,1)}, u32[]{:S(2)}, u32[]{:S(2)}) collective-permute-start(bf16[32,4096]{1,0:T(8,128)(2,1)S(1)} %slice.233), channel_id=1, source_target_pairs={{0,16},{8,24},{16,0},{24,8},{1,17},{9,25},{17,1},{25,9},{2,18},{10... | collective-permute-start | bytes 786440 | tf_op jit(solution)/shard_map/ppermute | solution.py:542
  41.5 201.7 %reduce-scatter.13.cloned.1.call-start = ((), (), s32[]{:S(2)}) async-start(), calls=%async_computation.13 | async-start | bytes 9437184 | tf_op jit(solution)/shard_map/reduce_scatter | solution.py:628
  168.3 222.3 %all-gather.14.cloned.1.call-start = ((), (), s32[]{:S(2)}) async-start(), calls=%async_computation.14 | async-start | bytes 9437184 | tf_op jit(solution)/shard_map/all_gather | solution.py:524
  168.4 74.8 %collective-permute-start.7 = (bf16[6400,256]{1,0:T(8,128)(2,1)S(1)}, bf16[6400,256]{1,0:T(8,128)(2,1)}, u32[]{:S(2)}, u32[]{:S(2)}) collective-permute-start(bf16[6400,256]{1,0:T(8,128)(2,1)S(1)} %copy-done.5), channel_id=1, source_target_pairs={{0,8},{8,16},{16,24},{24,0},{1,9},{9,17},{17,25},{25,1},{2,10},{10... | collective-permute-start | bytes 9830408 | tf_op jit(solution)/shard_map/ppermute | solution.py:542
  243.2 181.4 %all-gather.16.cloned.1.call-start = ((), (), s32[]{:S(2)}) async-start(), calls=%async_computation.15 | async-start | bytes 11796480 | tf_op jit(solution)/shard_map/all_gather | solution.py:524
  272.8 72.3 %collective-permute-start.8 = (bf16[6400,256]{1,0:T(8,128)(2,1)}, bf16[6400,256]{1,0:T(8,128)(2,1)}, u32[]{:S(2)}, u32[]{:S(2)}) collective-permute-start(bf16[6400,256]{1,0:T(8,128)(2,1)} %pad.13.refs_0_), channel_id=1, source_target_pairs={{0,24},{8,0},{16,8},{24,16},{1,25},{9,1},{17,9},{25,17},{2,26},{10... | collective-permute-start | bytes 9830408 | tf_op jit(solution)/shard_map/ppermute | solution.py:542
  372.6 139.7 %all-gather.18.cloned.1.call-start = ((), (), s32[]{:S(2)}) async-start(), calls=%async_computation.16 | async-start | bytes 9437184 | tf_op jit(solution)/shard_map/all_gather | solution.py:675
  456.0 303.0 %reduce-scatter.15.cloned.1.call-start = ((), (), s32[]{:S(2)}) async-start(), calls=%async_computation.17 | async-start | bytes 9437184 | tf_op jit(solution)/shard_map/reduce_scatter | solution.py:699
  719.7 92.4 %collective-permute-start.12 = (bf16[6400,256]{1,0:T(8,128)(2,1)}, bf16[6400,256]{1,0:T(8,128)(2,1)}, u32[]{:S(2)}, u32[]{:S(2)}) collective-permute-start(bf16[6400,256]{1,0:T(8,128)(2,1)} %slice.254), channel_id=1, source_target_pairs={{0,24},{8,0},{16,8},{24,16},{1,25},{9,1},{17,9},{25,17},{2,26},{10... | collective-permute-start | bytes 9830408 | tf_op jit(solution)/shard_map/ppermute | solution.py:542
  782.8 187.1 %reduce-scatter.19.cloned.1.call-start = ((), (), s32[]{:S(2)}) async-start(), calls=%async_computation.20 | async-start | bytes 9437184
  820.2 182.4 %reduce-scatter.17.cloned.1.call-start = ((), (), s32[]{:S(2)}) async-start(), calls=%async_computation.18 | async-start | bytes 11796480 | tf_op jit(solution)/shard_map/reduce_scatter | solution.py:533
  874.8 49.1 %all-to-all-start.4 = ((bf16[8,3,2,256,128]{4,3,2,1,0:T(8,128)(2,1)}), bf16[8,3,2,256,128]{4,3,2,1,0:T(8,128)(2,1)}, u32[]{:S(2)}, u32[]{:S(2)}) async-start(bf16[8,3,2,256,128]{4,3,2,1,0:T(8,128)(2,1)} %attend_backward.1), calls=%async_computation.6 | async-start | bytes 6291456 | tf_op jit(solution)/shard_map/all_to_all | solution.py:757
  879.3 189.8 %reduce-scatter.21.cloned.1.call-start = ((), (), s32[]{:S(2)}) async-start(), calls=%async_computation.21 | async-start | bytes 7372800
  883.6 59.5 %collective-permute-start.14 = (bf16[1600,256]{1,0:T(8,128)(2,1)}, bf16[1600,256]{1,0:T(8,128)(2,1)}, u32[]{:S(2)}, u32[]{:S(2)}) collective-permute-start(bf16[1600,256]{1,0:T(8,128)(2,1)} %get-tuple-element.148), channel_id=1, source_target_pairs={{0,16},{8,24},{16,0},{24,8},{1,17},{9,25},{17,1},{25,9},{2,18},{10... | collective-permute-start | bytes 2457608 | tf_op jit(solution)/shard_map/ppermute | solution.py:542
  969.9 155.9 %all-gather.20.cloned.1.call-start = ((), (), s32[]{:S(2)}) async-start(), calls=%async_computation.19 | async-start | bytes 9437184 | tf_op jit(solution)/shard_map/all_gather | solution.py:779
  1002.7 219.2 %reduce-scatter.23.cloned.1.call-start = ((), (), s32[]{:S(2)}) async-start(), calls=%async_computation.22 | async-start | bytes 3973120
  1002.7 109.8 %collective-permute-start.15 = (bf16[6400,256]{1,0:T(8,128)(2,1)}, bf16[6400,256]{1,0:T(8,128)(2,1)}, u32[]{:S(2)}, u32[]{:S(2)}) collective-permute-start(bf16[6400,256]{1,0:T(8,128)(2,1)} %slice.216), channel_id=1, source_target_pairs={{0,8},{8,16},{16,24},{24,0},{1,9},{9,17},{17,25},{25,1},{2,10},{10... | collective-permute-start | bytes 9830408 | tf_op jit(solution)/shard_map/ppermute | solution.py:542
  1004.3 108.2 %collective-permute-start.16 = (bf16[1600,256]{1,0:T(8,128)(2,1)S(1)}, bf16[1600,256]{1,0:T(8,128)(2,1)}, u32[]{:S(2)}, u32[]{:S(2)}) collective-permute-start(bf16[1600,256]{1,0:T(8,128)(2,1)S(1)} %copy-done.17), channel_id=1, source_target_pairs={{0,16},{8,24},{16,0},{24,8},{1,17},{9,25},{17,1},{25,9},{2,18},{10... | collective-permute-start | bytes 2457608 | tf_op jit(solution)/shard_map/ppermute | solution.py:542
  1133.2 92.1 %collective-permute-start.17 = (bf16[1600,256]{1,0:T(8,128)(2,1)}, bf16[1600,256]{1,0:T(8,128)(2,1)}, u32[]{:S(2)}, u32[]{:S(2)}) collective-permute-start(bf16[1600,256]{1,0:T(8,128)(2,1)} %get-tuple-element.170), channel_id=1, source_target_pairs={{0,16},{8,24},{16,0},{24,8},{1,17},{9,25},{17,1},{25,9},{2,18},{10... | collective-permute-start | bytes 2457608 | tf_op jit(solution)/shard_map/ppermute | solution.py:542
  (65 other events, 1851.9 us)
Sparse Core Ops, SparseCore 0:
  41.6 74.4 all-gather.11
  168.5 70.3 reduce-scatter.12
  243.3 52.4 all-gather.13
  298.2 82.7 all-gather.15
  456.1 56.1 all-gather.17
  683.4 71.3 reduce-scatter.14
  820.3 77.0 reduce-scatter.18
  900.9 101.6 reduce-scatter.16
  1006.1 63.0 reduce-scatter.20
  1071.4 54.2 all-gather.19
  1133.3 86.7 reduce-scatter.22
